TPU v7x, 128 devices: a whole 4x4x4 slice. The times are simulated.
128 devices in a mesh: dp: 2 (over core), lat: 8 (over z, y_hi), lon: 8 (over y_lo, x).
Axes of the slice: x: 4, y: 4 (y_hi: 2, y_lo: 2; y = y_hi * 2 + y_lo), z: 4, core: 2. Of those that a mesh axis runs over, the one named last changes fastest.
Arguments:
- fields: bfloat16 [2, 640, 1024, 128], P('dp', 'lat', 'lon'), may hold values from -6 to 6
- down_weight: bfloat16 [3, 3, 128, 128], P(None, None, 'dp'), may hold values from -0.1875 to 0.1875
- mid_weight: bfloat16 [3, 3, 128, 128], P(None, None, 'dp'), may hold values from -0.1875 to 0.1875
- up_weight: bfloat16 [3, 3, 128, 128], P(None, None, 'dp'), may hold values from -0.1875 to 0.1875
- cotangent: bfloat16 [2, 640, 1024, 128], P('dp', 'lat', 'lon'), may hold values from -6 to 6
Outputs:
- level_out: bfloat16 [2, 640, 1024, 128], P('dp', 'lat', 'lon')
- grad_fields: bfloat16 [2, 640, 1024, 128], P('dp', 'lat', 'lon')
- grad_down: float32 [3, 3, 128, 128], P(None, None, 'dp')
- grad_mid: float32 [3, 3, 128, 128], P(None, None, 'dp')
- grad_up: float32 [3, 3, 128, 128], P(None, None, 'dp')
All inputs are finite; a program needn't handle non-finite values.
Results may differ from a plain program's by a relative error of at most 0.012.
Values may be sent and summed in bfloat16 or wider, within the bound.
No kernel may reach another device: no remote copies, remote signals or barrier semaphores. Data moves between devices by JAX's collectives and lax.ppermute only.
A program may use at most 128 MiB of HBM per device.

v0:
```python
import math

import jax
import jax.numpy as jnp
from jax import lax
from jax.sharding import PartitionSpec as P


def extended(block, sides, width, periodic):
    for axis, dim in sides:
        count = lax.axis_size(axis)
        forward = [(i, i + 1) for i in range(count - 1)]
        if periodic:
            forward.append((count - 1, 0))
        backward = [(target, source) for source, target in forward]
        low = lax.ppermute(
            lax.slice_in_dim(block, block.shape[dim] - width, None, axis=dim), axis, forward
        )
        high = lax.ppermute(lax.slice_in_dim(block, 0, width, axis=dim), axis, backward)
        block = jnp.concatenate([low, block, high], axis=dim)
    return block


def framed(field):
    tall = extended(field, (("lat", 1),), 1, False)
    return extended(tall, (("lon", 2),), 1, True)


def convolve(padded, kernel, stride, dilate, padding):
    return lax.conv_general_dilated(
        padded,
        kernel,
        (stride, stride),
        padding,
        lhs_dilation=(dilate, dilate),
        dimension_numbers=("NHWC", "HWIO", "NHWC"),
        preferred_element_type=jnp.float32,
    )


def taps_down(padded, kernel):
    return convolve(padded, kernel, 2, 1, "VALID")


def taps_same(padded, kernel):
    return convolve(padded, kernel, 1, 1, "VALID")


def taps_up(padded, kernel):
    return convolve(padded, kernel[::-1, ::-1], 1, 2, ((-1, 0), (-1, 0)))


def kernel_grad(padded, grad, dilate, layout):
    result = lax.conv_general_dilated(
        padded,
        grad,
        (1, 1),
        "VALID",
        rhs_dilation=(dilate, dilate),
        dimension_numbers=("CHWN", "IHWO", layout),
        preferred_element_type=jnp.float32,
    )
    return result[:3, :3]


def swap_io(kernel):
    return jnp.transpose(kernel, (0, 1, 3, 2))


def body(fields, down_weight, mid_weight, up_weight, cotangent):
    kernel_down, kernel_mid, kernel_up = (
        lax.all_gather(down_weight, "dp", axis=2, tiled=True),
        lax.all_gather(mid_weight, "dp", axis=2, tiled=True),
        lax.all_gather(up_weight, "dp", axis=2, tiled=True),
    )
    cells = (
        fields.shape[0]
        * lax.axis_size("dp")
        * fields.shape[1]
        * lax.axis_size("lat")
        * fields.shape[2]
        * lax.axis_size("lon")
    )
    scale = 1.0 / math.sqrt(cells)
    framed_in = framed(fields)
    down = taps_down(framed_in, kernel_down).astype(jnp.bfloat16)
    framed_down = framed(down)
    pre = taps_same(framed_down, kernel_mid)
    mid = jax.nn.silu(pre).astype(jnp.bfloat16)
    framed_mid = framed(mid)
    level_out = (fields.astype(jnp.float32) + taps_up(framed_mid, kernel_up)).astype(jnp.bfloat16)
    framed_cot = framed(cotangent)
    up_term = kernel_grad(framed_cot, mid, 2, "HWCN") * scale
    grad_mid_map = taps_down(framed_cot, swap_io(kernel_up))
    sig = jax.nn.sigmoid(pre)
    grad_pre = (grad_mid_map * sig * (1.0 + pre * (1.0 - sig))).astype(jnp.bfloat16)
    mid_term = kernel_grad(framed_down, grad_pre, 1, "HWNC") * scale
    grad_down_map = taps_same(framed(grad_pre), swap_io(kernel_mid)[::-1, ::-1]).astype(
        jnp.bfloat16
    )
    down_term = kernel_grad(framed_in, grad_down_map, 2, "HWNC") * scale
    grad_fields = (
        cotangent.astype(jnp.float32) + taps_up(framed(grad_down_map), swap_io(kernel_down))
    ).astype(jnp.bfloat16)
    totals = lax.psum((down_term, mid_term, up_term), ("lat", "lon"))
    grad_down, grad_mid, grad_up = (
        lax.psum_scatter(
            totals[0].astype(jnp.bfloat16), "dp", scatter_dimension=2, tiled=True
        ).astype(jnp.float32),
        lax.psum_scatter(
            totals[1].astype(jnp.bfloat16), "dp", scatter_dimension=2, tiled=True
        ).astype(jnp.float32),
        lax.psum_scatter(
            totals[2].astype(jnp.bfloat16), "dp", scatter_dimension=2, tiled=True
        ).astype(jnp.float32),
    )
    return (level_out, grad_fields, grad_down, grad_mid, grad_up)


def solution(mesh):
    in_specs = (
        P("dp", "lat", "lon", None),
        P(None, None, "dp", None),
        P(None, None, "dp", None),
        P(None, None, "dp", None),
        P("dp", "lat", "lon", None),
    )
    out_specs = (
        P("dp", "lat", "lon", None),
        P("dp", "lat", "lon", None),
        P(None, None, "dp", None),
        P(None, None, "dp", None),
        P(None, None, "dp", None),
    )
    return jax.shard_map(body, mesh=mesh, in_specs=in_specs, out_specs=out_specs, check_vma=False)
```

profile of v0, /device:TPU:0, one launch (start us, length us, event | category | flops | bytes accessed | tf_op | source)
XLA Modules:
  0.0 591.5 jit_solution(1721154471314080505)
XLA Ops:
  8.0 1.3 collective-permute-start.1
  9.3 6.1 %collective-permute-start = (bf16[1,1,128,128]{3,2,1,0:T(8,128)(2,1)S(1)}, bf16[1,1,128,128]{3,2,1,0:T(8,128)(2,1)S(1)}, u32[]{:S(2)}, u32[]{:S(2)}) collective-permute-start(bf16[1,1,128,128]{3,2,1,0:T(8,128)(2,1)S(1)} %get-tuple-element.33), channel_id=1, source_target_pairs={{0,8},{8,16},{16,24},{24,32},{32,40},{40,48},{48,56},{1,9},{9,17},... | collective-permute-start | bytes 98312 | tf_op jit(solution)/shard_map/ppermute | solution.py:16
  16.1 1.3 collective-permute-start.13
  17.4 6.7 %collective-permute-start.12 = (bf16[1,1,128,128]{3,2,1,0:T(8,128)(2,1)S(1)}, bf16[1,1,128,128]{3,2,1,0:T(8,128)(2,1)S(1)}, u32[]{:S(2)}, u32[]{:S(2)}) collective-permute-start(bf16[1,1,128,128]{3,2,1,0:T(8,128)(2,1)S(1)} %get-tuple-element.31), channel_id=1, source_target_pairs={{0,8},{8,16},{16,24},{24,32},{32,40},{40,48},{48,56},{1,9},{9,17},... | collective-permute-start | bytes 98312 | tf_op jit(solution)/shard_map/ppermute | solution.py:16
  24.1 2.3 all_gather.9
  26.4 3.7 all_gather.10
  30.1 3.9 all_gather.11
  34.0 2.4 constant_dynamic-update-slice_fusion.1
  36.9 1.6 collective-permute-start.2
  38.4 2.6 collective-permute-start.3
  41.3 4.6 collective-permute-start.15
  45.8 1.7 maximum_bitcast_fusion
  49.4 1.0 fusion.135
  50.3 1.9 select_convert_fusion.1
  52.4 1.7 maximum_bitcast_fusion.1
  56.7 0.9 fusion.134
  57.6 1.8 slice.186
  59.4 0.9 slice_bitcast_fusion.3
  60.3 6.3 %collective-permute-start.4 = (bf16[1,1,64,128]{3,2,1,0:T(8,128)(2,1)S(1)}, bf16[1,1,64,128]{3,2,1,0:T(8,128)(2,1)S(1)}, u32[]{:S(2)}, u32[]{:S(2)}) collective-permute-start(bf16[1,1,64,128]{3,2,1,0:T(8,128)(2,1)S(1)} %slice.150), channel_id=1, source_target_pairs={{0,8},{8,16},{16,24},{24,32},{32,40},{40,48},{48,56},{1,9},{9,17},... | collective-permute-start | bytes 49160 | tf_op jit(solution)/shard_map/ppermute | solution.py:16
  66.7 1.5 collective-permute-start.5
  68.2 4.4 fusion.132
  72.8 1.6 slice-done
  74.4 2.4 fusion.133
  76.9 1.9 fusion.41
  79.9 4.1 collective-permute-start.7
  84.0 1.9 fusion.38
  85.9 1.1 copy-done.3
  87.1 2.4 copy.61
  91.6 2.0 multiply_convert_fusion.1
  93.6 1.1 copy.34
  94.8 2.4 multiply_convert_fusion
  97.2 1.0 copy.44
  98.2 1.1 copy.67
  99.3 1.1 fusion.131
  100.3 0.9 slice.184
  102.6 6.6 %collective-permute-start.8 = (bf16[1,1,64,128]{3,0,2,1:T(2,128)(2,1)}, bf16[1,1,64,128]{3,0,2,1:T(2,128)(2,1)}, u32[]{:S(2)}, u32[]{:S(2)}) collective-permute-start(bf16[1,1,64,128]{3,0,2,1:T(2,128)(2,1)} %slice.156), channel_id=1, source_target_pairs={{0,8},{8,16},{16,24},{24,32},{32,40},{40,48},{48,56},{1,9},{9,17},... | collective-permute-start | bytes 49160 | tf_op jit(solution)/shard_map/ppermute | solution.py:16
  109.3 1.3 collective-permute-start.9
  110.6 2.0 slice_bitcast_fusion.2
  113.2 6.0 %collective-permute-start.16 = (bf16[1,1,64,128]{3,2,1,0:T(8,128)(2,1)}, bf16[1,1,64,128]{3,2,1,0:T(8,128)(2,1)S(1)}, u32[]{:S(2)}, u32[]{:S(2)}) collective-permute-start(bf16[1,1,64,128]{3,2,1,0:T(8,128)(2,1)} %slice.166), channel_id=1, source_target_pairs={{0,8},{8,16},{16,24},{24,32},{32,40},{40,48},{48,56},{1,9},{9,17},... | collective-permute-start | bytes 49160 | tf_op jit(solution)/shard_map/ppermute | solution.py:16
  119.3 1.7 collective-permute-start.17
  121.0 1.2 fusion.96
  122.2 5.3 fusion.79
  127.6 2.3 fusion.73
  130.1 4.1 collective-permute-start.19
  136.7 1.9 select_convert_fusion
  139.7 3.6 fusion.76
  143.4 368.3 %all-reduce.2 = (bf16[3,3,128,128]{3,2,1,0:T(8,128)(2,1)}, bf16[3,3,128,128]{3,2,1,0:T(8,128)(2,1)}, bf16[3,3,128,128]{3,2,1,0:T(8,128)(2,1)}) all-reduce(f32[3,3,128,128]{3,2,1,0:T(8,128)} %fusion.76, f32[3,3,128,128]{3,2,1,0:T(8,128)S(1)} %copy-done.25, ...), channel_id=1, replica_groups=mesh['dp'=2,'lat'=8,'lon'=8] {'lat','lon'}, use_global_device_ids=true, to_apply=%region_0.1 | all-reduce | flops 442368 | bytes 2654208 | tf_op jit(solution)/shard_map/psum | solution.py:105
  511.9 1.4 copy_dynamic-update-slice_fusion.1
  513.6 4.1 collective-permute-start.11
  517.7 1.2 copy.52
  519.1 1.3 collective-permute-start.20
  520.4 1.3 collective-permute-start.21
  521.8 3.7 pad_maximum_fusion.15
  525.6 1.5 copy_dynamic-update-slice_fusion
  527.9 0.9 copy-done.18
  528.8 3.2 collective-permute-start.23
  532.0 20.0 %fusion.21 = bf16[1,80,128,128]{3,0,2,1:T(2,128)(2,1)S(1)} fusion(bf16[1,80,128,128]{3,2,1,0:T(8,128)(2,1)S(1)} %copy-done.12, bf16[3,3,128,128]{3,2,1,0:T(8,128)(2,1)S(1)} %copy-done.29, bf16[1,42,66,128]{3,0,2,1:T(2,128)(2,1)S(1)} %pad_maximum_fusion.15), kind=kOutput, calls=%fused_computation.25 | convolution fusion | flops 758906880 | bytes 6247424 | tf_op jit(solution)/shard_map/conv_general_dilated | solution.py:30
  552.1 2.0 copy.78
  554.1 3.7 pad_maximum_fusion.14
  557.8 20.0 %fusion.19 = bf16[1,80,128,128]{3,0,2,1:T(2,128)(2,1)S(1)} fusion(bf16[1,80,128,128]{3,2,1,0:T(8,128)(2,1)S(1)} %copy-done.14, bf16[3,3,128,128]{3,2,1,0:T(8,128)(2,1)S(1)} %copy-done.27, bf16[1,42,66,128]{3,0,2,1:T(2,128)(2,1)S(1)} %pad_maximum_fusion.14), kind=kOutput, calls=%fused_computation.22 | convolution fusion | flops 758906880 | bytes 6247424 | tf_op jit(solution)/shard_map/conv_general_dilated | solution.py:30
  577.8 2.0 copy.79
  579.8 1.6 convert_element_type.55
  581.5 1.6 convert_element_type.53
  583.1 1.6 convert_element_type.51
  (173 shorter events, 17.8 us)
Async XLA Ops:
  7.2 572.7 %reduce-scatter.8.cloned.1.call-start = ((), (), s32[]{:S(2)}) async-start(), calls=%async_computation.5 | async-start | bytes 442368 | tf_op jit(solution)/shard_map/reduce_scatter | solution.py:113
  8.0 28.4 %collective-permute-start.1 = (bf16[1,1,128,128]{3,2,1,0:T(8,128)(2,1)S(1)}, bf16[1,1,128,128]{3,2,1,0:T(8,128)(2,1)S(1)}, u32[]{:S(2)}, u32[]{:S(2)}) collective-permute-start(bf16[1,1,128,128]{3,2,1,0:T(8,128)(2,1)S(1)} %get-tuple-element.32), channel_id=1, source_target_pairs={{8,0},{16,8},{24,16},{32,24},{40,32},{48,40},{56,48},{9,1},{17,9},... | collective-permute-start | bytes 98312 | tf_op jit(solution)/shard_map/ppermute | solution.py:19
  9.3 24.7 %collective-permute-start = (bf16[1,1,128,128]{3,2,1,0:T(8,128)(2,1)S(1)}, bf16[1,1,128,128]{3,2,1,0:T(8,128)(2,1)S(1)}, u32[]{:S(2)}, u32[]{:S(2)}) collective-permute-start(bf16[1,1,128,128]{3,2,1,0:T(8,128)(2,1)S(1)} %get-tuple-element.33), channel_id=1, source_target_pairs={{0,8},{8,16},{16,24},{24,32},{32,40},{40,48},{48,56},{1,9},{9,17},... | collective-permute-start | bytes 98312 | tf_op jit(solution)/shard_map/ppermute | solution.py:16
  16.1 25.0 %collective-permute-start.13 = (bf16[1,1,128,128]{3,2,1,0:T(8,128)(2,1)S(1)}, bf16[1,1,128,128]{3,2,1,0:T(8,128)(2,1)S(1)}, u32[]{:S(2)}, u32[]{:S(2)}) collective-permute-start(bf16[1,1,128,128]{3,2,1,0:T(8,128)(2,1)S(1)} %get-tuple-element.30), channel_id=1, source_target_pairs={{8,0},{16,8},{24,16},{32,24},{40,32},{48,40},{56,48},{9,1},{17,9},... | collective-permute-start | bytes 98312 | tf_op jit(solution)/shard_map/ppermute | solution.py:19
  17.4 19.1 %collective-permute-start.12 = (bf16[1,1,128,128]{3,2,1,0:T(8,128)(2,1)S(1)}, bf16[1,1,128,128]{3,2,1,0:T(8,128)(2,1)S(1)}, u32[]{:S(2)}, u32[]{:S(2)}) collective-permute-start(bf16[1,1,128,128]{3,2,1,0:T(8,128)(2,1)S(1)} %get-tuple-element.31), channel_id=1, source_target_pairs={{0,8},{8,16},{16,24},{24,32},{32,40},{40,48},{48,56},{1,9},{9,17},... | collective-permute-start | bytes 98312 | tf_op jit(solution)/shard_map/ppermute | solution.py:16
  26.4 23.9 %copy-start.26 = (bf16[3,3,128,128]{3,2,1,0:T(8,128)(2,1)}, bf16[3,3,128,128]{3,2,1,0:T(8,128)(2,1)S(1)}, u32[]{:S(2)}) copy-start(bf16[3,3,128,128]{3,2,1,0:T(8,128)(2,1)S(1)} %all_gather.9) | copy-start | bytes 884740
  34.0 2.5 copy-start.13
  36.9 8.9 %collective-permute-start.2 = (bf16[1,82,1,128]{3,2,1,0:T(2,128)(2,1)S(1)}, bf16[1,82,1,128]{3,2,1,0:T(2,128)(2,1)S(1)}, u32[]{:S(2)}, u32[]{:S(2)}) collective-permute-start(bf16[1,82,1,128]{3,2,1,0:T(2,128)(2,1)S(1)} %get-tuple-element.28), channel_id=1, source_target_pairs={{0,1},{1,2},{2,3},{3,4},{4,5},{5,6},{6,7},{7,0},{8,9},{9,10},{10,1... | collective-permute-start | bytes 62984 | tf_op jit(solution)/shard_map/ppermute | solution.py:16
  38.4 7.4 %collective-permute-start.3 = (bf16[1,82,1,128]{3,2,1,0:T(2,128)(2,1)S(1)}, bf16[1,82,1,128]{3,2,1,0:T(2,128)(2,1)S(1)}, u32[]{:S(2)}, u32[]{:S(2)}) collective-permute-start(bf16[1,82,1,128]{3,2,1,0:T(2,128)(2,1)S(1)} %get-tuple-element.29), channel_id=1, source_target_pairs={{1,0},{2,1},{3,2},{4,3},{5,4},{6,5},{7,6},{0,7},{9,8},{10,9},{11,1... | collective-permute-start | bytes 62984 | tf_op jit(solution)/shard_map/ppermute | solution.py:19
  41.2 11.2 %collective-permute-start.14 = (bf16[1,82,1,128]{3,2,1,0:T(2,128)(2,1)S(1)}, bf16[1,82,1,128]{3,2,1,0:T(2,128)(2,1)S(1)}, u32[]{:S(2)}, u32[]{:S(2)}) collective-permute-start(bf16[1,82,1,128]{3,2,1,0:T(2,128)(2,1)S(1)} %get-tuple-element.26), channel_id=1, source_target_pairs={{0,1},{1,2},{2,3},{3,4},{4,5},{5,6},{6,7},{7,0},{8,9},{9,10},{10,1... | collective-permute-start | bytes 62984 | tf_op jit(solution)/shard_map/ppermute | solution.py:16
  41.3 11.1 %collective-permute-start.15 = (bf16[1,82,1,128]{3,2,1,0:T(2,128)(2,1)S(1)}, bf16[1,82,1,128]{3,2,1,0:T(2,128)(2,1)S(1)}, u32[]{:S(2)}, u32[]{:S(2)}) collective-permute-start(bf16[1,82,1,128]{3,2,1,0:T(2,128)(2,1)S(1)} %get-tuple-element.27), channel_id=1, source_target_pairs={{1,0},{2,1},{3,2},{4,3},{5,4},{6,5},{7,6},{0,7},{9,8},{10,9},{11,1... | collective-permute-start | bytes 62984 | tf_op jit(solution)/shard_map/ppermute | solution.py:19
  48.5 1.9 copy-start.31
  49.3 3.0 copy-start.4
  55.0 1.7 copy-start
  56.7 2.7 copy-start.2
  60.3 18.6 %collective-permute-start.4 = (bf16[1,1,64,128]{3,2,1,0:T(8,128)(2,1)S(1)}, bf16[1,1,64,128]{3,2,1,0:T(8,128)(2,1)S(1)}, u32[]{:S(2)}, u32[]{:S(2)}) collective-permute-start(bf16[1,1,64,128]{3,2,1,0:T(8,128)(2,1)S(1)} %slice.150), channel_id=1, source_target_pairs={{0,8},{8,16},{16,24},{24,32},{32,40},{40,48},{48,56},{1,9},{9,17},... | collective-permute-start | bytes 49160 | tf_op jit(solution)/shard_map/ppermute | solution.py:16
  66.7 12.2 %collective-permute-start.5 = (bf16[1,1,64,128]{3,1,2,0:T(2,128)(2,1)S(1)}, bf16[1,1,64,128]{3,1,2,0:T(2,128)(2,1)S(1)}, u32[]{:S(2)}, u32[]{:S(2)}) collective-permute-start(bf16[1,1,64,128]{3,1,2,0:T(2,128)(2,1)S(1)} %slice.153), channel_id=1, source_target_pairs={{8,0},{16,8},{24,16},{32,24},{40,32},{48,40},{56,48},{9,1},{17,9},... | collective-permute-start | bytes 49160 | tf_op jit(solution)/shard_map/ppermute | solution.py:19
  72.6 1.8 slice-start
  74.4 2.4 copy-start.24
  78.7 1.1 copy-start.5
  78.7 5.3 copy-start.23
  79.8 10.4 %collective-permute-start.6 = (bf16[1,42,1,128]{3,1,2,0:T(8,128)(2,1)S(1)}, bf16[1,42,1,128]{3,1,2,0:T(8,128)(2,1)S(1)}, u32[]{:S(2)}, u32[]{:S(2)}) collective-permute-start(bf16[1,42,1,128]{3,1,2,0:T(8,128)(2,1)S(1)} %get-tuple-element.52), channel_id=1, source_target_pairs={{0,1},{1,2},{2,3},{3,4},{4,5},{5,6},{6,7},{7,0},{8,9},{9,10},{10,1... | collective-permute-start | bytes 32264 | tf_op jit(solution)/shard_map/ppermute | solution.py:16
  79.9 10.3 %collective-permute-start.7 = (bf16[1,42,1,128]{3,1,2,0:T(8,128)(2,1)S(1)}, bf16[1,42,1,128]{3,1,2,0:T(8,128)(2,1)S(1)}, u32[]{:S(2)}, u32[]{:S(2)}) collective-permute-start(bf16[1,42,1,128]{3,1,2,0:T(8,128)(2,1)S(1)} %get-tuple-element.53), channel_id=1, source_target_pairs={{1,0},{2,1},{3,2},{4,3},{5,4},{6,5},{7,6},{0,7},{9,8},{10,9},{11,1... | collective-permute-start | bytes 32264 | tf_op jit(solution)/shard_map/ppermute | solution.py:19
  84.0 2.9 copy-start.3
  87.1 2.4 copy-start.1
  90.7 1.0 copy-start.30
  91.0 2.6 copy-start.6
  91.6 3.1 copy-start.28
  93.6 3.5 copy-start.19
  97.2 4.1 copy-start.21
  97.2 2.1 slice-start.1
  102.6 31.6 %collective-permute-start.8 = (bf16[1,1,64,128]{3,0,2,1:T(2,128)(2,1)}, bf16[1,1,64,128]{3,0,2,1:T(2,128)(2,1)}, u32[]{:S(2)}, u32[]{:S(2)}) collective-permute-start(bf16[1,1,64,128]{3,0,2,1:T(2,128)(2,1)} %slice.156), channel_id=1, source_target_pairs={{0,8},{8,16},{16,24},{24,32},{32,40},{40,48},{48,56},{1,9},{9,17},... | collective-permute-start | bytes 49160 | tf_op jit(solution)/shard_map/ppermute | solution.py:16
  109.3 404.1 %collective-permute-start.9 = (bf16[1,1,64,128]{3,0,2,1:T(2,128)(2,1)}, bf16[1,1,64,128]{3,0,2,1:T(2,128)(2,1)S(1)}, u32[]{:S(2)}, u32[]{:S(2)}) collective-permute-start(bf16[1,1,64,128]{3,0,2,1:T(2,128)(2,1)} %slice.159), channel_id=1, source_target_pairs={{8,0},{16,8},{24,16},{32,24},{40,32},{48,40},{56,48},{9,1},{17,9},... | collective-permute-start | bytes 49160 | tf_op jit(solution)/shard_map/ppermute | solution.py:19
  113.2 16.7 %collective-permute-start.16 = (bf16[1,1,64,128]{3,2,1,0:T(8,128)(2,1)}, bf16[1,1,64,128]{3,2,1,0:T(8,128)(2,1)S(1)}, u32[]{:S(2)}, u32[]{:S(2)}) collective-permute-start(bf16[1,1,64,128]{3,2,1,0:T(8,128)(2,1)} %slice.166), channel_id=1, source_target_pairs={{0,8},{8,16},{16,24},{24,32},{32,40},{40,48},{48,56},{1,9},{9,17},... | collective-permute-start | bytes 49160 | tf_op jit(solution)/shard_map/ppermute | solution.py:16
  119.3 10.6 %collective-permute-start.17 = (bf16[1,1,64,128]{3,1,2,0:T(2,128)(2,1)S(1)}, bf16[1,1,64,128]{3,1,2,0:T(2,128)(2,1)S(1)}, u32[]{:S(2)}, u32[]{:S(2)}) collective-permute-start(bf16[1,1,64,128]{3,1,2,0:T(2,128)(2,1)S(1)} %slice.169), channel_id=1, source_target_pairs={{8,0},{16,8},{24,16},{32,24},{40,32},{48,40},{56,48},{9,1},{17,9},... | collective-permute-start | bytes 49160 | tf_op jit(solution)/shard_map/ppermute | solution.py:19
  122.2 5.3 copy-start.9
  122.2 5.3 copy-start.10
  122.2 5.3 copy-start.20
  127.6 2.3 copy-start.15
  130.0 5.9 collective-permute-start.18
  130.1 5.8 collective-permute-start.19
  135.9 2.7 copy-start.11
  136.7 2.2 copy-start.7
  136.7 3.1 copy-start.8
  138.6 379.1 %copy-start.22 = (bf16[40,8,9,128]{3,1,2,0:T(8,128)(2,1)}, bf16[40,8,9,128]{3,1,2,0:T(8,128)(2,1)S(1)}, u32[]{:S(2)}) copy-start(bf16[40,8,9,128]{3,1,2,0:T(8,128)(2,1)S(1)} %select_convert_fusion) | copy-start | bytes 2211844
  139.7 3.6 copy-start.25
  139.7 372.2 %copy-start.16 = (bf16[1,40,64,128]{3,1,2,0:T(8,128)(2,1)S(1)}, bf16[1,40,64,128]{3,1,2,0:T(8,128)(2,1)}, u32[]{:S(2)}) copy-start(bf16[1,40,64,128]{3,1,2,0:T(8,128)(2,1)} %slice_bitcast_fusion.2) | copy-start | bytes 1966084
  511.7 69.8 %reduce-scatter.6.cloned.1.call-start = ((), (), s32[]{:S(2)}) async-start(), calls=%async_computation.4 | async-start | bytes 442368 | tf_op jit(solution)/shard_map/reduce_scatter | solution.py:110
  513.4 8.3 %copy-start.17 = (bf16[1,42,64,128]{3,0,2,1:T(2,128)(2,1)}, bf16[1,42,64,128]{3,0,2,1:T(2,128)(2,1)S(1)}, u32[]{:S(2)}) copy-start(bf16[1,42,64,128]{3,0,2,1:T(2,128)(2,1)S(1)} %constant_dynamic-update-slice_fusion.3) | copy-start | bytes 2064388
  513.5 8.3 %collective-permute-start.10 = (bf16[1,42,1,128]{3,0,2,1:T(2,128)(2,1)S(1)}, bf16[1,42,1,128]{3,0,2,1:T(2,128)(2,1)}, u32[]{:S(2)}, u32[]{:S(2)}) collective-permute-start(bf16[1,42,1,128]{3,0,2,1:T(2,128)(2,1)S(1)} %get-tuple-element.36), channel_id=1, source_target_pairs={{0,1},{1,2},{2,3},{3,4},{4,5},{5,6},{6,7},{7,0},{8,9},{9,10},{10,1... | collective-permute-start | bytes 32264 | tf_op jit(solution)/shard_map/ppermute | solution.py:16
  513.6 8.2 %collective-permute-start.11 = (bf16[1,42,1,128]{3,0,2,1:T(2,128)(2,1)S(1)}, bf16[1,42,1,128]{3,0,2,1:T(2,128)(2,1)}, u32[]{:S(2)}, u32[]{:S(2)}) collective-permute-start(bf16[1,42,1,128]{3,0,2,1:T(2,128)(2,1)S(1)} %get-tuple-element.37), channel_id=1, source_target_pairs={{1,0},{2,1},{3,2},{4,3},{5,4},{6,5},{7,6},{0,7},{9,8},{10,9},{11,1... | collective-permute-start | bytes 32264 | tf_op jit(solution)/shard_map/ppermute | solution.py:19
  519.1 6.5 %collective-permute-start.20 = (bf16[1,1,64,128]{3,0,2,1:T(2,128)(2,1)S(1)}, bf16[1,1,64,128]{3,0,2,1:T(2,128)(2,1)S(1)}, u32[]{:S(2)}, u32[]{:S(2)}) collective-permute-start(bf16[1,1,64,128]{3,0,2,1:T(2,128)(2,1)S(1)} %slice.172), channel_id=1, source_target_pairs={{0,8},{8,16},{16,24},{24,32},{32,40},{40,48},{48,56},{1,9},{9,17},... | collective-permute-start | bytes 49160 | tf_op jit(solution)/shard_map/ppermute | solution.py:16
  520.4 7.3 %collective-permute-start.21 = (bf16[1,1,64,128]{3,0,2,1:T(2,128)(2,1)S(1)}, bf16[1,1,64,128]{3,0,2,1:T(2,128)(2,1)S(1)}, u32[]{:S(2)}, u32[]{:S(2)}) collective-permute-start(bf16[1,1,64,128]{3,0,2,1:T(2,128)(2,1)S(1)} %slice.175), channel_id=1, source_target_pairs={{8,0},{16,8},{24,16},{32,24},{40,32},{48,40},{56,48},{9,1},{17,9},... | collective-permute-start | bytes 49160 | tf_op jit(solution)/shard_map/ppermute | solution.py:19
  521.7 10.3 %copy-start.12 = (bf16[1,80,128,128]{3,2,1,0:T(8,128)(2,1)S(1)}, bf16[1,80,128,128]{3,2,1,0:T(8,128)(2,1)}, u32[]{:S(2)}) copy-start(bf16[1,80,128,128]{3,2,1,0:T(8,128)(2,1)} %param.5) | copy-start | bytes 7864324
  521.7 61.4 %reduce-scatter.4.cloned.1.call-start = ((), (), s32[]{:S(2)}) async-start(), calls=%async_computation.3 | async-start | bytes 442368 | tf_op jit(solution)/shard_map/reduce_scatter | solution.py:107
  521.8 10.2 %copy-start.29 = (bf16[3,3,128,128]{3,2,1,0:T(8,128)(2,1)S(1)}, bf16[3,3,128,128]{3,2,1,0:T(8,128)(2,1)}, u32[]{:S(2)}) copy-start(bf16[3,3,128,128]{3,2,1,0:T(8,128)(2,1)} %all_gather.11) | copy-start | bytes 884740
  527.8 1.1 copy-start.18
  527.8 26.3 %collective-permute-start.22 = (bf16[1,42,1,128]{3,0,2,1:T(2,128)(2,1)S(1)}, bf16[1,42,1,128]{3,0,2,1:T(2,128)(2,1)S(1)}, u32[]{:S(2)}, u32[]{:S(2)}) collective-permute-start(bf16[1,42,1,128]{3,0,2,1:T(2,128)(2,1)S(1)} %get-tuple-element.34), channel_id=1, source_target_pairs={{0,1},{1,2},{2,3},{3,4},{4,5},{5,6},{6,7},{7,0},{8,9},{9,10},{10,1... | collective-permute-start | bytes 32264 | tf_op jit(solution)/shard_map/ppermute | solution.py:16
  528.8 25.3 %collective-permute-start.23 = (bf16[1,42,1,128]{3,0,2,1:T(2,128)(2,1)S(1)}, bf16[1,42,1,128]{3,0,2,1:T(2,128)(2,1)S(1)}, u32[]{:S(2)}, u32[]{:S(2)}) collective-permute-start(bf16[1,42,1,128]{3,0,2,1:T(2,128)(2,1)S(1)} %get-tuple-element.35), channel_id=1, source_target_pairs={{1,0},{2,1},{3,2},{4,3},{5,4},{6,5},{7,6},{0,7},{9,8},{10,9},{11,1... | collective-permute-start | bytes 32264 | tf_op jit(solution)/shard_map/ppermute | solution.py:19
  554.1 3.7 copy-start.14
  554.1 3.7 copy-start.27
Sparse Core Ops, SparseCore 0:
  511.8 4.8 reduce-scatter.7
  521.9 9.4 reduce-scatter.5
  554.2 7.0 reduce-scatter.3
where the time goes:
time: 596 us; the launch traced here: 591 us
  blocking collectives  378 us (63%)
  starting transfers between devices  66.4 us (11%)
  matrix products  59.4 us (10%)
  local copies, waits for them, and re-layouts  41.8 us (7%)
  other arithmetic  29.3 us (5%)
  between operations  14.9 us (2%)
    psum x1, blocking collectives, body(): totals = lax.psum((down_term, mid_term, up_term), ('lat', 'lon'))  368 us
    conv_general_dilated x6, matrix products, convolve(): lax.conv_general_dilated(padded, kernel, (stride, stride), padding, lhs_d...  48.2 us
    ppermute x12, starting transfers between devices, extended(): lax.ppermute(lax.slice_in_dim(block, block.shape[dim] - width, None, axis...  35 us
    ppermute x12, starting transfers between devices, extended(): lax.ppermute(lax.slice_in_dim(block, 0, width, axis=dim), axis, backward)  31.1 us
    concatenate x10, other arithmetic, extended(): block = jnp.concatenate([low, block, high], axis=dim)  17 us
    unnamed x76, local copies, waits for them, and re-layouts  16.7 us
    concatenate x22, local copies, waits for them, and re-layouts, extended(): block = jnp.concatenate([low, block, high], axis=dim)  12.3 us
  transfers between devices with their start and end apart: 27, of which 2 were waited for; matrix products, arithmetic and copies ran while one was open for 17% of the time, Pallas kernels for 0%

commit v1 on v0

--- a/solution.py
+++ b/solution.py
@@ -67,6 +67,24 @@
     return jnp.transpose(kernel, (0, 1, 3, 2))
 
 
+def reduced(terms):
+    bands = lax.axis_size("lat") * lax.axis_size("lon")
+    rows, cols, ins, outs = terms.shape
+    half = ins // lax.axis_size("dp")
+    me = lax.axis_index("dp")
+    own = lax.dynamic_slice_in_dim(terms, me * half, half, axis=2)
+    other = lax.dynamic_slice_in_dim(terms, (1 - me) * half, half, axis=2)
+    came = lax.ppermute(other.astype(jnp.bfloat16), "dp", [(0, 1), (1, 0)])
+    both = (own + came.astype(jnp.float32)).astype(jnp.bfloat16)
+    pieces = both.reshape(bands, -1, outs)
+    pieces = lax.all_to_all(pieces, ("lat", "lon"), 0, 0, tiled=True)
+    piece = jnp.sum(pieces.astype(jnp.float32), axis=0, keepdims=True).astype(jnp.bfloat16)
+    whole = lax.all_to_all(
+        jnp.broadcast_to(piece, pieces.shape), ("lat", "lon"), 0, 0, tiled=True
+    )
+    return whole.reshape(rows, cols, half, outs).astype(jnp.float32)
+
+
 def body(fields, down_weight, mid_weight, up_weight, cotangent):
     kernel_down, kernel_mid, kernel_up = (
         lax.all_gather(down_weight, "dp", axis=2, tiled=True),
@@ -102,18 +120,8 @@
     grad_fields = (
         cotangent.astype(jnp.float32) + taps_up(framed(grad_down_map), swap_io(kernel_down))
     ).astype(jnp.bfloat16)
-    totals = lax.psum((down_term, mid_term, up_term), ("lat", "lon"))
-    grad_down, grad_mid, grad_up = (
-        lax.psum_scatter(
-            totals[0].astype(jnp.bfloat16), "dp", scatter_dimension=2, tiled=True
-        ).astype(jnp.float32),
-        lax.psum_scatter(
-            totals[1].astype(jnp.bfloat16), "dp", scatter_dimension=2, tiled=True
-        ).astype(jnp.float32),
-        lax.psum_scatter(
-            totals[2].astype(jnp.bfloat16), "dp", scatter_dimension=2, tiled=True
-        ).astype(jnp.float32),
-    )
+    totals = reduced(jnp.concatenate([down_term, mid_term, up_term], axis=0))
+    grad_down, grad_mid, grad_up = totals[0:3], totals[3:6], totals[6:9]
     return (level_out, grad_fields, grad_down, grad_mid, grad_up)
 
 

time: 596 us -> 235 us (0.39)
  blocking collectives: 378 us -> 11.2 us
  starting transfers between devices: 66.4 us -> 92.7 us
  between operations: 14.9 us -> 1.97 us
    psum x1 -> x0, blocking collectives: 368 us -> none  [body(): totals = lax.psum((down_term, mid_term, up_term), ('lat', 'lon'))]
    all_to_all x0 -> x2, starting transfers between devices: none -> 21.4 us  [the longest x1 10.9 us: reduced(): pieces = lax.all_to_all(pieces, ('lat', 'lon'), 0, 0, tiled=True)]
  transfers between devices with their start and end apart: 27 -> 27, of which waited for: 2 -> 0; matrix products, arithmetic and copies ran while one was open for 17% -> 46% of each run, Pallas kernels for 0% -> 0%
where the time goes in v1:
time: 235 us; the launch traced here: 231 us
  starting transfers between devices  92.7 us (39%)
  matrix products  58.6 us (25%)
  local copies, waits for them, and re-layouts  42.1 us (18%)
  other arithmetic  24.9 us (11%)
  blocking collectives  11.2 us (5%)
    conv_general_dilated x6, matrix products, convolve(): lax.conv_general_dilated(padded, kernel, (stride, stride), padding, lhs_d...  49 us
    ppermute x12, starting transfers between devices, extended(): lax.ppermute(lax.slice_in_dim(block, block.shape[dim] - width, None, axis...  39.8 us
    ppermute x12, starting transfers between devices, extended(): lax.ppermute(lax.slice_in_dim(block, 0, width, axis=dim), axis, backward)  31.5 us
    concatenate x10, other arithmetic, extended(): block = jnp.concatenate([low, block, high], axis=dim)  16.4 us
    unnamed x76, local copies, waits for them, and re-layouts  14.5 us
    concatenate x22, local copies, waits for them, and re-layouts, extended(): block = jnp.concatenate([low, block, high], axis=dim)  13 us
    all_to_all x1, starting transfers between devices, reduced(): pieces = lax.all_to_all(pieces, ('lat', 'lon'), 0, 0, tiled=True)  10.9 us
    all_to_all x1, starting transfers between devices, reduced(): lax.all_to_all(jnp.broadcast_to(piece, pieces.shape), ('lat', 'lon'), 0,...  10.5 us
  transfers between devices with their start and end apart: 27, of which 0 were waited for; matrix products, arithmetic and copies ran while one was open for 46% of the time, Pallas kernels for 0%

profile of v1, /device:TPU:0, one launch (start us, length us, event | category | flops | bytes accessed | tf_op | source)
XLA Modules:
  0.0 231.5 jit_solution(7474294646583860021)
XLA Ops:
  0.6 0.8 fusion.145
  1.4 5.2 %collective-permute-start = (bf16[1,1,128,128]{3,2,1,0:T(8,128)(2,1)S(1)}, bf16[1,1,128,128]{3,2,1,0:T(8,128)(2,1)S(1)}, u32[]{:S(2)}, u32[]{:S(2)}) collective-permute-start(bf16[1,1,128,128]{3,2,1,0:T(8,128)(2,1)S(1)} %get-tuple-element.30), channel_id=1, source_target_pairs={{0,8},{8,16},{16,24},{24,32},{32,40},{40,48},{48,56},{1,9},{9,17},... | collective-permute-start | bytes 98312 | tf_op jit(solution)/shard_map/ppermute | solution.py:16
  6.6 1.3 collective-permute-start.1
  8.7 6.0 %collective-permute-start.12 = (bf16[1,1,128,128]{3,2,1,0:T(8,128)(2,1)S(1)}, bf16[1,1,128,128]{3,2,1,0:T(8,128)(2,1)S(1)}, u32[]{:S(2)}, u32[]{:S(2)}) collective-permute-start(bf16[1,1,128,128]{3,2,1,0:T(8,128)(2,1)S(1)} %get-tuple-element.28), channel_id=1, source_target_pairs={{0,8},{8,16},{16,24},{24,32},{32,40},{40,48},{48,56},{1,9},{9,17},... | collective-permute-start | bytes 98312 | tf_op jit(solution)/shard_map/ppermute | solution.py:16
  14.7 1.3 collective-permute-start.13
  16.0 3.7 %all_gather.9 = bf16[3,3,128,128]{3,2,1,0:T(8,128)(2,1)} all-gather(bf16[3,3,64,128]{3,2,1,0:T(8,128)(2,1)} %param.6), channel_id=1, replica_groups=mesh['dp'=2,'lat'=8,'lon'=8] {'dp'}, dimensions={2}, use_global_device_ids=true | all-gather | bytes 442368 | tf_op jit(solution)/shard_map/all_gather | solution.py:90
  19.7 3.9 %all_gather.10 = bf16[3,3,128,128]{3,2,1,0:T(8,128)(2,1)} all-gather(bf16[3,3,64,128]{3,2,1,0:T(8,128)(2,1)} %param.7), channel_id=1, replica_groups=mesh['dp'=2,'lat'=8,'lon'=8] {'dp'}, dimensions={2}, use_global_device_ids=true | all-gather | bytes 442368 | tf_op jit(solution)/shard_map/all_gather | solution.py:91
  23.6 3.7 %all_gather.11 = bf16[3,3,128,128]{3,2,1,0:T(8,128)(2,1)} all-gather(bf16[3,3,64,128]{3,2,1,0:T(8,128)(2,1)} %param.8), channel_id=1, replica_groups=mesh['dp'=2,'lat'=8,'lon'=8] {'dp'}, dimensions={2}, use_global_device_ids=true | all-gather | bytes 442368 | tf_op jit(solution)/shard_map/all_gather | solution.py:92
  27.2 2.4 %constant_dynamic-update-slice_fusion.1 = bf16[1,82,128,128]{3,2,1,0:T(8,128)(2,1)S(1)} fusion(bf16[1,82,128,128]{3,2,1,0:T(8,128)(2,1)S(1)} %constant_dynamic-update-slice_fusion.2, bf16[1,80,128,128]{3,2,1,0:T(8,128)(2,1)} %param.5), kind=kLoop, calls=%fused_computation.121 | loop fusion | bytes 5242880
  29.7 1.6 collective-permute-start.2
  31.3 2.6 %collective-permute-start.3 = (bf16[1,82,1,128]{3,2,1,0:T(2,128)(2,1)S(1)}, bf16[1,82,1,128]{3,2,1,0:T(2,128)(2,1)S(1)}, u32[]{:S(2)}, u32[]{:S(2)}) collective-permute-start(bf16[1,82,1,128]{3,2,1,0:T(2,128)(2,1)S(1)} %get-tuple-element.26), channel_id=1, source_target_pairs={{1,0},{2,1},{3,2},{4,3},{5,4},{6,5},{7,6},{0,7},{9,8},{10,9},{11,1... | collective-permute-start | bytes 62984 | tf_op jit(solution)/shard_map/ppermute | solution.py:19
  34.5 4.4 %collective-permute-start.15 = (bf16[1,82,1,128]{3,2,1,0:T(2,128)(2,1)S(1)}, bf16[1,82,1,128]{3,2,1,0:T(2,128)(2,1)S(1)}, u32[]{:S(2)}, u32[]{:S(2)}) collective-permute-start(bf16[1,82,1,128]{3,2,1,0:T(2,128)(2,1)S(1)} %get-tuple-element.24), channel_id=1, source_target_pairs={{1,0},{2,1},{3,2},{4,3},{5,4},{6,5},{7,6},{0,7},{9,8},{10,9},{11,1... | collective-permute-start | bytes 62984 | tf_op jit(solution)/shard_map/ppermute | solution.py:19
  38.9 1.7 maximum_bitcast_fusion
  43.2 1.9 select_convert_fusion.1
  45.1 1.0 copy.28
  46.0 1.7 slice.190
  47.8 1.7 maximum_bitcast_fusion.1
  51.2 0.9 copy-done
  52.1 1.0 fusion.141
  53.1 0.9 copy-done.2
  54.1 1.3 collective-permute-start.5
  55.4 7.2 %collective-permute-start.4 = (bf16[1,1,64,128]{3,2,1,0:T(8,128)(2,1)S(1)}, bf16[1,1,64,128]{3,2,1,0:T(8,128)(2,1)S(1)}, u32[]{:S(2)}, u32[]{:S(2)}) collective-permute-start(bf16[1,1,64,128]{3,2,1,0:T(8,128)(2,1)S(1)} %slice.162), channel_id=1, source_target_pairs={{0,8},{8,16},{16,24},{24,32},{32,40},{40,48},{48,56},{1,9},{9,17},... | collective-permute-start | bytes 49160 | tf_op jit(solution)/shard_map/ppermute | solution.py:16
  62.6 1.1 slice_bitcast_fusion.3
  63.8 4.2 %fusion.139 = (bf16[82,8,18,128,1]{3,1,4,2,0:T(8,128)(2,1)}, bf16[82,1,8,18,128]{4,2,3,0,1:T(8,128)(2,1)S(1)}) fusion(bf16[82,1,7,1,128]{4,2,3,0,1:T(8,128)(2,1)S(1)} %get-tuple-element.17, bf16[82,1,8,17,128]{4,2,3,0,1:T(8,128)(2,1)} %slice.190), kind=kLoop, calls=%fused_computation.158 | loop fusion | flops 9068544 | bytes 9047552 | tf_op jit(solution)/shard_map/concatenate | solution.py:20
  68.2 1.6 slice-done
  69.8 2.5 %fusion.138 = (bf16[82,8,18,128,1]{3,1,4,2,0:T(8,128)(2,1)}, bf16[82,1,8,18,128]{4,2,3,0,1:T(8,128)(2,1)S(1)}) fusion(bf16[82,1,7,1,128]{4,2,3,0,1:T(8,128)(2,1)S(1)} %copy-done.19, bf16[82,1,8,17,128]{4,2,3,0,1:T(8,128)(2,1)S(1)} %slice-done), kind=kLoop, calls=%fused_computation.157 | loop fusion | flops 9068544 | bytes 9047552 | tf_op jit(solution)/shard_map/concatenate | solution.py:20
  72.3 1.8 fusion.38
  74.5 4.1 %collective-permute-start.7 = (bf16[1,42,1,128]{3,1,2,0:T(8,128)(2,1)S(1)}, bf16[1,42,1,128]{3,1,2,0:T(8,128)(2,1)S(1)}, u32[]{:S(2)}, u32[]{:S(2)}) collective-permute-start(bf16[1,42,1,128]{3,1,2,0:T(8,128)(2,1)S(1)} %get-tuple-element.53), channel_id=1, source_target_pairs={{1,0},{2,1},{3,2},{4,3},{5,4},{6,5},{7,6},{0,7},{9,8},{10,9},{11,1... | collective-permute-start | bytes 32264 | tf_op jit(solution)/shard_map/ppermute | solution.py:19
  78.6 1.8 fusion.41
  80.4 1.1 copy-done.3
  81.7 2.5 %copy.63 = bf16[82,8,18,128,1]{3,1,4,2,0:T(8,128)(2,1)} copy(bf16[82,8,18,128,1]{3,0,2,1,4:T(8,128)(2,1)S(1)} %bitcast.111) | data formatting | bytes 6045696 | tf_op jit(solution)/shard_map/concatenate | solution.py:20
  84.2 2.4 %copy.78 = bf16[82,8,18,128,1]{3,1,4,2,0:T(8,128)(2,1)} copy(bf16[82,8,18,128,1]{3,0,2,1,4:T(8,128)(2,1)S(1)} %bitcast.113) | data formatting | bytes 6045696 | tf_op jit(solution)/shard_map/concatenate | solution.py:20
  87.5 2.0 multiply_convert_fusion.1
  89.5 2.4 %multiply_convert_fusion = bf16[40,8,9,128]{3,1,2,0:T(8,128)(2,1)S(1)} fusion(f32[40,8,9,128]{3,1,2,0:T(8,128)S(1)} %get-tuple-element.55, bf16[3,3,128,128]{3,2,1,0:T(8,128)(2,1)S(1)} %copy-done.25, bf16[82,1,7,2,128]{4,2,3,0,1:T(8,128)(2,1)S(1)} %slice.176, bf16[82,1,8,18,128]{4,2,3,0,1:T(8,128)(2,1)S(1)} %copy-done.3, pred[8,9]{0,1:T(8,128)(4,1)S(1)} %copy-done.30), kind=kOutput, calls=%fused_computation.62 | convolution fusion | flops 863109120 | bytes 5823560 | tf_op jit(solution)/shard_map/conv_general_dilated | solution.py:30
  93.7 1.3 collective-permute-start.17
  95.6 7.5 %collective-permute-start.16 = (bf16[1,1,64,128]{3,2,1,0:T(8,128)(2,1)}, bf16[1,1,64,128]{3,2,1,0:T(8,128)(2,1)}, u32[]{:S(2)}, u32[]{:S(2)}) collective-permute-start(bf16[1,1,64,128]{3,2,1,0:T(8,128)(2,1)} %slice.178), channel_id=1, source_target_pairs={{0,8},{8,16},{16,24},{24,32},{32,40},{40,48},{48,56},{1,9},{9,17},... | collective-permute-start | bytes 49160 | tf_op jit(solution)/shard_map/ppermute | solution.py:16
  103.1 1.1 fusion.137
  104.3 1.1 copy.70
  105.5 5.9 %collective-permute-start.8 = (bf16[1,1,64,128]{3,0,2,1:T(2,128)(2,1)S(1)}, bf16[1,1,64,128]{3,0,2,1:T(2,128)(2,1)S(1)}, u32[]{:S(2)}, u32[]{:S(2)}) collective-permute-start(bf16[1,1,64,128]{3,0,2,1:T(2,128)(2,1)S(1)} %slice.168), channel_id=1, source_target_pairs={{0,8},{8,16},{16,24},{24,32},{32,40},{40,48},{48,56},{1,9},{9,17},... | collective-permute-start | bytes 49160 | tf_op jit(solution)/shard_map/ppermute | solution.py:16
  111.5 4.5 %fusion.76 = f32[3,3,128,128]{3,2,1,0:T(8,128)S(1)} fusion(bf16[42,8,9,128,1]{3,1,4,2,0:T(8,128)(2,1)S(1)} %fusion.102, bf16[42,8,9,128,1]{3,1,4,2,0:T(8,128)(2,1)} %get-tuple-element.38, bf16[42,8,9,128,1]{3,1,4,2,0:T(8,128)(2,1)} %copy.70, bf16[40,8,9,128]{3,1,2,0:T(8,128)(2,1)} %copy-done.18, pred[8,9]{0,1:T(8,128)(4,1)} %constant.56), kind=kOutput, calls=%fused_computation.81 | convolution fusion | flops 852185088 | bytes 3649608 | tf_op jit(solution)/shard_map/conv_general_dilated | solution.py:54
  116.1 2.3 fusion.85
  118.5 1.3 collective-permute-start.9
  121.3 4.1 %collective-permute-start.19 = (bf16[1,42,1,128]{3,1,2,0:T(8,128)(2,1)S(1)}, bf16[1,42,1,128]{3,1,2,0:T(8,128)(2,1)S(1)}, u32[]{:S(2)}, u32[]{:S(2)}) collective-permute-start(bf16[1,42,1,128]{3,1,2,0:T(8,128)(2,1)S(1)} %get-tuple-element.51), channel_id=1, source_target_pairs={{1,0},{2,1},{3,2},{4,3},{5,4},{6,5},{7,6},{0,7},{9,8},{10,9},{11,1... | collective-permute-start | bytes 32264 | tf_op jit(solution)/shard_map/ppermute | solution.py:19
  125.4 1.5 copy_dynamic-update-slice_fusion.1
  127.6 4.3 %collective-permute-start.11 = (bf16[1,42,1,128]{3,0,2,1:T(2,128)(2,1)}, bf16[1,42,1,128]{3,0,2,1:T(2,128)(2,1)}, u32[]{:S(2)}, u32[]{:S(2)}) collective-permute-start(bf16[1,42,1,128]{3,0,2,1:T(2,128)(2,1)} %get-tuple-element.34), channel_id=1, source_target_pairs={{1,0},{2,1},{3,2},{4,3},{5,4},{6,5},{7,6},{0,7},{9,8},{10,9},{11,1... | collective-permute-start | bytes 32264 | tf_op jit(solution)/shard_map/ppermute | solution.py:19
  132.0 1.2 maximum_bitcast_fusion.3
  133.5 1.9 select_convert_fusion
  136.1 0.8 copy-done.6
  136.9 2.8 %fusion.67 = f32[3,3,128,128]{3,2,1,0:T(8,128)S(1)} fusion(bf16[82,8,18,128,1]{3,1,4,2,0:T(8,128)(2,1)S(1)} %copy-done.6, bf16[82,8,18,128,1]{3,1,4,2,0:T(8,128)(2,1)S(1)} %copy-done.5, bf16[82,8,18,128,1]{3,1,4,2,0:T(8,128)(2,1)S(1)} %copy-done.9, bf16[40,8,9,128]{3,1,2,0:T(8,128)(2,1)S(1)} %select_convert_fusion, pred[8,9]{0,1:T(8,128)(4,1)S(1)} %copy-done.31), kind=kOutput, calls=%fused_computation.78 | convolution fusion | flops 877068288 | bytes 10395720 | tf_op jit(solution)/shard_map/slice | solution.py:63
  140.2 6.1 %collective-permute-start.20 = (bf16[1,1,64,128]{3,0,2,1:T(2,128)(2,1)S(1)}, bf16[1,1,64,128]{3,0,2,1:T(2,128)(2,1)S(1)}, u32[]{:S(2)}, u32[]{:S(2)}) collective-permute-start(bf16[1,1,64,128]{3,0,2,1:T(2,128)(2,1)S(1)} %slice.184), channel_id=1, source_target_pairs={{0,8},{8,16},{16,24},{24,32},{32,40},{40,48},{48,56},{1,9},{9,17},... | collective-permute-start | bytes 49160 | tf_op jit(solution)/shard_map/ppermute | solution.py:16
  147.1 1.3 collective-permute-start.21
  148.4 4.5 %pad_maximum_fusion.16 = bf16[1,42,66,128]{3,0,2,1:T(2,128)(2,1)} fusion(bf16[1,42,1,128]{3,0,2,1:T(2,128)(2,1)} %collective-permute-done.11, bf16[1,42,64,128]{3,0,2,1:T(2,128)(2,1)} %copy-done.13, bf16[1,42,1,128]{3,0,2,1:T(2,128)(2,1)} %collective-permute-done.10), kind=kLoop, calls=%fused_computation.67.clone.clone.1 | loop fusion | flops 709632 | bytes 1419264 | tf_op jit(solution)/shard_map/conv_general_dilated | solution.py:30
  153.0 1.5 copy_dynamic-update-slice_fusion
  154.7 4.1 %collective-permute-start.23 = (bf16[1,42,1,128]{3,0,2,1:T(2,128)(2,1)S(1)}, bf16[1,42,1,128]{3,0,2,1:T(2,128)(2,1)S(1)}, u32[]{:S(2)}, u32[]{:S(2)}) collective-permute-start(bf16[1,42,1,128]{3,0,2,1:T(2,128)(2,1)S(1)} %get-tuple-element.32), channel_id=1, source_target_pairs={{1,0},{2,1},{3,2},{4,3},{5,4},{6,5},{7,6},{0,7},{9,8},{10,9},{11,1... | collective-permute-start | bytes 32264 | tf_op jit(solution)/shard_map/ppermute | solution.py:19
  158.9 1.0 reshape.20
  159.9 10.9 %all-to-all-start = ((bf16[64,27,128]{2,1,0:T(8,128)(2,1)}), bf16[64,27,128]{2,1,0:T(8,128)(2,1)S(1)}, u32[]{:S(2)}, u32[]{:S(2)}) async-start(bf16[64,27,128]{2,1,0:T(8,128)(2,1)} %reshape.20), calls=%async_computation | async-start | bytes 1048576 | tf_op jit(solution)/shard_map/all_to_all | solution.py:80
  170.8 19.9 %fusion.21 = bf16[1,80,128,128]{3,0,2,1:T(2,128)(2,1)S(1)} fusion(bf16[1,80,128,128]{3,2,1,0:T(8,128)(2,1)} %param.5, bf16[3,3,128,128]{3,2,1,0:T(8,128)(2,1)S(1)} %copy-done.26, bf16[1,42,66,128]{3,0,2,1:T(2,128)(2,1)} %pad_maximum_fusion.16), kind=kOutput, calls=%fused_computation.25 | convolution fusion | flops 758906880 | bytes 6247424 | tf_op jit(solution)/shard_map/conv_general_dilated | solution.py:30
  190.8 2.0 copy.82
  192.8 3.0 %pad_maximum_fusion.15 = bf16[1,42,66,128]{3,0,2,1:T(2,128)(2,1)} fusion(bf16[1,42,1,128]{3,0,2,1:T(2,128)(2,1)S(1)} %collective-permute-done.23, bf16[1,42,64,128]{3,0,2,1:T(2,128)(2,1)S(1)} %copy-done.15, bf16[1,42,1,128]{3,0,2,1:T(2,128)(2,1)S(1)} %collective-permute-done.22), kind=kLoop, calls=%fused_computation.71.clone.clone.1 | loop fusion | flops 709632 | bytes 1419264 | tf_op jit(solution)/shard_map/conv_general_dilated | solution.py:30
  195.9 0.9 broadcast_in_dim.2
  196.8 10.5 %all-to-all-start.1 = ((bf16[64,27,128]{2,1,0:T(8,128)(2,1)}), bf16[64,27,128]{2,1,0:T(8,128)(2,1)S(1)}, u32[]{:S(2)}, u32[]{:S(2)}) async-start(bf16[64,27,128]{2,1,0:T(8,128)(2,1)} %broadcast_in_dim.2), calls=%async_computation.1 | async-start | bytes 1048576 | tf_op jit(solution)/shard_map/all_to_all | solution.py:82
  207.3 20.8 %fusion.19 = bf16[1,80,128,128]{3,0,2,1:T(2,128)(2,1)S(1)} fusion(bf16[1,80,128,128]{3,2,1,0:T(8,128)(2,1)S(1)} %copy-done.12, bf16[3,3,128,128]{3,2,1,0:T(8,128)(2,1)S(1)} %copy-done.24, bf16[1,42,66,128]{3,0,2,1:T(2,128)(2,1)} %pad_maximum_fusion.15), kind=kOutput, calls=%fused_computation.22 | convolution fusion | flops 758906880 | bytes 6247424 | tf_op jit(solution)/shard_map/conv_general_dilated | solution.py:30
  228.1 2.0 copy.83
  230.3 0.9 fusion.148
  (174 shorter events, 15.1 us)
Async XLA Ops:
  1.4 25.8 %collective-permute-start = (bf16[1,1,128,128]{3,2,1,0:T(8,128)(2,1)S(1)}, bf16[1,1,128,128]{3,2,1,0:T(8,128)(2,1)S(1)}, u32[]{:S(2)}, u32[]{:S(2)}) collective-permute-start(bf16[1,1,128,128]{3,2,1,0:T(8,128)(2,1)S(1)} %get-tuple-element.30), channel_id=1, source_target_pairs={{0,8},{8,16},{16,24},{24,32},{32,40},{40,48},{48,56},{1,9},{9,17},... | collective-permute-start | bytes 98312 | tf_op jit(solution)/shard_map/ppermute | solution.py:16
  6.6 23.0 %collective-permute-start.1 = (bf16[1,1,128,128]{3,2,1,0:T(8,128)(2,1)S(1)}, bf16[1,1,128,128]{3,2,1,0:T(8,128)(2,1)S(1)}, u32[]{:S(2)}, u32[]{:S(2)}) collective-permute-start(bf16[1,1,128,128]{3,2,1,0:T(8,128)(2,1)S(1)} %get-tuple-element.29), channel_id=1, source_target_pairs={{8,0},{16,8},{24,16},{32,24},{40,32},{48,40},{56,48},{9,1},{17,9},... | collective-permute-start | bytes 98312 | tf_op jit(solution)/shard_map/ppermute | solution.py:19
  8.7 25.3 %collective-permute-start.12 = (bf16[1,1,128,128]{3,2,1,0:T(8,128)(2,1)S(1)}, bf16[1,1,128,128]{3,2,1,0:T(8,128)(2,1)S(1)}, u32[]{:S(2)}, u32[]{:S(2)}) collective-permute-start(bf16[1,1,128,128]{3,2,1,0:T(8,128)(2,1)S(1)} %get-tuple-element.28), channel_id=1, source_target_pairs={{0,8},{8,16},{16,24},{24,32},{32,40},{40,48},{48,56},{1,9},{9,17},... | collective-permute-start | bytes 98312 | tf_op jit(solution)/shard_map/ppermute | solution.py:16
  14.7 19.6 %collective-permute-start.13 = (bf16[1,1,128,128]{3,2,1,0:T(8,128)(2,1)S(1)}, bf16[1,1,128,128]{3,2,1,0:T(8,128)(2,1)S(1)}, u32[]{:S(2)}, u32[]{:S(2)}) collective-permute-start(bf16[1,1,128,128]{3,2,1,0:T(8,128)(2,1)S(1)} %get-tuple-element.27), channel_id=1, source_target_pairs={{8,0},{16,8},{24,16},{32,24},{40,32},{48,40},{56,48},{9,1},{17,9},... | collective-permute-start | bytes 98312 | tf_op jit(solution)/shard_map/ppermute | solution.py:19
  27.2 6.7 %copy-start.11 = (bf16[1,80,128,128]{3,2,1,0:T(8,128)(2,1)S(1)}, bf16[1,80,128,128]{3,2,1,0:T(8,128)(2,1)}, u32[]{:S(2)}) copy-start(bf16[1,80,128,128]{3,2,1,0:T(8,128)(2,1)} %param.9) | copy-start | bytes 7864324
  29.7 9.2 %collective-permute-start.2 = (bf16[1,82,1,128]{3,2,1,0:T(2,128)(2,1)S(1)}, bf16[1,82,1,128]{3,2,1,0:T(2,128)(2,1)S(1)}, u32[]{:S(2)}, u32[]{:S(2)}) collective-permute-start(bf16[1,82,1,128]{3,2,1,0:T(2,128)(2,1)S(1)} %get-tuple-element.25), channel_id=1, source_target_pairs={{0,1},{1,2},{2,3},{3,4},{4,5},{5,6},{6,7},{7,0},{8,9},{9,10},{10,1... | collective-permute-start | bytes 62984 | tf_op jit(solution)/shard_map/ppermute | solution.py:16
  31.3 7.6 %collective-permute-start.3 = (bf16[1,82,1,128]{3,2,1,0:T(2,128)(2,1)S(1)}, bf16[1,82,1,128]{3,2,1,0:T(2,128)(2,1)S(1)}, u32[]{:S(2)}, u32[]{:S(2)}) collective-permute-start(bf16[1,82,1,128]{3,2,1,0:T(2,128)(2,1)S(1)} %get-tuple-element.26), channel_id=1, source_target_pairs={{1,0},{2,1},{3,2},{4,3},{5,4},{6,5},{7,6},{0,7},{9,8},{10,9},{11,1... | collective-permute-start | bytes 62984 | tf_op jit(solution)/shard_map/ppermute | solution.py:19
  34.4 13.4 %collective-permute-start.14 = (bf16[1,82,1,128]{3,2,1,0:T(2,128)(2,1)S(1)}, bf16[1,82,1,128]{3,2,1,0:T(2,128)(2,1)S(1)}, u32[]{:S(2)}, u32[]{:S(2)}) collective-permute-start(bf16[1,82,1,128]{3,2,1,0:T(2,128)(2,1)S(1)} %get-tuple-element.23), channel_id=1, source_target_pairs={{0,1},{1,2},{2,3},{3,4},{4,5},{5,6},{6,7},{7,0},{8,9},{9,10},{10,1... | collective-permute-start | bytes 62984 | tf_op jit(solution)/shard_map/ppermute | solution.py:16
  34.5 13.3 %collective-permute-start.15 = (bf16[1,82,1,128]{3,2,1,0:T(2,128)(2,1)S(1)}, bf16[1,82,1,128]{3,2,1,0:T(2,128)(2,1)S(1)}, u32[]{:S(2)}, u32[]{:S(2)}) collective-permute-start(bf16[1,82,1,128]{3,2,1,0:T(2,128)(2,1)S(1)} %get-tuple-element.24), channel_id=1, source_target_pairs={{1,0},{2,1},{3,2},{4,3},{5,4},{6,5},{7,6},{0,7},{9,8},{10,9},{11,1... | collective-permute-start | bytes 62984 | tf_op jit(solution)/shard_map/ppermute | solution.py:19
  41.5 1.7 copy-start.23
  41.5 1.7 copy-start.30
  50.4 1.7 copy-start
  52.1 1.9 copy-start.2
  54.1 20.3 %collective-permute-start.5 = (bf16[1,1,64,128]{3,1,2,0:T(2,128)(2,1)S(1)}, bf16[1,1,64,128]{3,1,2,0:T(2,128)(2,1)S(1)}, u32[]{:S(2)}, u32[]{:S(2)}) collective-permute-start(bf16[1,1,64,128]{3,1,2,0:T(2,128)(2,1)S(1)} %slice.165), channel_id=1, source_target_pairs={{8,0},{16,8},{24,16},{32,24},{40,32},{48,40},{56,48},{9,1},{17,9},... | collective-permute-start | bytes 49160 | tf_op jit(solution)/shard_map/ppermute | solution.py:19
  55.4 18.9 %collective-permute-start.4 = (bf16[1,1,64,128]{3,2,1,0:T(8,128)(2,1)S(1)}, bf16[1,1,64,128]{3,2,1,0:T(8,128)(2,1)S(1)}, u32[]{:S(2)}, u32[]{:S(2)}) collective-permute-start(bf16[1,1,64,128]{3,2,1,0:T(8,128)(2,1)S(1)} %slice.162), channel_id=1, source_target_pairs={{0,8},{8,16},{16,24},{24,32},{32,40},{40,48},{48,56},{1,9},{9,17},... | collective-permute-start | bytes 49160 | tf_op jit(solution)/shard_map/ppermute | solution.py:16
  68.0 1.8 slice-start
  68.0 1.8 copy-start.19
  69.8 2.5 %copy-start.20 = (bf16[82,1,7,1,128]{4,2,3,0,1:T(8,128)(2,1)S(1)}, bf16[82,1,7,1,128]{4,2,3,0,1:T(8,128)(2,1)}, u32[]{:S(2)}) copy-start(bf16[82,1,7,1,128]{4,2,3,0,1:T(8,128)(2,1)} %get-tuple-element.18) | copy-start | bytes 440836
  74.1 4.5 %copy-start.21 = (bf16[82,1,7,1,128]{4,2,3,0,1:T(8,128)(2,1)S(1)}, bf16[82,1,7,1,128]{4,2,3,0,1:T(8,128)(2,1)}, u32[]{:S(2)}) copy-start(bf16[82,1,7,1,128]{4,2,3,0,1:T(8,128)(2,1)} %get-tuple-element.22) | copy-start | bytes 440836
  74.4 12.1 %collective-permute-start.6 = (bf16[1,42,1,128]{3,1,2,0:T(8,128)(2,1)S(1)}, bf16[1,42,1,128]{3,1,2,0:T(8,128)(2,1)S(1)}, u32[]{:S(2)}, u32[]{:S(2)}) collective-permute-start(bf16[1,42,1,128]{3,1,2,0:T(8,128)(2,1)S(1)} %get-tuple-element.52), channel_id=1, source_target_pairs={{0,1},{1,2},{2,3},{3,4},{4,5},{5,6},{6,7},{7,0},{8,9},{9,10},{10,1... | collective-permute-start | bytes 32264 | tf_op jit(solution)/shard_map/ppermute | solution.py:16
  74.5 12.1 %collective-permute-start.7 = (bf16[1,42,1,128]{3,1,2,0:T(8,128)(2,1)S(1)}, bf16[1,42,1,128]{3,1,2,0:T(8,128)(2,1)S(1)}, u32[]{:S(2)}, u32[]{:S(2)}) collective-permute-start(bf16[1,42,1,128]{3,1,2,0:T(8,128)(2,1)S(1)} %get-tuple-element.53), channel_id=1, source_target_pairs={{1,0},{2,1},{3,2},{4,3},{5,4},{6,5},{7,6},{0,7},{9,8},{10,9},{11,1... | collective-permute-start | bytes 32264 | tf_op jit(solution)/shard_map/ppermute | solution.py:19
  78.6 2.9 %copy-start.3 = (bf16[82,1,8,18,128]{4,2,3,0,1:T(8,128)(2,1)S(1)}, bf16[82,1,8,18,128]{4,2,3,0,1:T(8,128)(2,1)}, u32[]{:S(2)}) copy-start(bf16[82,1,8,18,128]{4,2,3,0,1:T(8,128)(2,1)} %copy-done.2) | copy-start | bytes 9068548
  81.7 2.5 %copy-start.1 = (bf16[82,1,144,128]{3,0,2,1:T(8,128)(2,1)S(1)}, bf16[82,1,144,128]{3,0,2,1:T(8,128)(2,1)}, u32[]{:S(2)}) copy-start(bf16[82,1,144,128]{3,0,2,1:T(8,128)(2,1)} %copy-done) | copy-start | bytes 9068548
  86.6 1.0 copy-start.27
  87.3 4.8 %copy-start.4 = (bf16[42,1,8,9,128]{4,2,3,0,1:T(8,128)(2,1)}, bf16[42,1,8,9,128]{4,2,3,0,1:T(8,128)(2,1)S(1)}, u32[]{:S(2)}) copy-start(bf16[42,1,8,9,128]{4,2,3,0,1:T(8,128)(2,1)S(1)} %copy.33) | copy-start | bytes 2322436
  87.5 2.0 copy-start.25
  89.5 3.3 %copy-start.16 = (bf16[40,8,9,128]{3,1,2,0:T(8,128)(2,1)}, bf16[40,8,9,128]{3,1,2,0:T(8,128)(2,1)S(1)}, u32[]{:S(2)}) copy-start(bf16[40,8,9,128]{3,1,2,0:T(8,128)(2,1)S(1)} %get-tuple-element.54) | copy-start | bytes 2211844
  92.0 1.0 copy-start.18
  92.2 11.0 %slice-start.1 = ((bf16[42,1,8,9,128]{4,2,3,0,1:T(8,128)(2,1)}), bf16[42,1,8,8,128]{4,2,3,0,1:T(8,128)(2,1)S(1)}, s32[]{:S(2)}) async-start(bf16[42,1,8,9,128]{4,2,3,0,1:T(8,128)(2,1)} %copy-done.4), calls=%async_computation.3 | async-start | bytes 1376256 | tf_op jit(solution)/shard_map/concatenate | solution.py:20
  93.7 26.9 %collective-permute-start.17 = (bf16[1,1,64,128]{3,1,2,0:T(2,128)(2,1)}, bf16[1,1,64,128]{3,1,2,0:T(2,128)(2,1)}, u32[]{:S(2)}, u32[]{:S(2)}) collective-permute-start(bf16[1,1,64,128]{3,1,2,0:T(2,128)(2,1)} %slice.181), channel_id=1, source_target_pairs={{8,0},{16,8},{24,16},{32,24},{40,32},{48,40},{56,48},{9,1},{17,9},... | collective-permute-start | bytes 49160 | tf_op jit(solution)/shard_map/ppermute | solution.py:19
  95.6 24.2 %collective-permute-start.16 = (bf16[1,1,64,128]{3,2,1,0:T(8,128)(2,1)}, bf16[1,1,64,128]{3,2,1,0:T(8,128)(2,1)}, u32[]{:S(2)}, u32[]{:S(2)}) collective-permute-start(bf16[1,1,64,128]{3,2,1,0:T(8,128)(2,1)} %slice.178), channel_id=1, source_target_pairs={{0,8},{8,16},{16,24},{24,32},{32,40},{40,48},{48,56},{1,9},{9,17},... | collective-permute-start | bytes 49160 | tf_op jit(solution)/shard_map/ppermute | solution.py:16
  105.5 19.9 %collective-permute-start.8 = (bf16[1,1,64,128]{3,0,2,1:T(2,128)(2,1)S(1)}, bf16[1,1,64,128]{3,0,2,1:T(2,128)(2,1)S(1)}, u32[]{:S(2)}, u32[]{:S(2)}) collective-permute-start(bf16[1,1,64,128]{3,0,2,1:T(2,128)(2,1)S(1)} %slice.168), channel_id=1, source_target_pairs={{0,8},{8,16},{16,24},{24,32},{32,40},{40,48},{48,56},{1,9},{9,17},... | collective-permute-start | bytes 49160 | tf_op jit(solution)/shard_map/ppermute | solution.py:16
  111.5 4.5 %copy-start.7 = (bf16[82,8,18,128,1]{3,1,4,2,0:T(8,128)(2,1)S(1)}, bf16[82,8,18,128,1]{3,1,4,2,0:T(8,128)(2,1)}, u32[]{:S(2)}) copy-start(bf16[82,8,18,128,1]{3,1,4,2,0:T(8,128)(2,1)} %get-tuple-element.19) | copy-start | bytes 9068548
  111.5 4.5 %copy-start.8 = (bf16[82,8,18,128,1]{3,1,4,2,0:T(8,128)(2,1)S(1)}, bf16[82,8,18,128,1]{3,1,4,2,0:T(8,128)(2,1)}, u32[]{:S(2)}) copy-start(bf16[82,8,18,128,1]{3,1,4,2,0:T(8,128)(2,1)} %fusion.41) | copy-start | bytes 9068548
  111.5 4.5 %copy-start.10 = (bf16[82,8,18,128,1]{3,1,4,2,0:T(8,128)(2,1)S(1)}, bf16[82,8,18,128,1]{3,1,4,2,0:T(8,128)(2,1)}, u32[]{:S(2)}) copy-start(bf16[82,8,18,128,1]{3,1,4,2,0:T(8,128)(2,1)} %copy.78) | copy-start | bytes 9068548
  111.5 4.5 %copy-start.17 = (bf16[40,8,9,128]{3,1,2,0:T(8,128)(2,1)S(1)}, bf16[40,8,9,128]{3,1,2,0:T(8,128)(2,1)}, u32[]{:S(2)}) copy-start(bf16[40,8,9,128]{3,1,2,0:T(8,128)(2,1)} %copy-done.16) | copy-start | bytes 2211844
  111.5 4.5 %copy-start.31 = (pred[8,9]{0,1:T(8,128)(4,1)S(1)}, pred[8,9]{0,1:T(8,128)(4,1)}, u32[]{:S(2)}) copy-start(pred[8,9]{0,1:T(8,128)(4,1)} %constant.56) | copy-start | bytes 220
  116.1 2.3 %copy-start.29 = (bf16[1,8,9,128]{3,1,2,0:T(8,128)(2,1)S(1)}, bf16[1,8,9,128]{3,1,2,0:T(8,128)(2,1)}, u32[]{:S(2)}) copy-start(bf16[1,8,9,128]{3,1,2,0:T(8,128)(2,1)} %get-tuple-element.46) | copy-start | bytes 55300
  118.5 8.4 %collective-permute-start.9 = (bf16[1,1,64,128]{3,0,2,1:T(2,128)(2,1)S(1)}, bf16[1,1,64,128]{3,0,2,1:T(2,128)(2,1)S(1)}, u32[]{:S(2)}, u32[]{:S(2)}) collective-permute-start(bf16[1,1,64,128]{3,0,2,1:T(2,128)(2,1)S(1)} %slice.171), channel_id=1, source_target_pairs={{8,0},{16,8},{24,16},{32,24},{40,32},{48,40},{56,48},{9,1},{17,9},... | collective-permute-start | bytes 49160 | tf_op jit(solution)/shard_map/ppermute | solution.py:19
  121.2 10.8 %collective-permute-start.18 = (bf16[1,42,1,128]{3,1,2,0:T(8,128)(2,1)S(1)}, bf16[1,42,1,128]{3,1,2,0:T(8,128)(2,1)S(1)}, u32[]{:S(2)}, u32[]{:S(2)}) collective-permute-start(bf16[1,42,1,128]{3,1,2,0:T(8,128)(2,1)S(1)} %get-tuple-element.50), channel_id=1, source_target_pairs={{0,1},{1,2},{2,3},{3,4},{4,5},{5,6},{6,7},{7,0},{8,9},{9,10},{10,1... | collective-permute-start | bytes 32264 | tf_op jit(solution)/shard_map/ppermute | solution.py:16
  121.3 10.7 %collective-permute-start.19 = (bf16[1,42,1,128]{3,1,2,0:T(8,128)(2,1)S(1)}, bf16[1,42,1,128]{3,1,2,0:T(8,128)(2,1)S(1)}, u32[]{:S(2)}, u32[]{:S(2)}) collective-permute-start(bf16[1,42,1,128]{3,1,2,0:T(8,128)(2,1)S(1)} %get-tuple-element.51), channel_id=1, source_target_pairs={{1,0},{2,1},{3,2},{4,3},{5,4},{6,5},{7,6},{0,7},{9,8},{10,9},{11,1... | collective-permute-start | bytes 32264 | tf_op jit(solution)/shard_map/ppermute | solution.py:19
  126.9 8.5 %copy-start.13 = (bf16[1,42,64,128]{3,0,2,1:T(2,128)(2,1)}, bf16[1,42,64,128]{3,0,2,1:T(2,128)(2,1)S(1)}, u32[]{:S(2)}) copy-start(bf16[1,42,64,128]{3,0,2,1:T(2,128)(2,1)S(1)} %constant_dynamic-update-slice_fusion.3) | copy-start | bytes 2064388
  127.0 6.5 %copy-start.28 = (bf16[3,3,128,128]{3,2,1,0:T(8,128)(2,1)S(1)}, bf16[3,3,128,128]{3,2,1,0:T(8,128)(2,1)}, u32[]{:S(2)}) copy-start(bf16[3,3,128,128]{3,2,1,0:T(8,128)(2,1)} %all_gather.10) | copy-start | bytes 884740
  127.6 20.8 %collective-permute-start.10 = (bf16[1,42,1,128]{3,0,2,1:T(2,128)(2,1)}, bf16[1,42,1,128]{3,0,2,1:T(2,128)(2,1)}, u32[]{:S(2)}, u32[]{:S(2)}) collective-permute-start(bf16[1,42,1,128]{3,0,2,1:T(2,128)(2,1)} %get-tuple-element.33), channel_id=1, source_target_pairs={{0,1},{1,2},{2,3},{3,4},{4,5},{5,6},{6,7},{7,0},{8,9},{9,10},{10,1... | collective-permute-start | bytes 32264 | tf_op jit(solution)/shard_map/ppermute | solution.py:16
  127.6 20.8 %collective-permute-start.11 = (bf16[1,42,1,128]{3,0,2,1:T(2,128)(2,1)}, bf16[1,42,1,128]{3,0,2,1:T(2,128)(2,1)}, u32[]{:S(2)}, u32[]{:S(2)}) collective-permute-start(bf16[1,42,1,128]{3,0,2,1:T(2,128)(2,1)} %get-tuple-element.34), channel_id=1, source_target_pairs={{1,0},{2,1},{3,2},{4,3},{5,4},{6,5},{7,6},{0,7},{9,8},{10,9},{11,1... | collective-permute-start | bytes 32264 | tf_op jit(solution)/shard_map/ppermute | solution.py:19
  133.1 2.9 %copy-start.9 = (bf16[82,8,18,128,1]{3,1,4,2,0:T(8,128)(2,1)S(1)}, bf16[82,8,18,128,1]{3,1,4,2,0:T(8,128)(2,1)}, u32[]{:S(2)}) copy-start(bf16[82,8,18,128,1]{3,1,4,2,0:T(8,128)(2,1)} %copy.63) | copy-start | bytes 9068548
  133.5 2.5 %copy-start.5 = (bf16[82,8,18,128,1]{3,1,4,2,0:T(8,128)(2,1)S(1)}, bf16[82,8,18,128,1]{3,1,4,2,0:T(8,128)(2,1)}, u32[]{:S(2)}) copy-start(bf16[82,8,18,128,1]{3,1,4,2,0:T(8,128)(2,1)} %get-tuple-element.15) | copy-start | bytes 9068548
  133.5 3.4 %copy-start.6 = (bf16[82,8,18,128,1]{3,1,4,2,0:T(8,128)(2,1)S(1)}, bf16[82,8,18,128,1]{3,1,4,2,0:T(8,128)(2,1)}, u32[]{:S(2)}) copy-start(bf16[82,8,18,128,1]{3,1,4,2,0:T(8,128)(2,1)} %fusion.38) | copy-start | bytes 9068548
  136.9 2.8 %copy-start.22 = (f32[3,3,128,128]{3,2,1,0:T(8,128)S(1)}, f32[3,3,128,128]{3,2,1,0:T(8,128)}, u32[]{:S(2)}) copy-start(f32[3,3,128,128]{3,2,1,0:T(8,128)} %fusion.85) | copy-start | bytes 1769476
  140.1 18.7 %collective-permute-start.24 = (bf16[9,3,64,128]{3,2,1,0:T(8,128)(2,1)S(1)}, bf16[9,3,64,128]{3,2,1,0:T(8,128)(2,1)S(1)}, u32[]{:S(2)}, u32[]{:S(2)}) collective-permute-start(bf16[9,3,64,128]{3,2,1,0:T(8,128)(2,1)S(1)} %dynamic-slice_convert_fusion), channel_id=1, source_target_pairs={{0,64},{64,0},{1,65},{65,1},{2,66},{66,2},{3,67},{67,3},{4,68},{68... | collective-permute-start | bytes 1327112 | tf_op jit(solution)/shard_map/ppermute | solution.py:77
  140.2 12.7 %collective-permute-start.20 = (bf16[1,1,64,128]{3,0,2,1:T(2,128)(2,1)S(1)}, bf16[1,1,64,128]{3,0,2,1:T(2,128)(2,1)S(1)}, u32[]{:S(2)}, u32[]{:S(2)}) collective-permute-start(bf16[1,1,64,128]{3,0,2,1:T(2,128)(2,1)S(1)} %slice.184), channel_id=1, source_target_pairs={{0,8},{8,16},{16,24},{24,32},{32,40},{40,48},{48,56},{1,9},{9,17},... | collective-permute-start | bytes 49160 | tf_op jit(solution)/shard_map/ppermute | solution.py:16
  147.1 7.4 %collective-permute-start.21 = (bf16[1,1,64,128]{3,0,2,1:T(2,128)(2,1)S(1)}, bf16[1,1,64,128]{3,0,2,1:T(2,128)(2,1)S(1)}, u32[]{:S(2)}, u32[]{:S(2)}) collective-permute-start(bf16[1,1,64,128]{3,0,2,1:T(2,128)(2,1)S(1)} %slice.187), channel_id=1, source_target_pairs={{8,0},{16,8},{24,16},{32,24},{40,32},{48,40},{56,48},{9,1},{17,9},... | collective-permute-start | bytes 49160 | tf_op jit(solution)/shard_map/ppermute | solution.py:19
  153.0 17.8 %copy-start.26 = (bf16[3,3,128,128]{3,2,1,0:T(8,128)(2,1)S(1)}, bf16[3,3,128,128]{3,2,1,0:T(8,128)(2,1)}, u32[]{:S(2)}) copy-start(bf16[3,3,128,128]{3,2,1,0:T(8,128)(2,1)} %all_gather.11) | copy-start | bytes 884740
  154.5 4.3 %copy-start.14 = (bf16[1,42,64,128]{3,0,2,1:T(2,128)(2,1)}, bf16[1,42,64,128]{3,0,2,1:T(2,128)(2,1)S(1)}, u32[]{:S(2)}) copy-start(bf16[1,42,64,128]{3,0,2,1:T(2,128)(2,1)S(1)} %constant_dynamic-update-slice_fusion.8) | copy-start | bytes 2064388
  154.6 38.2 %collective-permute-start.22 = (bf16[1,42,1,128]{3,0,2,1:T(2,128)(2,1)S(1)}, bf16[1,42,1,128]{3,0,2,1:T(2,128)(2,1)S(1)}, u32[]{:S(2)}, u32[]{:S(2)}) collective-permute-start(bf16[1,42,1,128]{3,0,2,1:T(2,128)(2,1)S(1)} %get-tuple-element.31), channel_id=1, source_target_pairs={{0,1},{1,2},{2,3},{3,4},{4,5},{5,6},{6,7},{7,0},{8,9},{9,10},{10,1... | collective-permute-start | bytes 32264 | tf_op jit(solution)/shard_map/ppermute | solution.py:16
  154.7 38.1 %collective-permute-start.23 = (bf16[1,42,1,128]{3,0,2,1:T(2,128)(2,1)S(1)}, bf16[1,42,1,128]{3,0,2,1:T(2,128)(2,1)S(1)}, u32[]{:S(2)}, u32[]{:S(2)}) collective-permute-start(bf16[1,42,1,128]{3,0,2,1:T(2,128)(2,1)S(1)} %get-tuple-element.32), channel_id=1, source_target_pairs={{1,0},{2,1},{3,2},{4,3},{5,4},{6,5},{7,6},{0,7},{9,8},{10,9},{11,1... | collective-permute-start | bytes 32264 | tf_op jit(solution)/shard_map/ppermute | solution.py:19
  159.9 35.9 %all-to-all-start = ((bf16[64,27,128]{2,1,0:T(8,128)(2,1)}), bf16[64,27,128]{2,1,0:T(8,128)(2,1)S(1)}, u32[]{:S(2)}, u32[]{:S(2)}) async-start(bf16[64,27,128]{2,1,0:T(8,128)(2,1)} %reshape.20), calls=%async_computation | async-start | bytes 1048576 | tf_op jit(solution)/shard_map/all_to_all | solution.py:80
  190.8 2.0 copy-start.15
  192.8 14.5 %copy-start.12 = (bf16[1,80,128,128]{3,2,1,0:T(8,128)(2,1)S(1)}, bf16[1,80,128,128]{3,2,1,0:T(8,128)(2,1)}, u32[]{:S(2)}) copy-start(bf16[1,80,128,128]{3,2,1,0:T(8,128)(2,1)} %param.9) | copy-start | bytes 7864324
  192.8 14.5 %copy-start.24 = (bf16[3,3,128,128]{3,2,1,0:T(8,128)(2,1)S(1)}, bf16[3,3,128,128]{3,2,1,0:T(8,128)(2,1)}, u32[]{:S(2)}) copy-start(bf16[3,3,128,128]{3,2,1,0:T(8,128)(2,1)} %all_gather.9) | copy-start | bytes 884740
  196.8 33.3 %all-to-all-start.1 = ((bf16[64,27,128]{2,1,0:T(8,128)(2,1)}), bf16[64,27,128]{2,1,0:T(8,128)(2,1)S(1)}, u32[]{:S(2)}, u32[]{:S(2)}) async-start(bf16[64,27,128]{2,1,0:T(8,128)(2,1)} %broadcast_in_dim.2), calls=%async_computation.1 | async-start | bytes 1048576 | tf_op jit(solution)/shard_map/all_to_all | solution.py:82

commit v2 on v0

v2 whole, which is shorter than its diff:
```python
import functools
import math

import jax
import jax.numpy as jnp
from jax import lax
from jax.experimental import pallas as pl
from jax.experimental.pallas import tpu as pltpu
from jax.sharding import PartitionSpec as P

BF16 = jnp.bfloat16
F32 = jnp.float32
C = 128
FIELD_LOW, FIELD_HIGH = 5, 6
COT_LOW, COT_HIGH = 3, 4
ROWS = 5
EDGE = 16
TAPS = 32


def dot(left, right):
    return jnp.dot(left, right, preferred_element_type=F32)


def flat(value):
    return value.reshape(-1, value.shape[-1])


def split_row(stage, row, dest, pair, parity, west, west_at, east):
    wide = row.shape[0]
    stage[24 : 24 + wide, :] = row.astype(F32)
    stage[west_at : west_at + west.shape[0], :] = west.astype(F32)
    stage[24 + wide : 24 + wide + east.shape[0], :] = east.astype(F32)
    own = wide // 2 + 8
    for tap in range(3):
        upper = stage[pl.ds(23 + tap, own, stride=2), :]
        lower = stage[pl.ds(7 + tap, 8, stride=2), :]
        dest[pair, parity, :, tap * C : (tap + 1) * C] = jnp.concatenate(
            [upper, lower], axis=0
        ).astype(BF16)


def fine_taps(source, source_row, pair, parity, count):
    return flat(source[pl.ds(source_row + pair, count), parity])


def grads_kernel(
    half_rows,
    half_cols,
    bands,
    scale,
    where,
    fields,
    cot,
    low,
    high,
    west,
    east,
    w_down,
    w_mid,
    w_up_t,
    w_mid_t,
    own_out,
    other_out,
    mid_pairs,
    grad_pairs,
    field_taps,
    cot_taps,
    down_taps,
    pre_taps,
    stage,
    line,
    acc,
):
    lat = where[0]
    part = where[1]
    slots = half_cols + EDGE
    wide = half_cols + 8
    rows = 2 * half_rows

    def field_row(k, row, p, pair, parity):
        split_row(
            stage.at[k], row, field_taps, pair, parity, west[p], 16, east[p, 0:8]
        )

    def cot_row(k, row, p, pair, parity):
        split_row(
            stage.at[k],
            row,
            cot_taps,
            pair,
            parity,
            west[p, 0:COT_LOW],
            24 - COT_LOW,
            east[p, FIELD_HIGH : FIELD_HIGH + COT_HIGH],
        )

    for k in range(FIELD_LOW):
        field_row(k % 4, low[k], k, k // 2, k % 2)
    for k in range(COT_LOW):
        cot_row(k % 4, low[FIELD_LOW + k], k + 2, k // 2, k % 2)
    for k in range(FIELD_HIGH):
        p = FIELD_LOW + rows + k
        field_row(k % 4, high[k], p, p // 2, p % 2)
    for k in range(COT_HIGH):
        p = COT_LOW + rows + k
        cot_row(k % 4, high[FIELD_HIGH + k], p + 2, p // 2, p % 2)

    def own_rows(t, carry):
        for k in range(4):
            q = 4 * t + k
            field_row(k, fields[q], q + FIELD_LOW, 2 * t + (k + FIELD_LOW) // 2, (k + FIELD_LOW) % 2)
        for k in range(4):
            q = 4 * t + k
            cot_row(k, cot[q], q + FIELD_LOW, 2 * t + (k + COT_LOW) // 2, (k + COT_LOW) % 2)
        return carry

    lax.fori_loop(0, rows // 4, own_rows, 0)

    def on_grid(value, first):
        at = lat * half_rows + first + lax.broadcasted_iota(jnp.int32, value.shape, 0)
        return jnp.where((at >= 0) & (at < bands * half_rows), value, 0.0)

    def lay(value):
        line[:, 8 : 16, :] = value[:, wide:]
        line[:, 16 : 16 + wide, :] = value[:, :wide]

    def shifted(shift):
        upper = line[:, 16 + shift : 16 + shift + wide, :]
        lower = line[:, 8 + shift : 16 + shift, :]
        return jnp.concatenate([upper, lower], axis=1).astype(BF16)

    def strip(value):
        return value.reshape(ROWS, slots, C)

    def down_strip(t, carry):
        a = ROWS * t
        left = jnp.concatenate(
            [fine_taps(field_taps, a, r // 2, r % 2, ROWS) for r in range(3)], axis=1
        )
        value = on_grid(strip(dot(left, w_down[...])), a - 2)
        lay(value)
        for shift in range(3):
            down_taps[pl.ds(a, ROWS), :, shift * C : (shift + 1) * C] = shifted(shift - 1)
        return carry

    lax.fori_loop(0, half_rows // ROWS + 1, down_strip, 0)

    def pre_strip(t, carry):
        b = ROWS * t
        left = jnp.concatenate([flat(down_taps[pl.ds(b + r, ROWS)]) for r in range(3)], axis=1)
        pre = strip(dot(left, w_mid[...]))
        left = jnp.concatenate(
            [fine_taps(cot_taps, b, r // 2, r % 2, ROWS) for r in range(3)], axis=1
        )
        grad = strip(dot(left, w_up_t[...]))
        sig = jax.nn.sigmoid(pre)
        lay(on_grid(pre * sig, b - 1))
        for shift in range(2):
            mid_pairs[pl.ds(b, ROWS), :, shift * C : (shift + 1) * C] = line[
                :, 16 + shift : 16 + shift + half_cols, :
            ].astype(BF16)
        lay(on_grid(grad * sig * (1.0 + pre * (1.0 - sig)), b - 1))
        for shift in range(3):
            pre_taps[pl.ds(b, ROWS), :, shift * C : (shift + 1) * C] = shifted(shift - 1)
        return carry

    lax.fori_loop(0, half_rows // ROWS + 1, pre_strip, 0)

    def back_strip(t, carry):
        d = ROWS * t
        left = jnp.concatenate([flat(pre_taps[pl.ds(d + r, ROWS)]) for r in range(3)], axis=1)
        lay(on_grid(strip(dot(left, w_mid_t[...])), d))
        for shift in range(2):
            grad_pairs[pl.ds(d, ROWS), :, shift * C : (shift + 1) * C] = line[
                :, 16 + shift : 16 + shift + half_cols, :
            ].astype(BF16)
        return carry

    lax.fori_loop(0, half_rows // ROWS + 1, back_strip, 0)

    acc[...] = jnp.zeros_like(acc)
    step = 8

    def outer(left, right):
        return lax.dot_general(left, right, (((0,), (0,)), ((), ())), preferred_element_type=F32)

    def outer_strip(t, carry):
        i = step * t
        here = slice(0, half_cols)
        right = jnp.concatenate(
            [flat(field_taps[pl.ds(i + 2 + r // 2, step), r % 2, here]) for r in range(3)], axis=1
        )
        acc[0] += outer(flat(grad_pairs[pl.ds(i, step), :, 0:C]), right)
        right = jnp.concatenate(
            [flat(pre_taps[pl.ds(i + r, step), here]) for r in range(3)], axis=1
        )
        acc[1] += outer(flat(down_taps[pl.ds(i + 2, step), here, C : 2 * C]), right)
        right = jnp.concatenate(
            [flat(cot_taps[pl.ds(i + 1 + r // 2, step), r % 2, here]) for r in range(3)], axis=1
        )
        acc[2] += outer(flat(mid_pairs[pl.ds(i + 1, step), :, 0:C]), right)
        return carry

    lax.fori_loop(0, half_rows // step, outer_strip, 0)

    half = C // 2
    for tap in range(9):
        at = slice(tap * C, (tap + 1) * C)
        acc[0, :, at] = acc[0, :, at].T
    mine = pl.ds(pl.multiple_of(part * half, half), half)
    theirs = pl.ds(pl.multiple_of((1 - part) * half, half), half)
    for kind in range(3):
        for tap in range(9):
            held = 8 - tap if kind == 1 else tap
            at = slice(held * C, (held + 1) * C)
            own_out[kind * 9 + tap] = acc[kind, mine, at] * scale
            other_out[kind * 9 + tap] = (acc[kind, theirs, at] * scale).astype(BF16)
    for tap in range(27, TAPS):
        own_out[tap] = jnp.zeros((half, C), F32)
        other_out[tap] = jnp.zeros((half, C), BF16)


def up_kernel(mid_pairs, grad_pairs, fields, cot, u1, u2, u3, level_out, grad_fields, whole):
    first = ROWS * pl.program_id(0)
    half_cols = mid_pairs.shape[1]

    def spread(pairs, at, base, out, which):
        near = flat(pairs[pl.ds(at, ROWS)])
        far = flat(pairs[pl.ds(at + 1, ROWS)])
        odd = dot(near, u1[which])
        last = dot(far, u2[which])
        even = dot(jnp.concatenate([near[:, :C], far[:, :C]], axis=1), u3[which])
        for k in range(ROWS):
            at_k = slice(k * half_cols, (k + 1) * half_cols)
            whole[2 * k, pl.ds(0, half_cols, stride=2), :] = even[at_k, :C]
            whole[2 * k, pl.ds(1, half_cols, stride=2), :] = odd[at_k, :C]
            whole[2 * k + 1, pl.ds(0, half_cols, stride=2), :] = even[at_k, C:]
            whole[2 * k + 1, pl.ds(1, half_cols, stride=2), :] = odd[at_k, C:] + last[at_k]
        out[...] = (base[...].astype(F32) + whole[...]).astype(BF16)

    spread(mid_pairs, first + 1, fields, level_out, 0)
    spread(grad_pairs, first, cot, grad_fields, 1)


def halos(fields, cot):
    lat = lax.axis_size("lat")
    lon = lax.axis_size("lon")
    up = [(i, i + 1) for i in range(lat - 1)]
    low = lax.ppermute(
        jnp.concatenate([fields[-FIELD_LOW:], cot[-COT_LOW:]], axis=0), "lat", up
    )
    high = lax.ppermute(
        jnp.concatenate([fields[:FIELD_HIGH], cot[:COT_HIGH]], axis=0),
        "lat",
        [(j, i) for i, j in up],
    )

    def columns(at_field, at_cot):
        field = jnp.concatenate(
            [low[:FIELD_LOW, at_field], fields[:, at_field], high[:FIELD_HIGH, at_field]], axis=0
        )
        other = jnp.concatenate(
            [low[FIELD_LOW:, at_cot], cot[:, at_cot], high[FIELD_HIGH:, at_cot]], axis=0
        )
        return field, jnp.pad(other, ((2, 2), (0, 0), (0, 0)))

    field, other = columns(slice(-FIELD_LOW, None), slice(-COT_LOW, None))
    around = [(i, (i + 1) % lon) for i in range(lon)]
    west = lax.ppermute(jnp.concatenate([other, field], axis=1), "lon", around)
    field, other = columns(slice(0, FIELD_HIGH), slice(0, COT_HIGH))
    east = lax.ppermute(
        jnp.concatenate([field, other], axis=1), "lon", [(j, i) for i, j in around]
    )
    return low, high, west, east


def swap_io(kernel):
    return jnp.transpose(kernel, (0, 1, 3, 2))


def spread_weights(kernel):
    none = jnp.zeros((C, C), kernel.dtype)
    k = kernel
    u1 = jnp.block([[k[1, 2], k[2, 2]], [k[1, 0], k[2, 0]]])
    u2 = jnp.concatenate([k[0, 2], k[0, 0]], axis=0)
    u3 = jnp.block([[k[1, 1], k[2, 1]], [none, k[0, 1]]])
    return u1, u2, u3


def body(fields, down_weight, mid_weight, up_weight, cotangent):
    lats, lons, parts = (lax.axis_size(axis) for axis in ("lat", "lon", "dp"))
    _, rows, cols, _ = fields.shape
    half_rows, half_cols = rows // 2, cols // 2
    scale = 1.0 / math.sqrt(parts * rows * lats * cols * lons)
    fields, cotangent = fields[0], cotangent[0]
    part = lax.axis_index("dp")
    low, high, west, east = halos(fields, cotangent)
    weights = lax.all_gather(
        jnp.stack([down_weight, mid_weight, up_weight]), "dp", axis=3, tiled=True
    )
    down_w, mid_w, up_w = weights[0], weights[1], weights[2]
    where = jnp.stack([lax.axis_index("lat"), part]).astype(jnp.int32)

    vmem = pl.BlockSpec(memory_space=pltpu.VMEM)
    slots = half_cols + EDGE
    strips = half_rows + ROWS
    own, other, mid_pairs, grad_pairs = pl.pallas_call(
        functools.partial(grads_kernel, half_rows, half_cols, lats, scale),
        out_shape=(
            jax.ShapeDtypeStruct((TAPS, C // 2, C), F32),
            jax.ShapeDtypeStruct((TAPS, C // 2, C), BF16),
            jax.ShapeDtypeStruct((strips, half_cols, 2 * C), BF16),
            jax.ShapeDtypeStruct((strips, half_cols, 2 * C), BF16),
        ),
        in_specs=[pl.BlockSpec(memory_space=pltpu.SMEM)] + [vmem] * 10,
        out_specs=(vmem,) * 4,
        scratch_shapes=[
            pltpu.VMEM((strips + 1, 2, slots, 3 * C), BF16),
            pltpu.VMEM((strips + 1, 2, slots, 3 * C), BF16),
            pltpu.VMEM((strips + 2, slots, 3 * C), BF16),
            pltpu.VMEM((strips + 2, slots, 3 * C), BF16),
            pltpu.VMEM((4, cols + 48, C), F32),
            pltpu.VMEM((ROWS, slots + 16, C), F32),
            pltpu.VMEM((3, C, 9 * C), F32),
        ],
        compiler_params=pltpu.CompilerParams(vmem_limit_bytes=56 * 2**20),
        cost_estimate=pl.CostEstimate(
            flops=70 * 2 * half_rows * half_cols * C * C,
            transcendentals=half_rows * half_cols * C,
            bytes_accessed=8 * 2**20,
        ),
        name="grads",
    )(
        where,
        fields,
        cotangent,
        low,
        high,
        west,
        east,
        down_w.reshape(9 * C, C),
        mid_w.reshape(9 * C, C),
        swap_io(up_w).reshape(9 * C, C),
        swap_io(mid_w)[::-1, ::-1].reshape(9 * C, C),
    )

    spreads = [
        jnp.stack(pair) for pair in zip(spread_weights(up_w), spread_weights(swap_io(down_w)))
    ]
    block = pl.BlockSpec((2 * ROWS, cols, C), lambda i: (i, 0, 0))

    def held(array):
        return pl.BlockSpec(array.shape, lambda i: (0,) * array.ndim)

    level_out, grad_fields = pl.pallas_call(
        up_kernel,
        grid=(half_rows // ROWS,),
        out_shape=(jax.ShapeDtypeStruct(fields.shape, BF16),) * 2,
        in_specs=[held(mid_pairs), held(grad_pairs), block, block] + [held(u) for u in spreads],
        out_specs=(block, block),
        scratch_shapes=[pltpu.VMEM((2 * ROWS, cols, C), F32)],
        compiler_params=pltpu.CompilerParams(vmem_limit_bytes=32 * 2**20),
        cost_estimate=pl.CostEstimate(
            flops=18 * 2 * half_rows * half_cols * C * C,
            transcendentals=0,
            bytes_accessed=13 * 2**20,
        ),
        name="spread",
    )(mid_pairs, grad_pairs, fields, cotangent, *spreads)

    came = lax.ppermute(other, "dp", [(0, 1), (1, 0)])
    both = (own + came.astype(F32)).astype(BF16)
    pieces = both.reshape(lats * lons, -1, C)
    pieces = lax.all_to_all(pieces, ("lat", "lon"), 0, 0, tiled=True)
    piece = jnp.sum(pieces.astype(F32), axis=0, keepdims=True).astype(BF16)
    totals = lax.all_to_all(
        jnp.broadcast_to(piece, pieces.shape), ("lat", "lon"), 0, 0, tiled=True
    )
    totals = totals.reshape(TAPS, C // 2, C).astype(F32)
    grad_down, grad_mid, grad_up = (
        totals[9 * k : 9 * k + 9].reshape(3, 3, C // 2, C) for k in range(3)
    )
    return (level_out[None], grad_fields[None], grad_down, grad_mid, grad_up)


def solution(mesh):
    field = P("dp", "lat", "lon", None)
    weight = P(None, None, "dp", None)
    return jax.shard_map(
        body,
        mesh=mesh,
        in_specs=(field, weight, weight, weight, field),
        out_specs=(field, field, weight, weight, weight),
        check_vma=False,
    )
```

time: 596 us -> 112 us (0.19)
  blocking collectives: 378 us -> 2.44 us
  matrix products: 59.4 us -> 0 us
  starting transfers between devices: 66.4 us -> 27.5 us
  Pallas kernels: 0 us -> 33 us
  local copies, waits for them, and re-layouts: 41.8 us -> 18.4 us
  other arithmetic: 29.3 us -> 7.36 us
  waiting for transfers between devices: 1.59 us -> 21.6 us
  between operations: 14.9 us -> 0.86 us
    psum x1 -> x0, blocking collectives: 368 us -> none  [body(): totals = lax.psum((down_term, mid_term, up_term), ('lat', 'lon'))]
    ppermute x24 -> x5, starting transfers between devices: 66.1 us -> 10.8 us  [the longest x1 5.2 us: halos(): lax.ppermute(jnp.concatenate([fields[-FIELD_LOW:], cot[-COT_LOW:]], axis=...]
    conv_general_dilated x7 -> x0, matrix products: 53.5 us -> none  [the longest x6 48.2 us: convolve(): lax.conv_general_dilated(padded, kernel, (stride, stride), padding, lhs_d...]
    pallas_call x0 -> x2, Pallas kernels: none -> 33 us  [the longest x1 27.6 us: body(): pl.pallas_call(functools.partial(grads_kernel, half_rows, half_cols, lats...]
    all_to_all x0 -> x2, starting transfers between devices: none -> 16.8 us  [the longest x1 12 us: body(): pieces = lax.all_to_all(pieces, ('lat', 'lon'), 0, 0, tiled=True)]
    concatenate x10 -> x6, other arithmetic: 17 us -> 0.38 us  [the longest x1 0.14 us: halos(): jnp.concatenate([field, other], axis=1)]
    unnamed x76 -> x16, local copies, waits for them, and re-layouts: 16.7 us -> 4.26 us
    all_to_all x0 -> x2, waiting for transfers between devices: none -> 12.4 us  [the longest x1 10.1 us: body(): pieces = lax.all_to_all(pieces, ('lat', 'lon'), 0, 0, tiled=True)]
  transfers between devices with their start and end apart: 27 -> 7, of which waited for: 2 -> 5; matrix products, arithmetic and copies ran while one was open for 17% -> 14% of each run, Pallas kernels for 0% -> 5%
where the time goes in v2:
time: 112 us; the launch traced here: 111 us
  Pallas kernels  33 us (29%)
  starting transfers between devices  27.5 us (25%)
  waiting for transfers between devices  21.6 us (19%)
  local copies, waits for them, and re-layouts  18.4 us (16%)
  other arithmetic  7.36 us (7%)
  blocking collectives  2.44 us (2%)
    pallas_call x1, Pallas kernels, body(): pl.pallas_call(functools.partial(grads_kernel, half_rows, half_cols, lats...  27.6 us
    all_to_all x1, starting transfers between devices, body(): pieces = lax.all_to_all(pieces, ('lat', 'lon'), 0, 0, tiled=True)  12 us
    all_to_all x1, waiting for transfers between devices, body(): pieces = lax.all_to_all(pieces, ('lat', 'lon'), 0, 0, tiled=True)  10.1 us
    pallas_call x1, Pallas kernels, body(): pl.pallas_call(up_kernel, grid=(half_rows // ROWS,), out_shape=(jax.Shape...  5.41 us
    ppermute x1, starting transfers between devices, halos(): lax.ppermute(jnp.concatenate([fields[-FIELD_LOW:], cot[-COT_LOW:]], axis=...  5.2 us
    all_to_all x1, starting transfers between devices, body(): lax.all_to_all(jnp.broadcast_to(piece, pieces.shape), ('lat', 'lon'), 0,...  4.73 us
    unnamed x16, local copies, waits for them, and re-layouts  4.26 us
    ppermute x1, waiting for transfers between devices, halos(): lax.ppermute(jnp.concatenate([fields[:FIELD_HIGH], cot[:COT_HIGH]], axis=...  4.07 us
  transfers between devices with their start and end apart: 7, of which 5 were waited for; matrix products, arithmetic and copies ran while one was open for 14% of the time, Pallas kernels for 5%

profile of v2, /device:TPU:0, one launch (start us, length us, event | category | flops | bytes accessed | tf_op | source)
XLA Modules:
  0.0 111.2 jit_solution(14464725397970066485)
XLA Ops:
  0.6 0.9 slice_bitcast_fusion.5
  1.5 0.9 slice_bitcast_fusion.3
  2.5 5.2 %collective-permute-start = (bf16[8,128,128]{2,1,0:T(8,128)(2,1)S(1)}, bf16[8,128,128]{2,1,0:T(8,128)(2,1)S(1)}, u32[]{:S(2)}, u32[]{:S(2)}) collective-permute-start(bf16[8,128,128]{2,1,0:T(8,128)(2,1)S(1)} %pad_maximum_fusion.3), channel_id=1, source_target_pairs={{0,8},{8,16},{16,24},{24,32},{32,40},{40,48},{48,56},{1,9},{9,17},... | collective-permute-start | bytes 786440 | tf_op jit(solution)/shard_map/ppermute | solution.py:250
  7.7 0.9 slice_bitcast_fusion.4
  8.6 0.9 slice_bitcast_fusion.2
  9.6 1.3 %collective-permute-start.1 = (bf16[10,128,128]{2,1,0:T(8,128)(2,1)S(1)}, bf16[10,128,128]{2,1,0:T(8,128)(2,1)S(1)}, u32[]{:S(2)}, u32[]{:S(2)}) collective-permute-start(bf16[10,128,128]{2,1,0:T(8,128)(2,1)S(1)} %pad_maximum_fusion.2), channel_id=1, source_target_pairs={{8,0},{16,8},{24,16},{32,24},{40,32},{48,40},{56,48},{9,1},{17,9},... | collective-permute-start | bytes 983048 | tf_op jit(solution)/shard_map/ppermute | solution.py:253
  10.9 1.1 pad_maximum_fusion
  12.0 0.9 slice.189
  13.0 1.0 slice.180
  13.9 0.9 slice.186
  14.9 1.0 slice.183
  15.8 2.4 %all_gather.3 = bf16[3,3,3,128,128]{4,3,2,1,0:T(8,128)(2,1)S(1)} all-gather(bf16[3,3,3,64,128]{4,3,2,1,0:T(8,128)(2,1)S(1)} %pad_maximum_fusion), channel_id=1, replica_groups=mesh['dp'=2,'lat'=8,'lon'=8] {'dp'}, dimensions={3}, use_global_device_ids=true | all-gather | bytes 1327104 | tf_op jit(solution)/shard_map/all_gather | solution.py:299
  18.3 0.0 collective-permute-done.low
  18.3 0.0 copy-start.5
  18.3 4.1 %collective-permute-done.1.high = bf16[10,128,128]{2,1,0:T(8,128)(2,1)S(1)} collective-permute-done((bf16[10,128,128]{2,1,0:T(8,128)(2,1)S(1)}, bf16[10,128,128]{2,1,0:T(8,128)(2,1)S(1)}, u32[]{:S(2)}, u32[]{:S(2)}) %collective-permute-start.1) | collective-permute-done | bytes 327712 | tf_op jit(solution)/shard_map/ppermute | solution.py:253
  22.4 0.0 copy-start.4
  22.5 0.1 maximum_maximum_fusion
  22.6 1.6 %collective-permute-start.2 = (bf16[91,8,128]{2,1,0:T(8,128)(2,1)S(1)}, bf16[91,8,128]{2,1,0:T(8,128)(2,1)S(1)}, u32[]{:S(2)}, u32[]{:S(2)}) collective-permute-start(bf16[91,8,128]{2,1,0:T(8,128)(2,1)S(1)} %maximum_maximum_fusion), channel_id=1, source_target_pairs={{0,1},{1,2},{2,3},{3,4},{4,5},{5,6},{6,7},{7,0},{8,9},{9,10},{10,1... | collective-permute-start | bytes 559112 | tf_op jit(solution)/shard_map/ppermute | solution.py:270
  24.2 0.1 pad_maximum_fusion.1
  24.4 2.7 %collective-permute-start.3 = (bf16[91,10,128]{2,1,0:T(8,128)(2,1)S(1)}, bf16[91,10,128]{2,1,0:T(8,128)(2,1)S(1)}, u32[]{:S(2)}, u32[]{:S(2)}) collective-permute-start(bf16[91,10,128]{2,1,0:T(8,128)(2,1)S(1)} %pad_maximum_fusion.1), channel_id=1, source_target_pairs={{1,0},{2,1},{3,2},{4,3},{5,4},{6,5},{7,6},{0,7},{9,8},{10,9},{11,1... | collective-permute-start | bytes 698888 | tf_op jit(solution)/shard_map/ppermute | solution.py:272
  27.1 1.3 %slice_bitcast_fusion.1 = (bf16[3,3,128,128]{3,2,1,0:T(8,128)(2,1)S(1)}, bf16[3,3,128,128]{3,2,1,0:T(8,128)(2,1)S(1)}, bf16[3,3,128,128]{2,3,1,0:T(8,128)(2,1)S(...) fusion(bf16[3,3,3,128,128]{4,3,2,1,0:T(8,128)(2,1)S(1)} %all_ga, ...), kind=kLoop, calls=%fused_computation.15 | loop fusion | bytes 2654208 | tf_op jit(solution)/shard_map/squeeze | solution.py:302
  28.4 0.9 copy.12
  29.3 0.0 copy-done.5
  29.3 0.0 copy-done.4
  29.3 0.9 copy.11
  30.2 0.7 pad_add_fusion.where
  30.9 0.0 collective-permute-done.2.west
  30.9 0.0 copy-start.7
  30.9 3.0 %collective-permute-done.3.east = bf16[91,10,128]{2,1,0:T(8,128)(2,1)S(1)} collective-permute-done((bf16[91,10,128]{2,1,0:T(8,128)(2,1)S(1)}, bf16[91,10,128]{2,1,0:T(8,128)(2,1)S(1)}, u32[]{:S(2)}, u32[]{:S(2)}) %collective-permute-start.3) | collective-permute-done | bytes 232992 | tf_op jit(solution)/shard_map/ppermute | solution.py:272
  33.9 0.0 copy-start.6
  33.9 0.0 copy-done.7
  33.9 0.7 copy-done.6
  34.7 27.6 %grads.1 = (f32[32,64,128]{2,1,0:T(8,128)}, bf16[32,64,128]{2,1,0:T(8,128)(2,1)}, bf16[45,64,256]{2,1,0:T(8,128)(2,1)}, bf16[45,64,256]{2,1,0:T(8,128)(2,1)}) custom-call(s32[2]{0:T(128)} %pad_add_fusion.where, bf16[80,128,128]{2,1,0:T(8,128)(2,1)} %bitcast.87, bf16[80,128,128]{2,1,0:T(8,128)(2,1)} %bitcast.91, bf16[8,128,128]{2,1,0:T(8,128)(2,1)} %copy-done.5, ...), custom_call_target="tpu_custom_call" | custom-call | flops 5872025600 | bytes 8388608 | tf_op jit(solution)/shard_map/grads/pallas_call | solution.py:308
  62.2 0.0 collective-permute-start.4
  62.2 2.1 %collective-permute-done.4 = bf16[32,64,128]{2,1,0:T(8,128)(2,1)S(1)} collective-permute-done((bf16[32,64,128]{2,1,0:T(8,128)(2,1)}, bf16[32,64,128]{2,1,0:T(8,128)(2,1)S(1)}, u32[]{:S(2)}, u32[]{:S(2)}) %collective-permute-start.4) | collective-permute-done | bytes 524320 | tf_op jit(solution)/shard_map/ppermute | solution.py:372
  64.3 2.2 %add_convert_fusion = bf16[32,64,128]{2,1,0:T(8,128)(2,1)} fusion(f32[32,64,128]{2,1,0:T(8,128)} %get-tuple-element.15, bf16[32,64,128]{2,1,0:T(8,128)(2,1)S(1)} %collective-permute-done.4), kind=kLoop, calls=%fused_computation | loop fusion | flops 786432 | bytes 2097152 | tf_op jit(solution)/shard_map/convert_element_type | solution.py:373
  66.5 12.0 %all-to-all-start = ((bf16[64,32,128]{2,1,0:T(8,128)(2,1)}), bf16[64,32,128]{2,1,0:T(8,128)(2,1)S(1)}, u32[]{:S(2)}, u32[]{:S(2)}) async-start(bf16[64,32,128]{2,1,0:T(8,128)(2,1)} %bitcast.47), calls=%async_computation | async-start | bytes 1048576 | tf_op jit(solution)/shard_map/all_to_all | solution.py:375
  78.6 0.8 slice_bitcast_fusion.11
  79.3 0.2 copy.13
  79.5 0.0 copy-start
  79.5 0.7 slice_bitcast_fusion.8
  80.2 1.0 maximum_bitcast_fusion.2
  81.2 0.9 fusion.5
  82.1 10.1 %all-to-all-done = bf16[64,32,128]{2,1,0:T(8,128)(2,1)S(1)} async-done(((bf16[64,32,128]{2,1,0:T(8,128)(2,1)}), bf16[64,32,128]{2,1,0:T(8,128)(2,1)S(1)}, u32[]{:S(2)}, u32[]{:S(2)}) %all-to-all-start) | async-done | bytes 524320 | tf_op jit(solution)/shard_map/all_to_all | solution.py:375
  92.2 0.1 reduce_sum.12
  92.3 0.9 broadcast_in_dim.14
  93.2 4.7 %all-to-all-start.1 = ((bf16[64,32,128]{2,1,0:T(8,128)(2,1)}), bf16[64,32,128]{2,1,0:T(8,128)(2,1)S(1)}, u32[]{:S(2)}, u32[]{:S(2)}) async-start(bf16[64,32,128]{2,1,0:T(8,128)(2,1)} %broadcast_in_dim.14), calls=%async_computation.1 | async-start | bytes 1048576 | tf_op jit(solution)/shard_map/all_to_all | solution.py:377
  97.9 0.0 copy-start.2
  98.0 1.0 fusion.7
  99.0 0.0 copy-done
  99.1 0.4 copy-done.2
  99.4 0.0 copy-start.1
  99.4 1.7 %copy-done.1 = bf16[1,80,128,128]{3,2,1,0:T(8,128)(2,1)S(1)} copy-done((bf16[1,80,128,128]{3,2,1,0:T(8,128)(2,1)S(1)}, bf16[1,80,128,128]{3,2,1,0:T(8,128)(2,1)}, u32[]{:S(2)}) %copy-start.1) | copy-done | bytes 2621464
  101.2 0.0 copy-start.3
  101.2 1.4 %copy-done.3 = bf16[45,64,256]{2,1,0:T(8,128)(2,1)S(1)} copy-done((bf16[45,64,256]{2,1,0:T(8,128)(2,1)S(1)}, bf16[45,64,256]{2,1,0:T(8,128)(2,1)}, u32[]{:S(2)}) %copy-start.3) | copy-done | bytes 1474584
  102.6 5.4 %spread.1 = (bf16[80,128,128]{2,1,0:T(8,128)(2,1)}, bf16[80,128,128]{2,1,0:T(8,128)(2,1)}) custom-call(bf16[45,64,256]{2,1,0:T(8,128)(2,1)S(1)} %copy-done.2, bf16[45,64,256]{2,1,0:T(8,128)(2,1)S(1)} %copy-done.3, bf16[80,128,128]{2,1,0:T(8,128)(2,1)S(1)} %bitcast.88, bf16[80,128,128]{2,1,0:T(8,128)(2,1)S(1)} %bitcast.92, ...), custom_call_target="tpu_custom_call" | custom-call | flops 1509949440 | bytes 13631488 | tf_op jit(solution)/shard_map/spread/pallas_call | solution.py:356
  108.0 2.3 %all-to-all-done.1 = bf16[64,32,128]{2,1,0:T(8,128)(2,1)S(1)} async-done(((bf16[64,32,128]{2,1,0:T(8,128)(2,1)}), bf16[64,32,128]{2,1,0:T(8,128)(2,1)S(1)}, u32[]{:S(2)}, u32[]{:S(2)}) %all-to-all-start.1) | async-done | bytes 524320 | tf_op jit(solution)/shard_map/all_to_all | solution.py:377
  110.3 0.9 fusion.8
  (16 shorter events, 0.3 us)
Async XLA Ops:
  2.5 15.8 %collective-permute-start = (bf16[8,128,128]{2,1,0:T(8,128)(2,1)S(1)}, bf16[8,128,128]{2,1,0:T(8,128)(2,1)S(1)}, u32[]{:S(2)}, u32[]{:S(2)}) collective-permute-start(bf16[8,128,128]{2,1,0:T(8,128)(2,1)S(1)} %pad_maximum_fusion.3), channel_id=1, source_target_pairs={{0,8},{8,16},{16,24},{24,32},{32,40},{40,48},{48,56},{1,9},{9,17},... | collective-permute-start | bytes 786440 | tf_op jit(solution)/shard_map/ppermute | solution.py:250
  9.6 12.8 %collective-permute-start.1 = (bf16[10,128,128]{2,1,0:T(8,128)(2,1)S(1)}, bf16[10,128,128]{2,1,0:T(8,128)(2,1)S(1)}, u32[]{:S(2)}, u32[]{:S(2)}) collective-permute-start(bf16[10,128,128]{2,1,0:T(8,128)(2,1)S(1)} %pad_maximum_fusion.2), channel_id=1, source_target_pairs={{8,0},{16,8},{24,16},{32,24},{40,32},{48,40},{56,48},{9,1},{17,9},... | collective-permute-start | bytes 983048 | tf_op jit(solution)/shard_map/ppermute | solution.py:253
  18.3 11.1 %copy-start.5 = (bf16[8,128,128]{2,1,0:T(8,128)(2,1)}, bf16[8,128,128]{2,1,0:T(8,128)(2,1)S(1)}, u32[]{:S(2)}) copy-start(bf16[8,128,128]{2,1,0:T(8,128)(2,1)S(1)} %collective-permute-done.low) | copy-start | bytes 786436
  22.4 6.9 %copy-start.4 = (bf16[10,128,128]{2,1,0:T(8,128)(2,1)}, bf16[10,128,128]{2,1,0:T(8,128)(2,1)S(1)}, u32[]{:S(2)}) copy-start(bf16[10,128,128]{2,1,0:T(8,128)(2,1)S(1)} %collective-permute-done.1.high) | copy-start | bytes 983044
  22.6 8.3 %collective-permute-start.2 = (bf16[91,8,128]{2,1,0:T(8,128)(2,1)S(1)}, bf16[91,8,128]{2,1,0:T(8,128)(2,1)S(1)}, u32[]{:S(2)}, u32[]{:S(2)}) collective-permute-start(bf16[91,8,128]{2,1,0:T(8,128)(2,1)S(1)} %maximum_maximum_fusion), channel_id=1, source_target_pairs={{0,1},{1,2},{2,3},{3,4},{4,5},{5,6},{6,7},{7,0},{8,9},{9,10},{10,1... | collective-permute-start | bytes 559112 | tf_op jit(solution)/shard_map/ppermute | solution.py:270
  24.4 9.5 %collective-permute-start.3 = (bf16[91,10,128]{2,1,0:T(8,128)(2,1)S(1)}, bf16[91,10,128]{2,1,0:T(8,128)(2,1)S(1)}, u32[]{:S(2)}, u32[]{:S(2)}) collective-permute-start(bf16[91,10,128]{2,1,0:T(8,128)(2,1)S(1)} %pad_maximum_fusion.1), channel_id=1, source_target_pairs={{1,0},{2,1},{3,2},{4,3},{5,4},{6,5},{7,6},{0,7},{9,8},{10,9},{11,1... | collective-permute-start | bytes 698888 | tf_op jit(solution)/shard_map/ppermute | solution.py:272
  30.9 3.0 %copy-start.7 = (bf16[91,8,128]{2,1,0:T(8,128)(2,1)}, bf16[91,8,128]{2,1,0:T(8,128)(2,1)S(1)}, u32[]{:S(2)}) copy-start(bf16[91,8,128]{2,1,0:T(8,128)(2,1)S(1)} %collective-permute-done.2.west) | copy-start | bytes 559108
  33.9 0.8 copy-start.6
  62.2 2.1 %collective-permute-start.4 = (bf16[32,64,128]{2,1,0:T(8,128)(2,1)}, bf16[32,64,128]{2,1,0:T(8,128)(2,1)S(1)}, u32[]{:S(2)}, u32[]{:S(2)}) collective-permute-start(bf16[32,64,128]{2,1,0:T(8,128)(2,1)} %get-tuple-element.16), channel_id=1, source_target_pairs={{0,64},{64,0},{1,65},{65,1},{2,66},{66,2},{3,67},{67,3},{4,68},{68... | collective-permute-start | bytes 1572872 | tf_op jit(solution)/shard_map/ppermute | solution.py:372
  66.5 25.7 %all-to-all-start = ((bf16[64,32,128]{2,1,0:T(8,128)(2,1)}), bf16[64,32,128]{2,1,0:T(8,128)(2,1)S(1)}, u32[]{:S(2)}, u32[]{:S(2)}) async-start(bf16[64,32,128]{2,1,0:T(8,128)(2,1)} %bitcast.47), calls=%async_computation | async-start | bytes 1048576 | tf_op jit(solution)/shard_map/all_to_all | solution.py:375
  79.5 19.5 %copy-start = (bf16[1,80,128,128]{3,2,1,0:T(8,128)(2,1)S(1)}, bf16[1,80,128,128]{3,2,1,0:T(8,128)(2,1)}, u32[]{:S(2)}) copy-start(bf16[1,80,128,128]{3,2,1,0:T(8,128)(2,1)} %param.5) | copy-start | bytes 7864324
  93.2 17.1 %all-to-all-start.1 = ((bf16[64,32,128]{2,1,0:T(8,128)(2,1)}), bf16[64,32,128]{2,1,0:T(8,128)(2,1)S(1)}, u32[]{:S(2)}, u32[]{:S(2)}) async-start(bf16[64,32,128]{2,1,0:T(8,128)(2,1)} %broadcast_in_dim.14), calls=%async_computation.1 | async-start | bytes 1048576 | tf_op jit(solution)/shard_map/all_to_all | solution.py:377
  97.9 1.5 %copy-start.2 = (bf16[45,64,256]{2,1,0:T(8,128)(2,1)S(1)}, bf16[45,64,256]{2,1,0:T(8,128)(2,1)}, u32[]{:S(2)}) copy-start(bf16[45,64,256]{2,1,0:T(8,128)(2,1)} %get-tuple-element.11.mid_pairs) | copy-start | bytes 4423684
  99.4 1.7 %copy-start.1 = (bf16[1,80,128,128]{3,2,1,0:T(8,128)(2,1)S(1)}, bf16[1,80,128,128]{3,2,1,0:T(8,128)(2,1)}, u32[]{:S(2)}) copy-start(bf16[1,80,128,128]{3,2,1,0:T(8,128)(2,1)} %param.9) | copy-start | bytes 7864324
  101.2 1.4 %copy-start.3 = (bf16[45,64,256]{2,1,0:T(8,128)(2,1)S(1)}, bf16[45,64,256]{2,1,0:T(8,128)(2,1)}, u32[]{:S(2)}) copy-start(bf16[45,64,256]{2,1,0:T(8,128)(2,1)} %get-tuple-element.12.grad_pairs) | copy-start | bytes 4423684

commit v3 on v2

v3 whole, which is shorter than its diff:
```python
import functools
import math

import jax
import jax.numpy as jnp
from jax import lax
from jax.experimental import pallas as pl
from jax.experimental.pallas import tpu as pltpu
from jax.sharding import PartitionSpec as P

BF16 = jnp.bfloat16
F32 = jnp.float32
C = 128
FIELD_LOW, FIELD_HIGH = 5, 6
COT_LOW, COT_HIGH = 3, 4
ROWS = 5
PAIRS = 4
CHUNKS = 4
EDGE = 16
TAPS = 32


def dot(left, right):
    return jnp.dot(left, right, preferred_element_type=F32)


def flat(value):
    return value.reshape(-1, value.shape[-1])


def split_row(stage, row, dest, block, place, west, *easts):
    wide = row.shape[0]
    stage[24 - west.shape[0] : 24, :] = west.astype(F32)
    stage[24 : 24 + wide, :] = row.astype(F32)
    at = 24 + wide
    for east in easts:
        stage[at : at + east.shape[0], :] = east.astype(F32)
        at += east.shape[0]
    own = wide // 2 + 8
    for tap in range(3):
        upper = stage[pl.ds(23 + tap, own, stride=2), :]
        lower = stage[pl.ds(7 + tap, 8, stride=2), :]
        dest[block, place, :, tap * C : (tap + 1) * C] = jnp.concatenate(
            [upper, lower], axis=0
        ).astype(BF16)


def joined(refs, count, first, offsets):
    return jnp.concatenate(
        [flat(refs[pl.ds(first + block, count), place]) for block, place in offsets], axis=1
    )


def grads_kernel(
    half_rows,
    half_cols,
    bands,
    scale,
    fields_hbm,
    cot_hbm,
    low_hbm,
    high_hbm,
    west_hbm,
    east_hbm,
    west_ends_hbm,
    east_ends_hbm,
    weights_hbm,
    own_out,
    other_out,
    mid_out,
    grad_out,
    fields,
    cot,
    low,
    high,
    west,
    east,
    west_ends,
    east_ends,
    weights,
    p_down,
    p_mid,
    p_up_t,
    p_mid_t,
    mid_pairs,
    grad_pairs,
    field_taps,
    cot_taps,
    down_taps,
    pre_taps,
    stage,
    line,
    acc,
    edge_sems,
    own_sems,
    weight_sem,
    out_sems,
):
    lat, part = lax.axis_index("lat"), lax.axis_index("dp")
    slots = half_cols + EDGE
    wide = half_cols + 8
    rows = 2 * half_rows
    chunk = rows // CHUNKS

    edge_copies = [
        pltpu.make_async_copy(source, dest, edge_sems.at[k])
        for k, (source, dest) in enumerate(
            [
                (low_hbm, low),
                (high_hbm, high),
                (west_hbm, west),
                (east_hbm, east),
                (west_ends_hbm, west_ends),
                (east_ends_hbm, east_ends),
            ]
        )
    ]
    own_copies = [
        pltpu.make_async_copy(
            source.at[pl.ds(n * chunk, chunk)], dest.at[pl.ds(n * chunk, chunk)], own_sems.at[k, n]
        )
        for n in range(CHUNKS)
        for k, (source, dest) in enumerate([(fields_hbm, fields), (cot_hbm, cot)])
    ]
    weight_copy = pltpu.make_async_copy(weights_hbm, weights, weight_sem)
    for copy in edge_copies + own_copies + [weight_copy]:
        copy.start()
    acc[...] = jnp.zeros_like(acc)
    for packed in (p_down, p_mid, p_up_t, p_mid_t):
        packed[...] = jnp.zeros_like(packed)
    for copy in edge_copies:
        copy.wait()

    def end_rows(rows_in, at, count, dest, p):
        for k in range(count):
            end = at + k if rows_in is low else low.shape[0] + at + k
            split_row(
                stage.at[k % 4],
                rows_in[at + k],
                dest,
                (p + k) // 4,
                (p + k) % 4,
                west_ends[end],
                east_ends[end],
            )

    end_rows(low, 0, FIELD_LOW, field_taps, 0)
    end_rows(low, FIELD_LOW, COT_LOW, cot_taps, 0)
    end_rows(high, 0, FIELD_HIGH, field_taps, FIELD_LOW + rows)
    end_rows(high, FIELD_HIGH, COT_HIGH, cot_taps, COT_LOW + rows)

    def own_rows(t, carry):
        for k in range(4):
            q, p = 4 * t + k, FIELD_LOW + k
            split_row(stage.at[k], fields[q], field_taps, t + p // 4, p % 4, west[q], east[q])
        for k in range(4):
            q, p = 4 * t + k, COT_LOW + k
            split_row(
                stage.at[k],
                cot[q],
                cot_taps,
                t + p // 4,
                p % 4,
                west[q, :COT_LOW],
                east[q, FIELD_HIGH:],
                east[rows + t, 2 * k : 2 * k + 2],
            )
        return carry

    for n in range(CHUNKS):
        own_copies[2 * n].wait()
        own_copies[2 * n + 1].wait()
        lax.fori_loop(n * chunk // 4, (n + 1) * chunk // 4, own_rows, 0)

    weight_copy.wait()
    for kind, packed, apart, swapped, turned in (
        (0, p_down, 2, False, False),
        (1, p_mid, 1, False, False),
        (2, p_up_t, 2, True, False),
        (1, p_mid_t, 1, True, True),
    ):
        for tap in range(9):
            held = (8 - tap if turned else tap) * C
            block = weights[kind, held : held + C, :]
            block = block.T if swapped else block
            for odd in range(2):
                at = (odd * apart * 3 + tap) * C
                packed[at : at + C, odd * C : (odd + 1) * C] = block

    def on_grid(value, first):
        at = lat * half_rows + first + 2 * lax.broadcasted_iota(jnp.int32, value.shape, 0)
        return jnp.where((at >= 0) & (at < bands * half_rows), value, 0.0)

    def lay(value):
        count = value.shape[0]
        line[:count, 8:16, :] = value[:, wide:]
        line[:count, 16 : 16 + wide, :] = value[:, :wide]

    def shifted(count, shift):
        upper = line[:count, 16 + shift : 16 + shift + wide, :]
        lower = line[:count, 8 + shift : 16 + shift, :]
        return jnp.concatenate([upper, lower], axis=1).astype(BF16)

    def keep_three(dest, at, odd, count, value):
        lay(value)
        for shift in range(3):
            dest[pl.ds(at, count), odd, :, shift * C : (shift + 1) * C] = shifted(count, shift - 1)

    def keep_two(dest, at, odd, count, value):
        lay(value)
        for shift in range(2):
            dest[pl.ds(at, count), odd, :, shift * C : (shift + 1) * C] = line[
                :count, 16 + shift : 16 + shift + half_cols, :
            ].astype(BF16)

    def both_rows(value, count):
        return [value[:, odd * C : (odd + 1) * C].reshape(count, slots, C) for odd in range(2)]

    near = [(q // 2, q % 2) for q in range(4)]
    fine = [(q // 4, q % 4) for q in range(5)]

    def over_pairs(total, work):
        lax.fori_loop(0, total // PAIRS, lambda t, carry: (work(PAIRS * t, PAIRS), carry)[1], 0)
        if total % PAIRS:
            work(total // PAIRS * PAIRS, total % PAIRS)

    def down_strip(m, count):
        values = both_rows(dot(joined(field_taps, count, m, fine), p_down[...]), count)
        for odd, value in enumerate(values):
            keep_three(down_taps, m, odd, count, on_grid(value, 2 * m + odd - 2))

    def pre_strip(m, count):
        pres = both_rows(dot(joined(down_taps, count, m, near), p_mid[...]), count)
        grads = both_rows(dot(joined(cot_taps, count, m, fine), p_up_t[...]), count)
        for odd in range(2):
            pre, grad, first = pres[odd], grads[odd], 2 * m + odd - 1
            sig = jax.nn.sigmoid(pre)
            keep_two(mid_pairs, m, odd, count, on_grid(pre * sig, first))
            keep_three(
                pre_taps, m, odd, count, on_grid(grad * sig * (1.0 + pre * (1.0 - sig)), first)
            )

    def back_strip(m, count):
        values = both_rows(dot(joined(pre_taps, count, m, near), p_mid_t[...]), count)
        for odd, value in enumerate(values):
            keep_two(grad_pairs, m, odd, count, on_grid(value, 2 * m + odd))

    over_pairs(half_rows // 2 + 3, down_strip)
    over_pairs(half_rows // 2 + 2, pre_strip)
    mid_copy = pltpu.make_async_copy(mid_pairs, mid_out, out_sems.at[0])
    mid_copy.start()
    over_pairs(half_rows // 2 + 1, back_strip)
    grad_copy = pltpu.make_async_copy(grad_pairs, grad_out, out_sems.at[1])
    grad_copy.start()

    here = slice(0, half_cols)

    def outer(kind, left, right):
        left = jnp.concatenate([flat(piece) for piece in left], axis=0)
        right = jnp.concatenate(
            [jnp.concatenate([flat(piece) for piece in pieces], axis=1) for pieces in right], axis=0
        )
        acc[kind] += lax.dot_general(
            left, right, (((0,), (0,)), ((), ())), preferred_element_type=F32
        )

    def outer_strip(t, carry):
        m = PAIRS * t

        def piece(ref, cells, every, row):
            return ref[pl.ds(m + row // every, PAIRS), row % every, here, cells]

        every_lane, middle, first_lane = slice(None), slice(C, 2 * C), slice(0, C)
        outer(
            0,
            [piece(grad_pairs, first_lane, 2, odd) for odd in range(2)],
            [[piece(field_taps, every_lane, 4, 4 + 2 * odd + r) for r in range(3)] for odd in range(2)],
        )
        outer(
            1,
            [piece(down_taps, middle, 2, 2 + odd) for odd in range(2)],
            [[piece(pre_taps, every_lane, 2, odd + r) for r in range(3)] for odd in range(2)],
        )
        outer(
            2,
            [piece(mid_pairs, first_lane, 2, 1 + odd) for odd in range(2)],
            [[piece(cot_taps, every_lane, 4, 2 + 2 * odd + r) for r in range(3)] for odd in range(2)],
        )
        return carry

    lax.fori_loop(0, half_rows // (2 * PAIRS), outer_strip, 0)

    half = C // 2
    for tap in range(9):
        at = slice(tap * C, (tap + 1) * C)
        acc[0, :, at] = acc[0, :, at].T
    mine = pl.ds(pl.multiple_of(part * half, half), half)
    theirs = pl.ds(pl.multiple_of((1 - part) * half, half), half)
    for kind in range(3):
        for tap in range(9):
            held = 8 - tap if kind == 1 else tap
            at = slice(held * C, (held + 1) * C)
            own_out[kind * 9 + tap] = acc[kind, mine, at] * scale
            other_out[kind * 9 + tap] = (acc[kind, theirs, at] * scale).astype(BF16)
    for tap in range(27, TAPS):
        own_out[tap] = jnp.zeros((half, C), F32)
        other_out[tap] = jnp.zeros((half, C), BF16)
    mid_copy.wait()
    grad_copy.wait()


def up_kernel(
    above,
    kind,
    swapped,
    pairs_hbm,
    base_hbm,
    weights_hbm,
    out_hbm,
    pairs,
    base,
    kernel,
    out,
    whole,
    in_sems,
    out_sems,
):
    half_cols = pairs.shape[1]
    fine = 2 * ROWS
    strips = base.shape[0] // fine
    whole_copies = [
        pltpu.make_async_copy(source, dest, in_sems.at[strips + k])
        for k, (source, dest) in enumerate([(weights_hbm.at[kind], kernel), (pairs_hbm, pairs)])
    ]

    def rows(n):
        return pl.ds(n * fine, fine)

    base_copies = [
        pltpu.make_async_copy(base_hbm.at[rows(n)], base.at[rows(n)], in_sems.at[n])
        for n in range(strips)
    ]
    out_copies = [
        pltpu.make_async_copy(out.at[rows(n)], out_hbm.at[rows(n)], out_sems.at[n])
        for n in range(strips)
    ]
    for copy in whole_copies + base_copies:
        copy.start()
    for copy in whole_copies:
        copy.wait()

    def tap(row, col):
        k = 3 * row + col
        block = kernel[k * C : (k + 1) * C, :]
        return block.T if swapped else block

    def lanes(*pieces):
        return jnp.concatenate(pieces, axis=1)

    odd_kernel = jnp.concatenate([lanes(tap(1, 2), tap(2, 2)), lanes(tap(1, 0), tap(2, 0))], axis=0)
    last_kernel = jnp.concatenate([tap(0, 2), tap(0, 0)], axis=0)
    even_kernel = jnp.concatenate(
        [lanes(tap(1, 1), tap(2, 1)), lanes(jnp.zeros((C, C), BF16), tap(0, 1))], axis=0
    )
    for n in range(strips):
        at = ROWS * n + above
        near = flat(pairs[at : at + ROWS])
        far = flat(pairs[at + 1 : at + 1 + ROWS])
        odd = dot(near, odd_kernel)
        last = dot(far, last_kernel)
        even = dot(lanes(near[:, :C], far[:, :C]), even_kernel)
        for k in range(ROWS):
            at_k = slice(k * half_cols, (k + 1) * half_cols)
            whole[2 * k, pl.ds(0, half_cols, stride=2), :] = even[at_k, :C]
            whole[2 * k, pl.ds(1, half_cols, stride=2), :] = odd[at_k, :C]
            whole[2 * k + 1, pl.ds(0, half_cols, stride=2), :] = even[at_k, C:]
            whole[2 * k + 1, pl.ds(1, half_cols, stride=2), :] = odd[at_k, C:] + last[at_k]
        base_copies[n].wait()
        out[rows(n)] = (base[rows(n)].astype(F32) + whole[...]).astype(BF16)
        out_copies[n].start()
    for copy in out_copies:
        copy.wait()


def spread(name, above, kind, swapped, pairs, base, weights):
    rows, cols, _ = base.shape
    strips = rows // (2 * ROWS)
    hbm = pl.BlockSpec(memory_space=pltpu.HBM)
    return pl.pallas_call(
        functools.partial(up_kernel, above, kind, swapped),
        out_shape=jax.ShapeDtypeStruct(base.shape, BF16),
        in_specs=[hbm] * 3,
        out_specs=hbm,
        scratch_shapes=[
            pltpu.VMEM(shape, BF16)
            for shape in (pairs.shape, base.shape, weights.shape[1:], base.shape)
        ]
        + [
            pltpu.VMEM((2 * ROWS, cols, C), F32),
            pltpu.SemaphoreType.DMA((strips + 2,)),
            pltpu.SemaphoreType.DMA((strips,)),
        ],
        compiler_params=pltpu.CompilerParams(vmem_limit_bytes=60 * 2**20),
        cost_estimate=pl.CostEstimate(
            flops=9 * rows * cols * C * C // 2, transcendentals=0, bytes_accessed=7 * 2**20
        ),
        name=name,
    )(pairs, base, weights)


def copied(name, out_shapes, moves, limit, *arrays):
    def kernel(*refs):
        ins, outs, sems = refs[: len(arrays)], refs[len(arrays) : -1], refs[-1]
        copies = [
            pltpu.make_async_copy(ins[i].at[cut], outs[o].at[place], sems.at[k])
            for k, (i, cut, o, place) in enumerate(moves)
        ]
        for copy in copies:
            copy.start()
        for copy in copies:
            copy.wait()

    return pl.pallas_call(
        kernel,
        out_shape=tuple(jax.ShapeDtypeStruct(shape, BF16) for shape in out_shapes),
        in_specs=[pl.BlockSpec(memory_space=pl.ANY)] * len(arrays),
        out_specs=(pl.BlockSpec(memory_space=pltpu.VMEM),) * len(out_shapes),
        scratch_shapes=[pltpu.SemaphoreType.DMA((len(moves),))],
        compiler_params=pltpu.CompilerParams(vmem_limit_bytes=limit * 2**20),
        name=name,
    )(*arrays)


def columns_kernel(fields_hbm, cot_hbm, east, west, ends, spare, sems):
    rows, cols, _ = fields_hbm.shape
    copies = [
        pltpu.make_async_copy(source.at[:, pl.ds(at, 8), :], ends.at[k], sems.at[k])
        for k, (source, at) in enumerate(
            [(fields_hbm, cols - 8), (cot_hbm, cols - 8), (fields_hbm, 0), (cot_hbm, 0)]
        )
    ]
    for copy in copies:
        copy.start()
    for copy in copies:
        copy.wait()
    field, other = ends[0].astype(F32), ends[1].astype(F32)
    east[...] = jnp.concatenate(
        [other[:, 8 - COT_LOW :], field[:, 8 - FIELD_LOW :]], axis=1
    ).astype(BF16)
    field, other = ends[2].astype(F32), ends[3].astype(F32)
    beside = 8 - FIELD_HIGH
    west[:rows] = jnp.concatenate([field[:, :FIELD_HIGH], other[:, :beside]], axis=1).astype(BF16)
    other = other.reshape(rows // 4, 4, 8, C)
    for k in range(4):
        spare[:, 2 * k : 2 * k + 2, :] = other[:, k, beside:COT_HIGH]
    west[rows:] = spare[...].astype(BF16)


def columns(fields, cot):
    rows = fields.shape[0]
    vmem = pl.BlockSpec(memory_space=pltpu.VMEM)
    return pl.pallas_call(
        columns_kernel,
        out_shape=(
            jax.ShapeDtypeStruct((rows, 8, C), BF16),
            jax.ShapeDtypeStruct((rows + rows // 4, 8, C), BF16),
        ),
        in_specs=[pl.BlockSpec(memory_space=pl.ANY)] * 2,
        out_specs=(vmem, vmem),
        scratch_shapes=[
            pltpu.VMEM((4, rows, 8, C), BF16),
            pltpu.VMEM((rows // 4, 8, C), F32),
            pltpu.SemaphoreType.DMA((4,)),
        ],
        compiler_params=pltpu.CompilerParams(vmem_limit_bytes=60 * 2**20),
        name="columns",
    )(fields, cot)


def halos(fields, cot, weights):
    lat = lax.axis_size("lat")
    lon = lax.axis_size("lon")
    rows, cols, _ = fields.shape
    lows, highs = FIELD_LOW + COT_LOW, FIELD_HIGH + COT_HIGH
    every = slice(None)

    def row(start, count):
        return (pl.ds(start, count), every, every)

    first, last = (every, pl.ds(0, 8), every), (every, pl.ds(cols - 8, 8), every)
    up, down = copied(
        "edges",
        [(lows, cols, C), (highs, cols, C)],
        [
            (0, row(rows - FIELD_LOW, FIELD_LOW), 0, row(0, FIELD_LOW)),
            (1, row(rows - COT_LOW, COT_LOW), 0, row(FIELD_LOW, COT_LOW)),
            (0, row(0, FIELD_HIGH), 1, row(0, FIELD_HIGH)),
            (1, row(0, COT_HIGH), 1, row(FIELD_HIGH, COT_HIGH)),
        ],
        60,
        fields,
        cot,
    )
    up, down, fields, cot = lax.optimization_barrier((up, down, fields, cot))
    east, west = columns(fields, cot)
    north = [(i, i + 1) for i in range(lat - 1)]
    south = [(j, i) for i, j in north]
    eastward = [(i, (i + 1) % lon) for i in range(lon)]
    westward = [(j, i) for i, j in eastward]
    low = lax.ppermute(up, "lat", north)
    high = lax.ppermute(down, "lat", south)
    from_west = lax.ppermute(east, "lon", eastward)
    from_east = lax.ppermute(west, "lon", westward)
    low, high, weights = lax.optimization_barrier((low, high, weights))
    east, west = copied(
        "ends",
        [(lows + highs, 8, C)] * 2,
        [
            (0, last, 0, row(0, lows)),
            (1, last, 0, row(lows, highs)),
            (0, first, 1, row(0, lows)),
            (1, first, 1, row(lows, highs)),
        ],
        2,
        low,
        high,
    )
    west_ends = lax.ppermute(east, "lon", eastward)
    east_ends = lax.ppermute(west, "lon", westward)
    return (low, high, from_west, from_east, west_ends, east_ends), weights


def body(fields, down_weight, mid_weight, up_weight, cotangent):
    lats, lons, parts = (lax.axis_size(axis) for axis in ("lat", "lon", "dp"))
    _, rows, cols, _ = fields.shape
    half_rows, half_cols = rows // 2, cols // 2
    scale = 1.0 / math.sqrt(parts * rows * lats * cols * lons)
    fields, cotangent = fields[0], cotangent[0]
    weights = lax.all_gather(
        jnp.stack([down_weight, mid_weight, up_weight]), "dp", axis=3, tiled=True
    )
    edges, weights = halos(fields, cotangent, weights)
    weights = weights.reshape(3, 9 * C, C)

    slots = half_cols + EDGE
    quads = half_rows // 2 + 5
    pairs = half_rows // 2 + 3
    hbm = pl.BlockSpec(memory_space=pl.ANY)
    inputs = (fields, cotangent, *edges, weights)
    own, other, mid_pairs, grad_pairs = pl.pallas_call(
        functools.partial(grads_kernel, half_rows, half_cols, lats, scale),
        out_shape=(
            jax.ShapeDtypeStruct((TAPS, C // 2, C), F32),
            jax.ShapeDtypeStruct((TAPS, C // 2, C), BF16),
            jax.ShapeDtypeStruct((pairs, 2, half_cols, 2 * C), BF16),
            jax.ShapeDtypeStruct((pairs, 2, half_cols, 2 * C), BF16),
        ),
        in_specs=[hbm] * len(inputs),
        out_specs=(pl.BlockSpec(memory_space=pltpu.VMEM),) * 2
        + (pl.BlockSpec(memory_space=pltpu.HBM),) * 2,
        scratch_shapes=[pltpu.VMEM(array.shape, BF16) for array in inputs]
        + [
            pltpu.VMEM((15 * C, 2 * C), BF16),
            pltpu.VMEM((12 * C, 2 * C), BF16),
            pltpu.VMEM((15 * C, 2 * C), BF16),
            pltpu.VMEM((12 * C, 2 * C), BF16),
            pltpu.VMEM((pairs, 2, half_cols, 2 * C), BF16),
            pltpu.VMEM((pairs, 2, half_cols, 2 * C), BF16),
            pltpu.VMEM((quads, 4, slots, 3 * C), BF16),
            pltpu.VMEM((quads, 4, slots, 3 * C), BF16),
            pltpu.VMEM((pairs + 1, 2, slots, 3 * C), BF16),
            pltpu.VMEM((pairs + 1, 2, slots, 3 * C), BF16),
            pltpu.VMEM((4, cols + 48, C), F32),
            pltpu.VMEM((PAIRS, slots + 16, C), F32),
            pltpu.VMEM((3, C, 9 * C), F32),
            pltpu.SemaphoreType.DMA((6,)),
            pltpu.SemaphoreType.DMA((2, CHUNKS)),
            pltpu.SemaphoreType.DMA,
            pltpu.SemaphoreType.DMA((2,)),
        ],
        compiler_params=pltpu.CompilerParams(vmem_limit_bytes=50 * 2**20),
        cost_estimate=pl.CostEstimate(
            flops=70 * 2 * half_rows * half_cols * C * C,
            transcendentals=half_rows * half_cols * C,
            bytes_accessed=8 * 2**20,
        ),
        name="grads",
    )(*inputs)
    mid_pairs = mid_pairs.reshape(2 * pairs, half_cols, 2 * C)
    grad_pairs = grad_pairs.reshape(2 * pairs, half_cols, 2 * C)

    came = lax.ppermute(other, "dp", [(0, 1), (1, 0)])
    both = (own + came.astype(F32)).astype(BF16)
    pieces = both.reshape(lats * lons, -1, C)
    pieces = lax.all_to_all(pieces, ("lat", "lon"), 0, 0, tiled=True)
    level_out = spread("level", 1, 2, False, mid_pairs, fields, weights)
    piece = jnp.sum(pieces.astype(F32), axis=0, keepdims=True).astype(BF16)
    piece, level_out = lax.optimization_barrier((piece, level_out))
    totals = lax.all_to_all(
        jnp.broadcast_to(piece, pieces.shape), ("lat", "lon"), 0, 0, tiled=True
    )
    _, grad_pairs = lax.optimization_barrier((piece, grad_pairs))
    grad_fields = spread("gradient", 0, 0, True, grad_pairs, cotangent, weights)
    totals = totals.reshape(TAPS, C // 2, C).astype(F32)
    grad_down, grad_mid, grad_up = (
        totals[9 * k : 9 * k + 9].reshape(3, 3, C // 2, C) for k in range(3)
    )
    return (level_out[None], grad_fields[None], grad_down, grad_mid, grad_up)


def solution(mesh):
    field = P("dp", "lat", "lon", None)
    weight = P(None, None, "dp", None)
    return jax.shard_map(
        body,
        mesh=mesh,
        in_specs=(field, weight, weight, weight, field),
        out_specs=(field, field, weight, weight, weight),
        check_vma=False,
    )
```

time: 112 us -> 100 us (0.89)
  local copies, waits for them, and re-layouts: 18.4 us -> 1.85 us
  other arithmetic: 7.36 us -> 1.12 us
  waiting for transfers between devices: 21.6 us -> 27.7 us
  starting transfers between devices: 27.5 us -> 31.8 us
  Pallas kernels: 33 us -> 34.2 us
    pallas_call x1 -> x5, Pallas kernels: 5.41 us -> 14.5 us  [the longest x2 10.4 us: spread(): pl.pallas_call(functools.partial(up_kernel, above, kind, swapped), out_sh...]
    pallas_call x1, Pallas kernels: 27.6 us -> 19.7 us  [body(): pl.pallas_call(functools.partial(grads_kernel, half_rows, half_cols, lats...]
    slice x16 -> x0, local copies, waits for them, and re-layouts: 7.54 us -> none  [the longest x2 1.91 us: columns(): cot[:, at_cot]]
    ppermute x4 -> x6, starting transfers between devices: 10.8 us -> 15.6 us  [the longest x1 5.33 us: halos(): low = lax.ppermute(up, 'lat', north)]
    all_to_all x1, waiting for transfers between devices: 2.3 us -> 7.09 us  [body(): lax.all_to_all(jnp.broadcast_to(piece, pieces.shape), ('lat', 'lon'), 0,...]
    unnamed x16 -> x8, local copies, waits for them, and re-layouts: 4.26 us -> 0.02 us
    another operation x7 -> x0, other arithmetic: 3.59 us -> none  [the longest x6 2.93 us: body(): jnp.stack(pair)]
    ppermute x4 -> x6, waiting for transfers between devices: 7.07 us -> 10.2 us  [the longest x1 8.34 us: halos(): high = lax.ppermute(down, 'lat', south)]
  transfers between devices with their start and end apart: 7 -> 9, of which waited for: 5 -> 5; matrix products, arithmetic and copies ran while one was open for 14% -> 0% of each run, Pallas kernels for 5% -> 13%
where the time goes in v3:
time: 100 us; the launch traced here: 99.8 us
  Pallas kernels  34.2 us (34%)
  starting transfers between devices  31.8 us (32%)
  waiting for transfers between devices  27.7 us (28%)
  blocking collectives  2.44 us (2%)
  local copies, waits for them, and re-layouts  1.85 us (2%)
  other arithmetic  1.12 us (1%)
    pallas_call x1, Pallas kernels, body(): pl.pallas_call(functools.partial(grads_kernel, half_rows, half_cols, lats...  19.7 us
    all_to_all x1, starting transfers between devices, body(): pieces = lax.all_to_all(pieces, ('lat', 'lon'), 0, 0, tiled=True)  11.4 us
    pallas_call x2, Pallas kernels, spread(): pl.pallas_call(functools.partial(up_kernel, above, kind, swapped), out_sh...  10.4 us
    all_to_all x1, waiting for transfers between devices, body(): pieces = lax.all_to_all(pieces, ('lat', 'lon'), 0, 0, tiled=True)  8.47 us
    ppermute x1, waiting for transfers between devices, halos(): high = lax.ppermute(down, 'lat', south)  8.34 us
    all_to_all x1, waiting for transfers between devices, body(): lax.all_to_all(jnp.broadcast_to(piece, pieces.shape), ('lat', 'lon'), 0,...  7.09 us
    ppermute x1, starting transfers between devices, halos(): low = lax.ppermute(up, 'lat', north)  5.33 us
    all_to_all x1, starting transfers between devices, body(): lax.all_to_all(jnp.broadcast_to(piece, pieces.shape), ('lat', 'lon'), 0,...  4.73 us
  transfers between devices with their start and end apart: 9, of which 5 were waited for; matrix products, arithmetic and copies ran while one was open for 0% of the time, Pallas kernels for 13%

profile of v3, /device:TPU:0, one launch (start us, length us, event | category | flops | bytes accessed | tf_op | source)
XLA Modules:
  0.0 99.8 jit_solution(8359992592411837398)
XLA Ops:
  0.6 2.0 %edges.1 = (bf16[8,128,128]{2,1,0:T(8,128)(2,1)}, bf16[10,128,128]{2,1,0:T(8,128)(2,1)}) custom-call(bf16[80,128,128]{2,1,0:T(8,128)(2,1)} %bitcast.19, bf16[80,128,128]{2,1,0:T(8,128)(2,1)} %bitcast.23), custom_call_target="tpu_custom_call" | custom-call | tf_op jit(solution)/shard_map/edges/pallas_call | solution.py:423
  2.6 0.0 copy-start.1
  2.6 0.0 copy-start.2
  2.6 0.0 copy-start.3
  2.6 5.3 %collective-permute-start = (bf16[8,128,128]{2,1,0:T(8,128)(2,1)}, bf16[8,128,128]{2,1,0:T(8,128)(2,1)S(1)}, u32[]{:S(2)}, u32[]{:S(2)}) collective-permute-start(bf16[8,128,128]{2,1,0:T(8,128)(2,1)} %get-tuple-element.27), channel_id=1, source_target_pairs={{0,8},{8,16},{16,24},{24,32},{32,40},{40,48},{48,56},{1,9},{9,17},... | collective-permute-start | bytes 786440 | tf_op jit(solution)/shard_map/ppermute | solution.py:510
  8.0 1.3 %collective-permute-start.1 = (bf16[10,128,128]{2,1,0:T(8,128)(2,1)}, bf16[10,128,128]{2,1,0:T(8,128)(2,1)S(1)}, u32[]{:S(2)}, u32[]{:S(2)}) collective-permute-start(bf16[10,128,128]{2,1,0:T(8,128)(2,1)} %get-tuple-element.28), channel_id=1, source_target_pairs={{8,0},{16,8},{24,16},{32,24},{40,32},{48,40},{56,48},{9,1},{17,9},... | collective-permute-start | bytes 983048 | tf_op jit(solution)/shard_map/ppermute | solution.py:511
  9.3 2.1 %columns.1 = (bf16[80,8,128]{2,1,0:T(8,128)(2,1)}, bf16[100,8,128]{2,1,0:T(8,128)(2,1)}) custom-call(bf16[80,128,128]{2,1,0:T(8,128)(2,1)} %bitcast.20, bf16[80,128,128]{2,1,0:T(8,128)(2,1)} %bitcast.24), custom_call_target="tpu_custom_call" | custom-call | tf_op jit(solution)/shard_map/columns/pallas_call | solution.py:462
  11.3 1.6 %collective-permute-start.2 = (bf16[80,8,128]{2,1,0:T(8,128)(2,1)}, bf16[80,8,128]{2,1,0:T(8,128)(2,1)S(1)}, u32[]{:S(2)}, u32[]{:S(2)}) collective-permute-start(bf16[80,8,128]{2,1,0:T(8,128)(2,1)} %get-tuple-element.33), channel_id=1, source_target_pairs={{0,1},{1,2},{2,3},{3,4},{4,5},{5,6},{6,7},{7,0},{8,9},{9,10},{10,1... | collective-permute-start | bytes 491528 | tf_op jit(solution)/shard_map/ppermute | solution.py:512
  12.9 2.6 %collective-permute-start.3 = (bf16[100,8,128]{2,1,0:T(8,128)(2,1)}, bf16[100,8,128]{2,1,0:T(8,128)(2,1)S(1)}, u32[]{:S(2)}, u32[]{:S(2)}) collective-permute-start(bf16[100,8,128]{2,1,0:T(8,128)(2,1)} %get-tuple-element.34), channel_id=1, source_target_pairs={{1,0},{2,1},{3,2},{4,3},{5,4},{6,5},{7,6},{0,7},{9,8},{10,9},{11,1... | collective-permute-start | bytes 614408 | tf_op jit(solution)/shard_map/ppermute | solution.py:513
  15.6 0.0 copy-done.1
  15.6 0.0 copy-done.2
  15.6 0.0 copy-done.3
  15.6 0.1 pad_maximum_fusion
  15.6 2.4 %all_gather.3 = bf16[3,3,3,128,128]{4,3,2,1,0:T(8,128)(2,1)S(1)} all-gather(bf16[3,3,3,64,128]{4,3,2,1,0:T(8,128)(2,1)S(1)} %pad_maximum_fusion), channel_id=1, replica_groups=mesh['dp'=2,'lat'=8,'lon'=8] {'dp'}, dimensions={3}, use_global_device_ids=true | all-gather | bytes 1327104 | tf_op jit(solution)/shard_map/all_gather | solution.py:539
  18.1 0.0 copy-start
  18.1 0.0 collective-permute-done.refs_0_.low_hbm
  18.1 8.3 %collective-permute-done.1.refs_1_.high_hbm = bf16[10,128,128]{2,1,0:T(8,128)(2,1)S(1)} collective-permute-done((bf16[10,128,128]{2,1,0:T(8,128)(2,1)}, bf16[10,128,128]{2,1,0:T(8,128)(2,1)S(1)}, u32[]{:S(2)}, u32[]{:S(2)}) %collective-permute-start.1) | collective-permute-done | bytes 327712 | tf_op jit(solution)/shard_map/ppermute | solution.py:511
  26.4 0.1 ends.1
  26.5 0.1 collective-permute-start.4
  26.6 4.7 %collective-permute-start.5 = (bf16[18,8,128]{2,1,0:T(8,128)(2,1)S(1)}, bf16[18,8,128]{2,1,0:T(8,128)(2,1)S(1)}, u32[]{:S(2)}, u32[]{:S(2)}) collective-permute-start(bf16[18,8,128]{2,1,0:T(8,128)(2,1)S(1)} %get-tuple-element.36), channel_id=1, source_target_pairs={{1,0},{2,1},{3,2},{4,3},{5,4},{6,5},{7,6},{0,7},{9,8},{10,9},{11,1... | collective-permute-start | bytes 110600 | tf_op jit(solution)/shard_map/ppermute | solution.py:529
  31.3 0.0 collective-permute-done.2.west_hbm
  31.3 0.0 collective-permute-done.3.east_hbm
  31.3 1.8 %collective-permute-done.4.west_ends_hbm = bf16[18,8,128]{2,1,0:T(8,128)(2,1)S(1)} collective-permute-done((bf16[18,8,128]{2,1,0:T(8,128)(2,1)S(1)}, bf16[18,8,128]{2,1,0:T(8,128)(2,1)S(1)}, u32[]{:S(2)}, u32[]{:S(2)}) %collective-permute-start.4) | collective-permute-done | bytes 36896 | tf_op jit(solution)/shard_map/ppermute | solution.py:528
  33.1 0.0 collective-permute-done.5.east_ends_hbm
  33.1 19.7 %grads.1 = (f32[32,64,128]{2,1,0:T(8,128)S(1)}, bf16[32,64,128]{2,1,0:T(8,128)(2,1)S(1)}, bf16[23,2,64,256]{3,2,1,0:T(8,128)(2,1)}, bf16[23,2,64,256]{3,2,1,0:T(8,128)(2,1)}) custom-call(bf16[80,128,128]{2,1,0:T(8,128)(2,1)} %bitcast.21, bf16[80,128,128]{2,1,0:T(8,128)(2,1)} %bitcast.25, bf16[8,128,128]{2,1,0:T(8,128)(2,1)S(1)} %collective-permute-done.refs_0_.low_hbm, ...), custom_call_target="tpu_custom_call" | custom-call | flops 5872025600 | bytes 8388608 | tf_op jit(solution)/shard_map/grads/pallas_call | solution.py:550
  52.9 0.0 copy-done
  52.9 0.1 collective-permute-start.6
  53.0 1.9 %collective-permute-done.6 = bf16[32,64,128]{2,1,0:T(8,128)(2,1)S(1)} collective-permute-done((bf16[32,64,128]{2,1,0:T(8,128)(2,1)S(1)}, bf16[32,64,128]{2,1,0:T(8,128)(2,1)S(1)}, u32[]{:S(2)}, u32[]{:S(2)}) %collective-permute-start.6) | collective-permute-done | bytes 524320 | tf_op jit(solution)/shard_map/ppermute | solution.py:592
  54.9 1.0 add_convert_fusion
  55.8 11.4 %all-to-all-start = ((bf16[64,32,128]{2,1,0:T(8,128)(2,1)}), bf16[64,32,128]{2,1,0:T(8,128)(2,1)S(1)}, u32[]{:S(2)}, u32[]{:S(2)}) async-start(bf16[64,32,128]{2,1,0:T(8,128)(2,1)} %bitcast.6), calls=%async_computation | async-start | bytes 1048576 | tf_op jit(solution)/shard_map/all_to_all | solution.py:595
  67.2 5.2 %level.1 = bf16[80,128,128]{2,1,0:T(8,128)(2,1)} custom-call(bf16[46,64,256]{2,1,0:T(8,128)(2,1)} %bitcast.30, bf16[80,128,128]{2,1,0:T(8,128)(2,1)} %bitcast.22, bf16[3,1152,128]{2,1,0:T(8,128)(2,1)} %bitcast.17), custom_call_target="tpu_custom_call" | custom-call | flops 754974720 | bytes 7340032 | tf_op jit(solution)/shard_map/level/pallas_call | solution.py:389
  72.4 8.5 %all-to-all-done = bf16[64,32,128]{2,1,0:T(8,128)(2,1)S(1)} async-done(((bf16[64,32,128]{2,1,0:T(8,128)(2,1)}), bf16[64,32,128]{2,1,0:T(8,128)(2,1)S(1)}, u32[]{:S(2)}, u32[]{:S(2)}) %all-to-all-start) | async-done | bytes 524320 | tf_op jit(solution)/shard_map/all_to_all | solution.py:595
  80.9 0.1 reduce_sum.12
  81.0 0.9 broadcast_in_dim.17
  81.8 4.7 %all-to-all-start.1 = ((bf16[64,32,128]{2,1,0:T(8,128)(2,1)}), bf16[64,32,128]{2,1,0:T(8,128)(2,1)S(1)}, u32[]{:S(2)}, u32[]{:S(2)}) async-start(bf16[64,32,128]{2,1,0:T(8,128)(2,1)} %broadcast_in_dim.17), calls=%async_computation.1 | async-start | bytes 1048576 | tf_op jit(solution)/shard_map/all_to_all | solution.py:599
  86.6 5.2 %gradient.1 = bf16[80,128,128]{2,1,0:T(8,128)(2,1)} custom-call(bf16[46,64,256]{2,1,0:T(8,128)(2,1)} %bitcast.29, bf16[80,128,128]{2,1,0:T(8,128)(2,1)} %bitcast.26, bf16[3,1152,128]{2,1,0:T(8,128)(2,1)} %bitcast.18), custom_call_target="tpu_custom_call" | custom-call | flops 754974720 | bytes 7340032 | tf_op jit(solution)/shard_map/gradient/pallas_call | solution.py:389
  91.8 7.1 %all-to-all-done.1 = bf16[64,32,128]{2,1,0:T(8,128)(2,1)S(1)} async-done(((bf16[64,32,128]{2,1,0:T(8,128)(2,1)}), bf16[64,32,128]{2,1,0:T(8,128)(2,1)S(1)}, u32[]{:S(2)}, u32[]{:S(2)}) %all-to-all-start.1) | async-done | bytes 524320 | tf_op jit(solution)/shard_map/all_to_all | solution.py:599
  98.9 0.9 fusion
Async XLA Ops:
  2.6 12.9 %copy-start.1 = (bf16[3,3,64,128]{3,2,1,0:T(8,128)(2,1)S(1)}, bf16[3,3,64,128]{3,2,1,0:T(8,128)(2,1)}, u32[]{:S(2)}) copy-start(bf16[3,3,64,128]{3,2,1,0:T(8,128)(2,1)} %param.8) | copy-start | bytes 442372
  2.6 12.9 %copy-start.2 = (bf16[3,3,64,128]{3,2,1,0:T(8,128)(2,1)S(1)}, bf16[3,3,64,128]{3,2,1,0:T(8,128)(2,1)}, u32[]{:S(2)}) copy-start(bf16[3,3,64,128]{3,2,1,0:T(8,128)(2,1)} %param.7) | copy-start | bytes 442372
  2.6 12.9 %copy-start.3 = (bf16[3,3,64,128]{3,2,1,0:T(8,128)(2,1)S(1)}, bf16[3,3,64,128]{3,2,1,0:T(8,128)(2,1)}, u32[]{:S(2)}) copy-start(bf16[3,3,64,128]{3,2,1,0:T(8,128)(2,1)} %param.6) | copy-start | bytes 442372
  2.6 15.4 %collective-permute-start = (bf16[8,128,128]{2,1,0:T(8,128)(2,1)}, bf16[8,128,128]{2,1,0:T(8,128)(2,1)S(1)}, u32[]{:S(2)}, u32[]{:S(2)}) collective-permute-start(bf16[8,128,128]{2,1,0:T(8,128)(2,1)} %get-tuple-element.27), channel_id=1, source_target_pairs={{0,8},{8,16},{16,24},{24,32},{32,40},{40,48},{48,56},{1,9},{9,17},... | collective-permute-start | bytes 786440 | tf_op jit(solution)/shard_map/ppermute | solution.py:510
  8.0 18.4 %collective-permute-start.1 = (bf16[10,128,128]{2,1,0:T(8,128)(2,1)}, bf16[10,128,128]{2,1,0:T(8,128)(2,1)S(1)}, u32[]{:S(2)}, u32[]{:S(2)}) collective-permute-start(bf16[10,128,128]{2,1,0:T(8,128)(2,1)} %get-tuple-element.28), channel_id=1, source_target_pairs={{8,0},{16,8},{24,16},{32,24},{40,32},{48,40},{56,48},{9,1},{17,9},... | collective-permute-start | bytes 983048 | tf_op jit(solution)/shard_map/ppermute | solution.py:511
  11.3 19.9 %collective-permute-start.2 = (bf16[80,8,128]{2,1,0:T(8,128)(2,1)}, bf16[80,8,128]{2,1,0:T(8,128)(2,1)S(1)}, u32[]{:S(2)}, u32[]{:S(2)}) collective-permute-start(bf16[80,8,128]{2,1,0:T(8,128)(2,1)} %get-tuple-element.33), channel_id=1, source_target_pairs={{0,1},{1,2},{2,3},{3,4},{4,5},{5,6},{6,7},{7,0},{8,9},{9,10},{10,1... | collective-permute-start | bytes 491528 | tf_op jit(solution)/shard_map/ppermute | solution.py:512
  12.9 18.4 %collective-permute-start.3 = (bf16[100,8,128]{2,1,0:T(8,128)(2,1)}, bf16[100,8,128]{2,1,0:T(8,128)(2,1)S(1)}, u32[]{:S(2)}, u32[]{:S(2)}) collective-permute-start(bf16[100,8,128]{2,1,0:T(8,128)(2,1)} %get-tuple-element.34), channel_id=1, source_target_pairs={{1,0},{2,1},{3,2},{4,3},{5,4},{6,5},{7,6},{0,7},{9,8},{10,9},{11,1... | collective-permute-start | bytes 614408 | tf_op jit(solution)/shard_map/ppermute | solution.py:513
  18.1 34.8 %copy-start = (bf16[3,3,3,128,128]{4,3,2,1,0:T(8,128)(2,1)}, bf16[3,3,3,128,128]{4,3,2,1,0:T(8,128)(2,1)S(1)}, u32[]{:S(2)}) copy-start(bf16[3,3,3,128,128]{4,3,2,1,0:T(8,128)(2,1)S(1)} %all_gather.3) | copy-start | bytes 2654212
  26.5 6.7 %collective-permute-start.4 = (bf16[18,8,128]{2,1,0:T(8,128)(2,1)S(1)}, bf16[18,8,128]{2,1,0:T(8,128)(2,1)S(1)}, u32[]{:S(2)}, u32[]{:S(2)}) collective-permute-start(bf16[18,8,128]{2,1,0:T(8,128)(2,1)S(1)} %get-tuple-element.35), channel_id=1, source_target_pairs={{0,1},{1,2},{2,3},{3,4},{4,5},{5,6},{6,7},{7,0},{8,9},{9,10},{10,1... | collective-permute-start | bytes 110600 | tf_op jit(solution)/shard_map/ppermute | solution.py:528
  26.6 6.6 %collective-permute-start.5 = (bf16[18,8,128]{2,1,0:T(8,128)(2,1)S(1)}, bf16[18,8,128]{2,1,0:T(8,128)(2,1)S(1)}, u32[]{:S(2)}, u32[]{:S(2)}) collective-permute-start(bf16[18,8,128]{2,1,0:T(8,128)(2,1)S(1)} %get-tuple-element.36), channel_id=1, source_target_pairs={{1,0},{2,1},{3,2},{4,3},{5,4},{6,5},{7,6},{0,7},{9,8},{10,9},{11,1... | collective-permute-start | bytes 110600 | tf_op jit(solution)/shard_map/ppermute | solution.py:529
  52.9 2.0 %collective-permute-start.6 = (bf16[32,64,128]{2,1,0:T(8,128)(2,1)S(1)}, bf16[32,64,128]{2,1,0:T(8,128)(2,1)S(1)}, u32[]{:S(2)}, u32[]{:S(2)}) collective-permute-start(bf16[32,64,128]{2,1,0:T(8,128)(2,1)S(1)} %get-tuple-element.39), channel_id=1, source_target_pairs={{0,64},{64,0},{1,65},{65,1},{2,66},{66,2},{3,67},{67,3},{4,68},{68... | collective-permute-start | bytes 1572872 | tf_op jit(solution)/shard_map/ppermute | solution.py:592
  55.8 25.0 %all-to-all-start = ((bf16[64,32,128]{2,1,0:T(8,128)(2,1)}), bf16[64,32,128]{2,1,0:T(8,128)(2,1)S(1)}, u32[]{:S(2)}, u32[]{:S(2)}) async-start(bf16[64,32,128]{2,1,0:T(8,128)(2,1)} %bitcast.6), calls=%async_computation | async-start | bytes 1048576 | tf_op jit(solution)/shard_map/all_to_all | solution.py:595
  81.8 17.1 %all-to-all-start.1 = ((bf16[64,32,128]{2,1,0:T(8,128)(2,1)}), bf16[64,32,128]{2,1,0:T(8,128)(2,1)S(1)}, u32[]{:S(2)}, u32[]{:S(2)}) async-start(bf16[64,32,128]{2,1,0:T(8,128)(2,1)} %broadcast_in_dim.17), calls=%async_computation.1 | async-start | bytes 1048576 | tf_op jit(solution)/shard_map/all_to_all | solution.py:599

commit v4 on v3

--- a/solution.py
+++ b/solution.py
@@ -17,6 +17,7 @@
 PAIRS = 4
 CHUNKS = 4
 EDGE = 16
+LOW_ENDS, HIGH_ENDS = 2 * FIELD_LOW + 2, 2 * FIELD_HIGH + 2
 TAPS = 32
 
 
@@ -62,8 +63,8 @@
     high_hbm,
     west_hbm,
     east_hbm,
-    west_ends_hbm,
-    east_ends_hbm,
+    low_ends_hbm,
+    high_ends_hbm,
     weights_hbm,
     own_out,
     other_out,
@@ -75,8 +76,8 @@
     high,
     west,
     east,
-    west_ends,
-    east_ends,
+    low_ends,
+    high_ends,
     weights,
     p_down,
     p_mid,
@@ -110,8 +111,8 @@
                 (high_hbm, high),
                 (west_hbm, west),
                 (east_hbm, east),
-                (west_ends_hbm, west_ends),
-                (east_ends_hbm, east_ends),
+                (low_ends_hbm, low_ends),
+                (high_ends_hbm, high_ends),
             ]
         )
     ]
@@ -131,23 +132,33 @@
     for copy in edge_copies:
         copy.wait()
 
-    def end_rows(rows_in, at, count, dest, p):
-        for k in range(count):
-            end = at + k if rows_in is low else low.shape[0] + at + k
+    def end_rows(rows_in, ends, fields_in, cots_in, row_of_cot, first_row, field_at, cot_at):
+        for k in range(fields_in):
             split_row(
                 stage.at[k % 4],
-                rows_in[at + k],
-                dest,
-                (p + k) // 4,
-                (p + k) % 4,
-                west_ends[end],
-                east_ends[end],
+                rows_in[k],
+                field_taps,
+                (field_at + k) // 4,
+                (field_at + k) % 4,
+                ends[k],
+                ends[fields_in + k],
             )
-
-    end_rows(low, 0, FIELD_LOW, field_taps, 0)
-    end_rows(low, FIELD_LOW, COT_LOW, cot_taps, 0)
-    end_rows(high, 0, FIELD_HIGH, field_taps, FIELD_LOW + rows)
-    end_rows(high, FIELD_HIGH, COT_HIGH, cot_taps, COT_LOW + rows)
+        for k in range(cots_in):
+            end = row_of_cot + k
+            spare = 2 * ((first_row + end) % 4)
+            split_row(
+                stage.at[k % 4],
+                rows_in[fields_in + k],
+                cot_taps,
+                (cot_at + k) // 4,
+                (cot_at + k) % 4,
+                ends[end, :COT_LOW],
+                ends[fields_in + end, FIELD_HIGH:],
+                ends[2 * fields_in + (first_row % 4 + end) // 4, spare : spare + 2],
+            )
+
+    end_rows(low, low_ends, FIELD_LOW, COT_LOW, FIELD_LOW - COT_LOW, rows - FIELD_LOW, 0, 0)
+    end_rows(high, high_ends, FIELD_HIGH, COT_HIGH, 0, 0, FIELD_LOW + rows, COT_LOW + rows)
 
     def own_rows(t, carry):
         for k in range(4):
@@ -487,7 +498,8 @@
     def row(start, count):
         return (pl.ds(start, count), every, every)
 
-    first, last = (every, pl.ds(0, 8), every), (every, pl.ds(cols - 8, 8), every)
+    east, west = columns(fields, cot)
+    east, west, fields, cot = lax.optimization_barrier((east, west, fields, cot))
     up, down = copied(
         "edges",
         [(lows, cols, C), (highs, cols, C)],
@@ -501,33 +513,34 @@
         fields,
         cot,
     )
-    up, down, fields, cot = lax.optimization_barrier((up, down, fields, cot))
-    east, west = columns(fields, cot)
     north = [(i, i + 1) for i in range(lat - 1)]
     south = [(j, i) for i, j in north]
     eastward = [(i, (i + 1) % lon) for i in range(lon)]
     westward = [(j, i) for i, j in eastward]
+    from_west = lax.ppermute(east, "lon", eastward)
+    from_east = lax.ppermute(west, "lon", westward)
     low = lax.ppermute(up, "lat", north)
     high = lax.ppermute(down, "lat", south)
-    from_west = lax.ppermute(east, "lon", eastward)
-    from_east = lax.ppermute(west, "lon", westward)
-    low, high, weights = lax.optimization_barrier((low, high, weights))
-    east, west = copied(
-        "ends",
-        [(lows + highs, 8, C)] * 2,
+    from_west, from_east, weights = lax.optimization_barrier((from_west, from_east, weights))
+    spare = rows + (rows - FIELD_LOW) // 4
+    up, down = copied(
+        "corners",
+        [(LOW_ENDS, 8, C), (HIGH_ENDS, 8, C)],
         [
-            (0, last, 0, row(0, lows)),
-            (1, last, 0, row(lows, highs)),
-            (0, first, 1, row(0, lows)),
-            (1, first, 1, row(lows, highs)),
+            (0, row(rows - FIELD_LOW, FIELD_LOW), 0, row(0, FIELD_LOW)),
+            (1, row(rows - FIELD_LOW, FIELD_LOW), 0, row(FIELD_LOW, FIELD_LOW)),
+            (1, row(spare, 2), 0, row(2 * FIELD_LOW, 2)),
+            (0, row(0, FIELD_HIGH), 1, row(0, FIELD_HIGH)),
+            (1, row(0, FIELD_HIGH), 1, row(FIELD_HIGH, FIELD_HIGH)),
+            (1, row(rows, 2), 1, row(2 * FIELD_HIGH, 2)),
         ],
         2,
-        low,
-        high,
-    )
-    west_ends = lax.ppermute(east, "lon", eastward)
-    east_ends = lax.ppermute(west, "lon", westward)
-    return (low, high, from_west, from_east, west_ends, east_ends), weights
+        from_west,
+        from_east,
+    )
+    low_ends = lax.ppermute(up, "lat", north)
+    high_ends = lax.ppermute(down, "lat", south)
+    return (low, high, from_west, from_east, low_ends, high_ends), weights
 
 
 def body(fields, down_weight, mid_weight, up_weight, cotangent):

time: 100 us -> 95.5 us (0.955)
  waiting for transfers between devices: 27.7 us -> 20.5 us
  starting transfers between devices: 31.8 us -> 33.9 us
    ppermute x1, waiting for transfers between devices: 8.34 us -> 0.01 us  [halos(): high = lax.ppermute(down, 'lat', south)]
    ppermute x2, starting transfers between devices: 4.79 us -> 7.97 us  [the longest x1 6.68 us: halos(): low_ends = lax.ppermute(up, 'lat', north)]
    ppermute x2, waiting for transfers between devices: 1.85 us -> 3 us  [the longest x1 1.5 us: halos(): low_ends = lax.ppermute(up, 'lat', north)]
where the time goes in v4:
time: 95.5 us; the launch traced here: 95.1 us
  Pallas kernels  34.5 us (36%)
  starting transfers between devices  33.9 us (35%)
  waiting for transfers between devices  20.5 us (21%)
  blocking collectives  2.44 us (3%)
  local copies, waits for them, and re-layouts  1.85 us (2%)
  other arithmetic  1.13 us (1%)
    pallas_call x1, Pallas kernels, body(): pl.pallas_call(functools.partial(grads_kernel, half_rows, half_cols, lats...  20 us
    pallas_call x2, Pallas kernels, spread(): pl.pallas_call(functools.partial(up_kernel, above, kind, swapped), out_sh...  10.4 us
    all_to_all x1, starting transfers between devices, body(): pieces = lax.all_to_all(pieces, ('lat', 'lon'), 0, 0, tiled=True)  10.4 us
    all_to_all x1, waiting for transfers between devices, body(): pieces = lax.all_to_all(pieces, ('lat', 'lon'), 0, 0, tiled=True)  8.47 us
    all_to_all x1, waiting for transfers between devices, body(): lax.all_to_all(jnp.broadcast_to(piece, pieces.shape), ('lat', 'lon'), 0,...  7.08 us
    ppermute x1, starting transfers between devices, halos(): low_ends = lax.ppermute(up, 'lat', north)  6.68 us
    ppermute x1, starting transfers between devices, halos(): low = lax.ppermute(up, 'lat', north)  5.2 us
    all_to_all x1, starting transfers between devices, body(): lax.all_to_all(jnp.broadcast_to(piece, pieces.shape), ('lat', 'lon'), 0,...  4.73 us
  transfers between devices with their start and end apart: 9, of which 5 were waited for; matrix products, arithmetic and copies ran while one was open for 0% of the time, Pallas kernels for 13%

profile of v4, /device:TPU:0, one launch (start us, length us, event | category | flops | bytes accessed | tf_op | source)
XLA Modules:
  0.0 95.1 jit_solution(14423120213041949432)
XLA Ops:
  0.6 2.1 %columns.1 = (bf16[80,8,128]{2,1,0:T(8,128)(2,1)}, bf16[100,8,128]{2,1,0:T(8,128)(2,1)}) custom-call(bf16[80,128,128]{2,1,0:T(8,128)(2,1)} %bitcast.19, bf16[80,128,128]{2,1,0:T(8,128)(2,1)} %bitcast.23), custom_call_target="tpu_custom_call" | custom-call | tf_op jit(solution)/shard_map/columns/pallas_call | solution.py:473
  2.7 0.0 copy-start.1
  2.7 0.0 copy-start.2
  2.7 0.0 copy-start.3
  2.7 1.6 %collective-permute-start.2 = (bf16[80,8,128]{2,1,0:T(8,128)(2,1)}, bf16[80,8,128]{2,1,0:T(8,128)(2,1)S(1)}, u32[]{:S(2)}, u32[]{:S(2)}) collective-permute-start(bf16[80,8,128]{2,1,0:T(8,128)(2,1)} %get-tuple-element.31), channel_id=1, source_target_pairs={{0,1},{1,2},{2,3},{3,4},{4,5},{5,6},{6,7},{7,0},{8,9},{9,10},{10,1... | collective-permute-start | bytes 491528 | tf_op jit(solution)/shard_map/ppermute | solution.py:520
  4.4 2.6 %collective-permute-start.3 = (bf16[100,8,128]{2,1,0:T(8,128)(2,1)}, bf16[100,8,128]{2,1,0:T(8,128)(2,1)S(1)}, u32[]{:S(2)}, u32[]{:S(2)}) collective-permute-start(bf16[100,8,128]{2,1,0:T(8,128)(2,1)} %get-tuple-element.32), channel_id=1, source_target_pairs={{1,0},{2,1},{3,2},{4,3},{5,4},{6,5},{7,6},{0,7},{9,8},{10,9},{11,1... | collective-permute-start | bytes 614408 | tf_op jit(solution)/shard_map/ppermute | solution.py:521
  6.9 2.0 %edges.1 = (bf16[8,128,128]{2,1,0:T(8,128)(2,1)}, bf16[10,128,128]{2,1,0:T(8,128)(2,1)}) custom-call(bf16[80,128,128]{2,1,0:T(8,128)(2,1)} %bitcast.20, bf16[80,128,128]{2,1,0:T(8,128)(2,1)} %bitcast.24), custom_call_target="tpu_custom_call" | custom-call | tf_op jit(solution)/shard_map/edges/pallas_call | solution.py:434
  8.9 5.2 %collective-permute-start = (bf16[8,128,128]{2,1,0:T(8,128)(2,1)}, bf16[8,128,128]{2,1,0:T(8,128)(2,1)S(1)}, u32[]{:S(2)}, u32[]{:S(2)}) collective-permute-start(bf16[8,128,128]{2,1,0:T(8,128)(2,1)} %get-tuple-element.29), channel_id=1, source_target_pairs={{0,8},{8,16},{16,24},{24,32},{32,40},{40,48},{48,56},{1,9},{9,17},... | collective-permute-start | bytes 786440 | tf_op jit(solution)/shard_map/ppermute | solution.py:522
  14.1 1.3 %collective-permute-start.1 = (bf16[10,128,128]{2,1,0:T(8,128)(2,1)}, bf16[10,128,128]{2,1,0:T(8,128)(2,1)S(1)}, u32[]{:S(2)}, u32[]{:S(2)}) collective-permute-start(bf16[10,128,128]{2,1,0:T(8,128)(2,1)} %get-tuple-element.30), channel_id=1, source_target_pairs={{8,0},{16,8},{24,16},{32,24},{40,32},{48,40},{56,48},{9,1},{17,9},... | collective-permute-start | bytes 983048 | tf_op jit(solution)/shard_map/ppermute | solution.py:523
  15.4 0.0 copy-done.1
  15.4 0.0 copy-done.2
  15.4 0.0 copy-done.3
  15.4 0.1 pad_maximum_fusion
  15.5 2.4 %all_gather.3 = bf16[3,3,3,128,128]{4,3,2,1,0:T(8,128)(2,1)S(1)} all-gather(bf16[3,3,3,64,128]{4,3,2,1,0:T(8,128)(2,1)S(1)} %pad_maximum_fusion), channel_id=1, replica_groups=mesh['dp'=2,'lat'=8,'lon'=8] {'dp'}, dimensions={3}, use_global_device_ids=true | all-gather | bytes 1327104 | tf_op jit(solution)/shard_map/all_gather | solution.py:552
  17.9 0.0 copy-start
  17.9 0.0 collective-permute-done.2.refs_0_.west_hbm
  18.0 0.0 collective-permute-done.3.refs_1_.east_hbm
  18.0 0.1 corners.1
  18.1 1.3 %collective-permute-start.5 = (bf16[14,8,128]{2,1,0:T(8,128)(2,1)S(1)}, bf16[14,8,128]{2,1,0:T(8,128)(2,1)S(1)}, u32[]{:S(2)}, u32[]{:S(2)}) collective-permute-start(bf16[14,8,128]{2,1,0:T(8,128)(2,1)S(1)} %get-tuple-element.36), channel_id=1, source_target_pairs={{8,0},{16,8},{24,16},{32,24},{40,32},{48,40},{56,48},{9,1},{17,9},... | collective-permute-start | bytes 86024 | tf_op jit(solution)/shard_map/ppermute | solution.py:542
  19.4 6.7 %collective-permute-start.4 = (bf16[12,8,128]{2,1,0:T(8,128)(2,1)S(1)}, bf16[12,8,128]{2,1,0:T(8,128)(2,1)S(1)}, u32[]{:S(2)}, u32[]{:S(2)}) collective-permute-start(bf16[12,8,128]{2,1,0:T(8,128)(2,1)S(1)} %get-tuple-element.35), channel_id=1, source_target_pairs={{0,8},{8,16},{16,24},{24,32},{32,40},{40,48},{48,56},{1,9},{9,17},... | collective-permute-start | bytes 73736 | tf_op jit(solution)/shard_map/ppermute | solution.py:541
  26.1 1.5 %collective-permute-done.4.low_ends_hbm = bf16[12,8,128]{2,1,0:T(8,128)(2,1)S(1)} collective-permute-done((bf16[12,8,128]{2,1,0:T(8,128)(2,1)S(1)}, bf16[12,8,128]{2,1,0:T(8,128)(2,1)S(1)}, u32[]{:S(2)}, u32[]{:S(2)}) %collective-permute-start.4) | collective-permute-done | bytes 24608 | tf_op jit(solution)/shard_map/ppermute | solution.py:541
  27.6 1.5 %collective-permute-done.5.high_ends_hbm = bf16[14,8,128]{2,1,0:T(8,128)(2,1)S(1)} collective-permute-done((bf16[14,8,128]{2,1,0:T(8,128)(2,1)S(1)}, bf16[14,8,128]{2,1,0:T(8,128)(2,1)S(1)}, u32[]{:S(2)}, u32[]{:S(2)}) %collective-permute-start.5) | collective-permute-done | bytes 28704 | tf_op jit(solution)/shard_map/ppermute | solution.py:542
  29.1 0.0 collective-permute-done.low_hbm
  29.1 0.0 collective-permute-done.1.high_hbm
  29.1 20.0 %grads.1 = (f32[32,64,128]{2,1,0:T(8,128)S(1)}, bf16[32,64,128]{2,1,0:T(8,128)(2,1)S(1)}, bf16[23,2,64,256]{3,2,1,0:T(8,128)(2,1)}, bf16[23,2,64,256]{3,2,1,0:T(8,128)(2,1)}) custom-call(bf16[80,128,128]{2,1,0:T(8,128)(2,1)} %bitcast.21, bf16[80,128,128]{2,1,0:T(8,128)(2,1)} %bitcast.25, bf16[8,128,128]{2,1,0:T(8,128)(2,1)S(1)} %collective-permute-done.low_hbm, ...), custom_call_target="tpu_custom_call" | custom-call | flops 5872025600 | bytes 8388608 | tf_op jit(solution)/shard_map/grads/pallas_call | solution.py:563
  49.1 0.0 copy-done
  49.1 0.1 collective-permute-start.6
  49.2 1.9 %collective-permute-done.6 = bf16[32,64,128]{2,1,0:T(8,128)(2,1)S(1)} collective-permute-done((bf16[32,64,128]{2,1,0:T(8,128)(2,1)S(1)}, bf16[32,64,128]{2,1,0:T(8,128)(2,1)S(1)}, u32[]{:S(2)}, u32[]{:S(2)}) %collective-permute-start.6) | collective-permute-done | bytes 524320 | tf_op jit(solution)/shard_map/ppermute | solution.py:605
  51.1 1.0 %add_convert_fusion = bf16[32,64,128]{2,1,0:T(8,128)(2,1)} fusion(f32[32,64,128]{2,1,0:T(8,128)S(1)} %get-tuple-element.38, bf16[32,64,128]{2,1,0:T(8,128)(2,1)S(1)} %collective-permute-done.6), kind=kLoop, calls=%fused_computation | loop fusion | flops 786432 | bytes 2097152 | tf_op jit(solution)/shard_map/convert_element_type | solution.py:606
  52.0 10.4 %all-to-all-start = ((bf16[64,32,128]{2,1,0:T(8,128)(2,1)}), bf16[64,32,128]{2,1,0:T(8,128)(2,1)S(1)}, u32[]{:S(2)}, u32[]{:S(2)}) async-start(bf16[64,32,128]{2,1,0:T(8,128)(2,1)} %bitcast.6), calls=%async_computation | async-start | bytes 1048576 | tf_op jit(solution)/shard_map/all_to_all | solution.py:608
  62.4 5.2 %level.1 = bf16[80,128,128]{2,1,0:T(8,128)(2,1)} custom-call(bf16[46,64,256]{2,1,0:T(8,128)(2,1)} %bitcast.30, bf16[80,128,128]{2,1,0:T(8,128)(2,1)} %bitcast.22, bf16[3,1152,128]{2,1,0:T(8,128)(2,1)} %bitcast.17), custom_call_target="tpu_custom_call" | custom-call | flops 754974720 | bytes 7340032 | tf_op jit(solution)/shard_map/level/pallas_call | solution.py:400
  67.6 8.5 %all-to-all-done = bf16[64,32,128]{2,1,0:T(8,128)(2,1)S(1)} async-done(((bf16[64,32,128]{2,1,0:T(8,128)(2,1)}), bf16[64,32,128]{2,1,0:T(8,128)(2,1)S(1)}, u32[]{:S(2)}, u32[]{:S(2)}) %all-to-all-start) | async-done | bytes 524320 | tf_op jit(solution)/shard_map/all_to_all | solution.py:608
  76.1 0.1 reduce_sum.12
  76.2 0.9 broadcast_in_dim.17
  77.1 4.7 %all-to-all-start.1 = ((bf16[64,32,128]{2,1,0:T(8,128)(2,1)}), bf16[64,32,128]{2,1,0:T(8,128)(2,1)S(1)}, u32[]{:S(2)}, u32[]{:S(2)}) async-start(bf16[64,32,128]{2,1,0:T(8,128)(2,1)} %broadcast_in_dim.17), calls=%async_computation.1 | async-start | bytes 1048576 | tf_op jit(solution)/shard_map/all_to_all | solution.py:612
  81.8 5.2 %gradient.1 = bf16[80,128,128]{2,1,0:T(8,128)(2,1)} custom-call(bf16[46,64,256]{2,1,0:T(8,128)(2,1)} %bitcast.29, bf16[80,128,128]{2,1,0:T(8,128)(2,1)} %bitcast.26, bf16[3,1152,128]{2,1,0:T(8,128)(2,1)} %bitcast.18), custom_call_target="tpu_custom_call" | custom-call | flops 754974720 | bytes 7340032 | tf_op jit(solution)/shard_map/gradient/pallas_call | solution.py:400
  87.1 7.1 %all-to-all-done.1 = bf16[64,32,128]{2,1,0:T(8,128)(2,1)S(1)} async-done(((bf16[64,32,128]{2,1,0:T(8,128)(2,1)}), bf16[64,32,128]{2,1,0:T(8,128)(2,1)S(1)}, u32[]{:S(2)}, u32[]{:S(2)}) %all-to-all-start.1) | async-done | bytes 524320 | tf_op jit(solution)/shard_map/all_to_all | solution.py:612
  94.1 0.9 fusion
Async XLA Ops:
  2.7 12.7 %copy-start.1 = (bf16[3,3,64,128]{3,2,1,0:T(8,128)(2,1)S(1)}, bf16[3,3,64,128]{3,2,1,0:T(8,128)(2,1)}, u32[]{:S(2)}) copy-start(bf16[3,3,64,128]{3,2,1,0:T(8,128)(2,1)} %param.8) | copy-start | bytes 442372
  2.7 12.7 %copy-start.2 = (bf16[3,3,64,128]{3,2,1,0:T(8,128)(2,1)S(1)}, bf16[3,3,64,128]{3,2,1,0:T(8,128)(2,1)}, u32[]{:S(2)}) copy-start(bf16[3,3,64,128]{3,2,1,0:T(8,128)(2,1)} %param.7) | copy-start | bytes 442372
  2.7 12.7 %copy-start.3 = (bf16[3,3,64,128]{3,2,1,0:T(8,128)(2,1)S(1)}, bf16[3,3,64,128]{3,2,1,0:T(8,128)(2,1)}, u32[]{:S(2)}) copy-start(bf16[3,3,64,128]{3,2,1,0:T(8,128)(2,1)} %param.6) | copy-start | bytes 442372
  2.7 15.2 %collective-permute-start.2 = (bf16[80,8,128]{2,1,0:T(8,128)(2,1)}, bf16[80,8,128]{2,1,0:T(8,128)(2,1)S(1)}, u32[]{:S(2)}, u32[]{:S(2)}) collective-permute-start(bf16[80,8,128]{2,1,0:T(8,128)(2,1)} %get-tuple-element.31), channel_id=1, source_target_pairs={{0,1},{1,2},{2,3},{3,4},{4,5},{5,6},{6,7},{7,0},{8,9},{9,10},{10,1... | collective-permute-start | bytes 491528 | tf_op jit(solution)/shard_map/ppermute | solution.py:520
  4.4 13.6 %collective-permute-start.3 = (bf16[100,8,128]{2,1,0:T(8,128)(2,1)}, bf16[100,8,128]{2,1,0:T(8,128)(2,1)S(1)}, u32[]{:S(2)}, u32[]{:S(2)}) collective-permute-start(bf16[100,8,128]{2,1,0:T(8,128)(2,1)} %get-tuple-element.32), channel_id=1, source_target_pairs={{1,0},{2,1},{3,2},{4,3},{5,4},{6,5},{7,6},{0,7},{9,8},{10,9},{11,1... | collective-permute-start | bytes 614408 | tf_op jit(solution)/shard_map/ppermute | solution.py:521
  8.9 20.2 %collective-permute-start = (bf16[8,128,128]{2,1,0:T(8,128)(2,1)}, bf16[8,128,128]{2,1,0:T(8,128)(2,1)S(1)}, u32[]{:S(2)}, u32[]{:S(2)}) collective-permute-start(bf16[8,128,128]{2,1,0:T(8,128)(2,1)} %get-tuple-element.29), channel_id=1, source_target_pairs={{0,8},{8,16},{16,24},{24,32},{32,40},{40,48},{48,56},{1,9},{9,17},... | collective-permute-start | bytes 786440 | tf_op jit(solution)/shard_map/ppermute | solution.py:522
  14.1 15.0 %collective-permute-start.1 = (bf16[10,128,128]{2,1,0:T(8,128)(2,1)}, bf16[10,128,128]{2,1,0:T(8,128)(2,1)S(1)}, u32[]{:S(2)}, u32[]{:S(2)}) collective-permute-start(bf16[10,128,128]{2,1,0:T(8,128)(2,1)} %get-tuple-element.30), channel_id=1, source_target_pairs={{8,0},{16,8},{24,16},{32,24},{40,32},{48,40},{56,48},{9,1},{17,9},... | collective-permute-start | bytes 983048 | tf_op jit(solution)/shard_map/ppermute | solution.py:523
  17.9 31.1 %copy-start = (bf16[3,3,3,128,128]{4,3,2,1,0:T(8,128)(2,1)}, bf16[3,3,3,128,128]{4,3,2,1,0:T(8,128)(2,1)S(1)}, u32[]{:S(2)}) copy-start(bf16[3,3,3,128,128]{4,3,2,1,0:T(8,128)(2,1)S(1)} %all_gather.3) | copy-start | bytes 2654212
  18.1 11.0 %collective-permute-start.5 = (bf16[14,8,128]{2,1,0:T(8,128)(2,1)S(1)}, bf16[14,8,128]{2,1,0:T(8,128)(2,1)S(1)}, u32[]{:S(2)}, u32[]{:S(2)}) collective-permute-start(bf16[14,8,128]{2,1,0:T(8,128)(2,1)S(1)} %get-tuple-element.36), channel_id=1, source_target_pairs={{8,0},{16,8},{24,16},{32,24},{40,32},{48,40},{56,48},{9,1},{17,9},... | collective-permute-start | bytes 86024 | tf_op jit(solution)/shard_map/ppermute | solution.py:542
  19.4 8.2 %collective-permute-start.4 = (bf16[12,8,128]{2,1,0:T(8,128)(2,1)S(1)}, bf16[12,8,128]{2,1,0:T(8,128)(2,1)S(1)}, u32[]{:S(2)}, u32[]{:S(2)}) collective-permute-start(bf16[12,8,128]{2,1,0:T(8,128)(2,1)S(1)} %get-tuple-element.35), channel_id=1, source_target_pairs={{0,8},{8,16},{16,24},{24,32},{32,40},{40,48},{48,56},{1,9},{9,17},... | collective-permute-start | bytes 73736 | tf_op jit(solution)/shard_map/ppermute | solution.py:541
  49.1 2.0 %collective-permute-start.6 = (bf16[32,64,128]{2,1,0:T(8,128)(2,1)S(1)}, bf16[32,64,128]{2,1,0:T(8,128)(2,1)S(1)}, u32[]{:S(2)}, u32[]{:S(2)}) collective-permute-start(bf16[32,64,128]{2,1,0:T(8,128)(2,1)S(1)} %get-tuple-element.39), channel_id=1, source_target_pairs={{0,64},{64,0},{1,65},{65,1},{2,66},{66,2},{3,67},{67,3},{4,68},{68... | collective-permute-start | bytes 1572872 | tf_op jit(solution)/shard_map/ppermute | solution.py:605
  52.0 24.0 %all-to-all-start = ((bf16[64,32,128]{2,1,0:T(8,128)(2,1)}), bf16[64,32,128]{2,1,0:T(8,128)(2,1)S(1)}, u32[]{:S(2)}, u32[]{:S(2)}) async-start(bf16[64,32,128]{2,1,0:T(8,128)(2,1)} %bitcast.6), calls=%async_computation | async-start | bytes 1048576 | tf_op jit(solution)/shard_map/all_to_all | solution.py:608
  77.1 17.1 %all-to-all-start.1 = ((bf16[64,32,128]{2,1,0:T(8,128)(2,1)}), bf16[64,32,128]{2,1,0:T(8,128)(2,1)S(1)}, u32[]{:S(2)}, u32[]{:S(2)}) async-start(bf16[64,32,128]{2,1,0:T(8,128)(2,1)} %broadcast_in_dim.17), calls=%async_computation.1 | async-start | bytes 1048576 | tf_op jit(solution)/shard_map/all_to_all | solution.py:612

commit v5 on v4

--- a/solution.py
+++ b/solution.py
@@ -442,17 +442,30 @@
     )(*arrays)
 
 
-def columns_kernel(fields_hbm, cot_hbm, east, west, ends, spare, sems):
+def pack_kernel(fields_hbm, cot_hbm, east, west, up, down, ends, spare, sems):
     rows, cols, _ = fields_hbm.shape
-    copies = [
+    column_copies = [
         pltpu.make_async_copy(source.at[:, pl.ds(at, 8), :], ends.at[k], sems.at[k])
         for k, (source, at) in enumerate(
             [(fields_hbm, cols - 8), (cot_hbm, cols - 8), (fields_hbm, 0), (cot_hbm, 0)]
         )
     ]
-    for copy in copies:
+    row_copies = [
+        pltpu.make_async_copy(
+            source.at[pl.ds(at, count)], dest.at[pl.ds(place, count)], sems.at[4 + k]
+        )
+        for k, (source, at, count, dest, place) in enumerate(
+            [
+                (fields_hbm, rows - FIELD_LOW, FIELD_LOW, up, 0),
+                (cot_hbm, rows - COT_LOW, COT_LOW, up, FIELD_LOW),
+                (fields_hbm, 0, FIELD_HIGH, down, 0),
+                (cot_hbm, 0, COT_HIGH, down, FIELD_HIGH),
+            ]
+        )
+    ]
+    for copy in column_copies + row_copies:
         copy.start()
-    for copy in copies:
+    for copy in column_copies:
         copy.wait()
     field, other = ends[0].astype(F32), ends[1].astype(F32)
     east[...] = jnp.concatenate(
@@ -465,54 +478,57 @@
     for k in range(4):
         spare[:, 2 * k : 2 * k + 2, :] = other[:, k, beside:COT_HIGH]
     west[rows:] = spare[...].astype(BF16)
-
-
-def columns(fields, cot):
-    rows = fields.shape[0]
+    for copy in row_copies:
+        copy.wait()
+
+
+def packed(fields, cot):
+    rows, cols, _ = fields.shape
     vmem = pl.BlockSpec(memory_space=pltpu.VMEM)
     return pl.pallas_call(
-        columns_kernel,
+        pack_kernel,
         out_shape=(
             jax.ShapeDtypeStruct((rows, 8, C), BF16),
             jax.ShapeDtypeStruct((rows + rows // 4, 8, C), BF16),
+            jax.ShapeDtypeStruct((FIELD_LOW + COT_LOW, cols, C), BF16),
+            jax.ShapeDtypeStruct((FIELD_HIGH + COT_HIGH, cols, C), BF16),
         ),
         in_specs=[pl.BlockSpec(memory_space=pl.ANY)] * 2,
-        out_specs=(vmem, vmem),
+        out_specs=(vmem,) * 4,
         scratch_shapes=[
             pltpu.VMEM((4, rows, 8, C), BF16),
             pltpu.VMEM((rows // 4, 8, C), F32),
-            pltpu.SemaphoreType.DMA((4,)),
+            pltpu.SemaphoreType.DMA((8,)),
         ],
-        compiler_params=pltpu.CompilerParams(vmem_limit_bytes=60 * 2**20),
-        name="columns",
+        compiler_params=pltpu.CompilerParams(vmem_limit_bytes=52 * 2**20),
+        name="pack",
     )(fields, cot)
+
+
+def passed(*arrays):
+    hbm = pl.BlockSpec(memory_space=pl.ANY)
+    return pl.pallas_call(
+        lambda *refs: None,
+        out_shape=tuple(jax.ShapeDtypeStruct(array.shape, array.dtype) for array in arrays),
+        in_specs=[hbm] * len(arrays),
+        out_specs=(hbm,) * len(arrays),
+        input_output_aliases={k: k for k in range(len(arrays))},
+        compiler_params=pltpu.CompilerParams(vmem_limit_bytes=2**20),
+        name="passed",
+    )(*arrays)
 
 
 def halos(fields, cot, weights):
     lat = lax.axis_size("lat")
     lon = lax.axis_size("lon")
-    rows, cols, _ = fields.shape
-    lows, highs = FIELD_LOW + COT_LOW, FIELD_HIGH + COT_HIGH
+    rows = fields.shape[0]
     every = slice(None)
 
     def row(start, count):
         return (pl.ds(start, count), every, every)
 
-    east, west = columns(fields, cot)
-    east, west, fields, cot = lax.optimization_barrier((east, west, fields, cot))
-    up, down = copied(
-        "edges",
-        [(lows, cols, C), (highs, cols, C)],
-        [
-            (0, row(rows - FIELD_LOW, FIELD_LOW), 0, row(0, FIELD_LOW)),
-            (1, row(rows - COT_LOW, COT_LOW), 0, row(FIELD_LOW, COT_LOW)),
-            (0, row(0, FIELD_HIGH), 1, row(0, FIELD_HIGH)),
-            (1, row(0, COT_HIGH), 1, row(FIELD_HIGH, COT_HIGH)),
-        ],
-        60,
-        fields,
-        cot,
-    )
+    east, west, up, down = packed(fields, cot)
+    up, down = passed(up, down)
     north = [(i, i + 1) for i in range(lat - 1)]
     south = [(j, i) for i, j in north]
     eastward = [(i, (i + 1) % lon) for i in range(lon)]
@@ -521,7 +537,6 @@
     from_east = lax.ppermute(west, "lon", westward)
     low = lax.ppermute(up, "lat", north)
     high = lax.ppermute(down, "lat", south)
-    from_west, from_east, weights = lax.optimization_barrier((from_west, from_east, weights))
     spare = rows + (rows - FIELD_LOW) // 4
     up, down = copied(
         "corners",
@@ -538,8 +553,10 @@
         from_west,
         from_east,
     )
+    up, down, weights = lax.optimization_barrier((up, down, weights))
     low_ends = lax.ppermute(up, "lat", north)
     high_ends = lax.ppermute(down, "lat", south)
+    weights = lax.all_gather(weights, "dp", axis=3, tiled=True)
     return (low, high, from_west, from_east, low_ends, high_ends), weights
 
 
@@ -549,9 +566,7 @@
     half_rows, half_cols = rows // 2, cols // 2
     scale = 1.0 / math.sqrt(parts * rows * lats * cols * lons)
     fields, cotangent = fields[0], cotangent[0]
-    weights = lax.all_gather(
-        jnp.stack([down_weight, mid_weight, up_weight]), "dp", axis=3, tiled=True
-    )
+    weights = jnp.stack([down_weight, mid_weight, up_weight])
     edges, weights = halos(fields, cotangent, weights)
     weights = weights.reshape(3, 9 * C, C)
 

time: 95.5 us -> 94.2 us (0.986)
  waiting for transfers between devices: 20.5 us -> 25.7 us
  starting transfers between devices: 33.9 us -> 29.9 us
  Pallas kernels: 34.5 us -> 32 us
    ppermute x1, waiting for transfers between devices: 1.49 us -> 6.61 us  [halos(): high_ends = lax.ppermute(down, 'lat', south)]
    pallas_call x2 -> x1, Pallas kernels: 2.1 us -> 0.12 us  [copied(): pl.pallas_call(kernel, out_shape=tuple((jax.ShapeDtypeStruct(shape, BF16)...]
    ppermute x1, starting transfers between devices: 6.68 us -> 4.81 us  [halos(): low_ends = lax.ppermute(up, 'lat', north)]
    ppermute x1, waiting for transfers between devices: 0.01 us -> 1.66 us  [halos(): from_west = lax.ppermute(east, 'lon', eastward)]
    ppermute x1, starting transfers between devices: 1.64 us -> 0.01 us  [halos(): from_west = lax.ppermute(east, 'lon', eastward)]
    ppermute x1, waiting for transfers between devices: 1.5 us -> 0.01 us  [halos(): low_ends = lax.ppermute(up, 'lat', north)]
    all_to_all x1, starting transfers between devices: 10.4 us -> 8.89 us  [body(): pieces = lax.all_to_all(pieces, ('lat', 'lon'), 0, 0, tiled=True)]
    ppermute x1, starting transfers between devices: 2.56 us -> 3.92 us  [halos(): from_east = lax.ppermute(west, 'lon', westward)]
  transfers between devices with their start and end apart: 9 -> 9, of which waited for: 5 -> 5; matrix products, arithmetic and copies ran while one was open for 0% -> 0% of each run, Pallas kernels for 13% -> 11%
where the time goes in v5:
time: 94.2 us; the launch traced here: 93.8 us
  Pallas kernels  32 us (34%)
  starting transfers between devices  29.9 us (32%)
  waiting for transfers between devices  25.7 us (27%)
  blocking collectives  2.44 us (3%)
  local copies, waits for them, and re-layouts  1.84 us (2%)
  other arithmetic  1.13 us (1%)
    pallas_call x1, Pallas kernels, body(): pl.pallas_call(functools.partial(grads_kernel, half_rows, half_cols, lats...  20 us
    pallas_call x2, Pallas kernels, spread(): pl.pallas_call(functools.partial(up_kernel, above, kind, swapped), out_sh...  10.4 us
    all_to_all x1, starting transfers between devices, body(): pieces = lax.all_to_all(pieces, ('lat', 'lon'), 0, 0, tiled=True)  8.89 us
    all_to_all x1, waiting for transfers between devices, body(): pieces = lax.all_to_all(pieces, ('lat', 'lon'), 0, 0, tiled=True)  8.47 us
    all_to_all x1, waiting for transfers between devices, body(): lax.all_to_all(jnp.broadcast_to(piece, pieces.shape), ('lat', 'lon'), 0,...  7.08 us
    ppermute x1, waiting for transfers between devices, halos(): high_ends = lax.ppermute(down, 'lat', south)  6.61 us
    ppermute x1, starting transfers between devices, halos(): low = lax.ppermute(up, 'lat', north)  4.81 us
    ppermute x1, starting transfers between devices, halos(): low_ends = lax.ppermute(up, 'lat', north)  4.81 us
  transfers between devices with their start and end apart: 9, of which 5 were waited for; matrix products, arithmetic and copies ran while one was open for 0% of the time, Pallas kernels for 11%

profile of v5, /device:TPU:0, one launch (start us, length us, event | category | flops | bytes accessed | tf_op | source)
XLA Modules:
  0.0 93.8 jit_solution(17381215072005764863)
XLA Ops:
  0.6 0.0 copy-start.1
  0.6 0.0 copy-start.2
  0.7 0.0 copy-start.3
  0.7 1.5 %pack.1 = (bf16[80,8,128]{2,1,0:T(8,128)(2,1)S(1)}, bf16[100,8,128]{2,1,0:T(8,128)(2,1)S(1)}, bf16[8,128,128]{2,1,0:T(8,128)(2,1)S(1)}, bf16[10,128,128]{2,1,0:T(8,128)(2,1)S(1)}) custom-call(bf16[80,128,128]{2,1,0:T(8,128)(2,1)} %bitcast.19, bf16[80,128,128]{2,1,0:T(8,128)(2,1)} %bitcast.22), custom_call_target="tpu_custom_call" | custom-call | tf_op jit(solution)/shard_map/pack/pallas_call | solution.py:488
  2.2 3.9 %collective-permute-start.3 = (bf16[100,8,128]{2,1,0:T(8,128)(2,1)S(1)}, bf16[100,8,128]{2,1,0:T(8,128)(2,1)S(1)}, u32[]{:S(2)}, u32[]{:S(2)}) collective-permute-start(bf16[100,8,128]{2,1,0:T(8,128)(2,1)S(1)} %get-tuple-element.28), channel_id=1, source_target_pairs={{1,0},{2,1},{3,2},{4,3},{5,4},{6,5},{7,6},{0,7},{9,8},{10,9},{11,1... | collective-permute-start | bytes 614408 | tf_op jit(solution)/shard_map/ppermute | solution.py:537
  6.1 0.0 collective-permute-start.2
  6.1 4.8 %collective-permute-start = (bf16[8,128,128]{2,1,0:T(8,128)(2,1)S(1)}, bf16[8,128,128]{2,1,0:T(8,128)(2,1)S(1)}, u32[]{:S(2)}, u32[]{:S(2)}) collective-permute-start(bf16[8,128,128]{2,1,0:T(8,128)(2,1)S(1)} %get-tuple-element.25), channel_id=1, source_target_pairs={{0,8},{8,16},{16,24},{24,32},{32,40},{40,48},{48,56},{1,9},{9,17},... | collective-permute-start | bytes 786440 | tf_op jit(solution)/shard_map/ppermute | solution.py:538
  10.9 1.3 %collective-permute-start.1 = (bf16[10,128,128]{2,1,0:T(8,128)(2,1)S(1)}, bf16[10,128,128]{2,1,0:T(8,128)(2,1)S(1)}, u32[]{:S(2)}, u32[]{:S(2)}) collective-permute-start(bf16[10,128,128]{2,1,0:T(8,128)(2,1)S(1)} %get-tuple-element.26), channel_id=1, source_target_pairs={{8,0},{16,8},{24,16},{32,24},{40,32},{48,40},{56,48},{9,1},{17,9},... | collective-permute-start | bytes 983048 | tf_op jit(solution)/shard_map/ppermute | solution.py:539
  12.2 0.0 copy-done.1
  12.2 0.0 copy-done.2
  12.2 0.0 copy-done.3
  12.2 0.1 pad_maximum_fusion
  12.3 1.7 %collective-permute-done.2.refs_0_.west_hbm = bf16[80,8,128]{2,1,0:T(8,128)(2,1)S(1)} collective-permute-done((bf16[80,8,128]{2,1,0:T(8,128)(2,1)S(1)}, bf16[80,8,128]{2,1,0:T(8,128)(2,1)S(1)}, u32[]{:S(2)}, u32[]{:S(2)}) %collective-permute-start.2) | collective-permute-done | bytes 163872 | tf_op jit(solution)/shard_map/ppermute | solution.py:536
  14.0 0.0 collective-permute-done.3.refs_1_.east_hbm
  14.0 0.1 corners.1
  14.1 4.8 %collective-permute-start.4 = (bf16[12,8,128]{2,1,0:T(8,128)(2,1)S(1)}, bf16[12,8,128]{2,1,0:T(8,128)(2,1)S(1)}, u32[]{:S(2)}, u32[]{:S(2)}) collective-permute-start(bf16[12,8,128]{2,1,0:T(8,128)(2,1)S(1)} %get-tuple-element.31), channel_id=1, source_target_pairs={{0,8},{8,16},{16,24},{24,32},{32,40},{40,48},{48,56},{1,9},{9,17},... | collective-permute-start | bytes 73736 | tf_op jit(solution)/shard_map/ppermute | solution.py:557
  18.9 1.3 %collective-permute-start.5 = (bf16[14,8,128]{2,1,0:T(8,128)(2,1)S(1)}, bf16[14,8,128]{2,1,0:T(8,128)(2,1)S(1)}, u32[]{:S(2)}, u32[]{:S(2)}) collective-permute-start(bf16[14,8,128]{2,1,0:T(8,128)(2,1)S(1)} %get-tuple-element.32), channel_id=1, source_target_pairs={{8,0},{16,8},{24,16},{32,24},{40,32},{48,40},{56,48},{9,1},{17,9},... | collective-permute-start | bytes 86024 | tf_op jit(solution)/shard_map/ppermute | solution.py:558
  20.2 2.4 %all_gather.3 = bf16[3,3,3,128,128]{4,3,2,1,0:T(8,128)(2,1)S(1)} all-gather(bf16[3,3,3,64,128]{4,3,2,1,0:T(8,128)(2,1)S(1)} %pad_maximum_fusion), channel_id=1, replica_groups=mesh['dp'=2,'lat'=8,'lon'=8] {'dp'}, dimensions={3}, use_global_device_ids=true | all-gather | bytes 1327104 | tf_op jit(solution)/shard_map/all_gather | solution.py:559
  22.6 0.0 copy-start
  22.6 0.0 collective-permute-done.4.low_ends_hbm
  22.6 6.6 %collective-permute-done.5.high_ends_hbm = bf16[14,8,128]{2,1,0:T(8,128)(2,1)S(1)} collective-permute-done((bf16[14,8,128]{2,1,0:T(8,128)(2,1)S(1)}, bf16[14,8,128]{2,1,0:T(8,128)(2,1)S(1)}, u32[]{:S(2)}, u32[]{:S(2)}) %collective-permute-start.5) | collective-permute-done | bytes 28704 | tf_op jit(solution)/shard_map/ppermute | solution.py:558
  29.3 0.0 collective-permute-done.low_hbm
  29.3 0.0 collective-permute-done.1.high_hbm
  29.3 20.0 %grads.1 = (f32[32,64,128]{2,1,0:T(8,128)S(1)}, bf16[32,64,128]{2,1,0:T(8,128)(2,1)S(1)}, bf16[23,2,64,256]{3,2,1,0:T(8,128)(2,1)}, bf16[23,2,64,256]{3,2,1,0:T(8,128)(2,1)}) custom-call(bf16[80,128,128]{2,1,0:T(8,128)(2,1)} %bitcast.20, bf16[80,128,128]{2,1,0:T(8,128)(2,1)} %bitcast.23, bf16[8,128,128]{2,1,0:T(8,128)(2,1)S(1)} %collective-permute-done.low_hbm, ...), custom_call_target="tpu_custom_call" | custom-call | flops 5872025600 | bytes 8388608 | tf_op jit(solution)/shard_map/grads/pallas_call | solution.py:578
  49.3 0.0 copy-done
  49.3 0.1 collective-permute-start.6
  49.4 1.9 %collective-permute-done.6 = bf16[32,64,128]{2,1,0:T(8,128)(2,1)S(1)} collective-permute-done((bf16[32,64,128]{2,1,0:T(8,128)(2,1)S(1)}, bf16[32,64,128]{2,1,0:T(8,128)(2,1)S(1)}, u32[]{:S(2)}, u32[]{:S(2)}) %collective-permute-start.6) | collective-permute-done | bytes 524320 | tf_op jit(solution)/shard_map/ppermute | solution.py:620
  51.3 1.0 %add_convert_fusion = bf16[32,64,128]{2,1,0:T(8,128)(2,1)} fusion(f32[32,64,128]{2,1,0:T(8,128)S(1)} %get-tuple-element.34, bf16[32,64,128]{2,1,0:T(8,128)(2,1)S(1)} %collective-permute-done.6), kind=kLoop, calls=%fused_computation | loop fusion | flops 786432 | bytes 2097152 | tf_op jit(solution)/shard_map/convert_element_type | solution.py:621
  52.2 8.9 %all-to-all-start = ((bf16[64,32,128]{2,1,0:T(8,128)(2,1)}), bf16[64,32,128]{2,1,0:T(8,128)(2,1)S(1)}, u32[]{:S(2)}, u32[]{:S(2)}) async-start(bf16[64,32,128]{2,1,0:T(8,128)(2,1)} %bitcast.6), calls=%async_computation | async-start | bytes 1048576 | tf_op jit(solution)/shard_map/all_to_all | solution.py:623
  61.1 5.2 %level.1 = bf16[80,128,128]{2,1,0:T(8,128)(2,1)} custom-call(bf16[46,64,256]{2,1,0:T(8,128)(2,1)} %bitcast.28, bf16[80,128,128]{2,1,0:T(8,128)(2,1)} %bitcast.21, bf16[3,1152,128]{2,1,0:T(8,128)(2,1)} %bitcast.17), custom_call_target="tpu_custom_call" | custom-call | flops 754974720 | bytes 7340032 | tf_op jit(solution)/shard_map/level/pallas_call | solution.py:400
  66.3 8.5 %all-to-all-done = bf16[64,32,128]{2,1,0:T(8,128)(2,1)S(1)} async-done(((bf16[64,32,128]{2,1,0:T(8,128)(2,1)}), bf16[64,32,128]{2,1,0:T(8,128)(2,1)S(1)}, u32[]{:S(2)}, u32[]{:S(2)}) %all-to-all-start) | async-done | bytes 524320 | tf_op jit(solution)/shard_map/all_to_all | solution.py:623
  74.8 0.1 reduce_sum.12
  74.9 0.9 broadcast_in_dim.17
  75.8 4.7 %all-to-all-start.1 = ((bf16[64,32,128]{2,1,0:T(8,128)(2,1)}), bf16[64,32,128]{2,1,0:T(8,128)(2,1)S(1)}, u32[]{:S(2)}, u32[]{:S(2)}) async-start(bf16[64,32,128]{2,1,0:T(8,128)(2,1)} %broadcast_in_dim.17), calls=%async_computation.1 | async-start | bytes 1048576 | tf_op jit(solution)/shard_map/all_to_all | solution.py:627
  80.5 5.2 %gradient.1 = bf16[80,128,128]{2,1,0:T(8,128)(2,1)} custom-call(bf16[46,64,256]{2,1,0:T(8,128)(2,1)} %bitcast.27, bf16[80,128,128]{2,1,0:T(8,128)(2,1)} %bitcast.24, bf16[3,1152,128]{2,1,0:T(8,128)(2,1)} %bitcast.18), custom_call_target="tpu_custom_call" | custom-call | flops 754974720 | bytes 7340032 | tf_op jit(solution)/shard_map/gradient/pallas_call | solution.py:400
  85.8 7.1 %all-to-all-done.1 = bf16[64,32,128]{2,1,0:T(8,128)(2,1)S(1)} async-done(((bf16[64,32,128]{2,1,0:T(8,128)(2,1)}), bf16[64,32,128]{2,1,0:T(8,128)(2,1)S(1)}, u32[]{:S(2)}, u32[]{:S(2)}) %all-to-all-start.1) | async-done | bytes 524320 | tf_op jit(solution)/shard_map/all_to_all | solution.py:627
  92.8 0.9 %fusion = (f32[18,32,128]{2,1,0:T(8,128)}, f32[18,32,128]{2,1,0:T(8,128)}, f32[18,32,128]{2,1,0:T(8,128)}) fusion(bf16[64,32,128]{2,1,0:T(8,128)(2,1)S(1)} %all-to-all-done.1), kind=kLoop, calls=%fused_computation.2 | loop fusion | bytes 1769472 | tf_op jit(solution)/shard_map/slice | solution.py:634
  (1 shorter events, 0.0 us)
Async XLA Ops:
  0.6 11.6 %copy-start.1 = (bf16[3,3,64,128]{3,2,1,0:T(8,128)(2,1)S(1)}, bf16[3,3,64,128]{3,2,1,0:T(8,128)(2,1)}, u32[]{:S(2)}) copy-start(bf16[3,3,64,128]{3,2,1,0:T(8,128)(2,1)} %param.8) | copy-start | bytes 442372
  0.6 11.6 %copy-start.2 = (bf16[3,3,64,128]{3,2,1,0:T(8,128)(2,1)S(1)}, bf16[3,3,64,128]{3,2,1,0:T(8,128)(2,1)}, u32[]{:S(2)}) copy-start(bf16[3,3,64,128]{3,2,1,0:T(8,128)(2,1)} %param.7) | copy-start | bytes 442372
  0.7 11.6 %copy-start.3 = (bf16[3,3,64,128]{3,2,1,0:T(8,128)(2,1)S(1)}, bf16[3,3,64,128]{3,2,1,0:T(8,128)(2,1)}, u32[]{:S(2)}) copy-start(bf16[3,3,64,128]{3,2,1,0:T(8,128)(2,1)} %param.6) | copy-start | bytes 442372
  2.2 11.8 %collective-permute-start.3 = (bf16[100,8,128]{2,1,0:T(8,128)(2,1)S(1)}, bf16[100,8,128]{2,1,0:T(8,128)(2,1)S(1)}, u32[]{:S(2)}, u32[]{:S(2)}) collective-permute-start(bf16[100,8,128]{2,1,0:T(8,128)(2,1)S(1)} %get-tuple-element.28), channel_id=1, source_target_pairs={{1,0},{2,1},{3,2},{4,3},{5,4},{6,5},{7,6},{0,7},{9,8},{10,9},{11,1... | collective-permute-start | bytes 614408 | tf_op jit(solution)/shard_map/ppermute | solution.py:537
  6.1 7.9 %collective-permute-start.2 = (bf16[80,8,128]{2,1,0:T(8,128)(2,1)S(1)}, bf16[80,8,128]{2,1,0:T(8,128)(2,1)S(1)}, u32[]{:S(2)}, u32[]{:S(2)}) collective-permute-start(bf16[80,8,128]{2,1,0:T(8,128)(2,1)S(1)} %get-tuple-element.27), channel_id=1, source_target_pairs={{0,1},{1,2},{2,3},{3,4},{4,5},{5,6},{6,7},{7,0},{8,9},{9,10},{10,1... | collective-permute-start | bytes 491528 | tf_op jit(solution)/shard_map/ppermute | solution.py:536
  6.1 23.2 %collective-permute-start = (bf16[8,128,128]{2,1,0:T(8,128)(2,1)S(1)}, bf16[8,128,128]{2,1,0:T(8,128)(2,1)S(1)}, u32[]{:S(2)}, u32[]{:S(2)}) collective-permute-start(bf16[8,128,128]{2,1,0:T(8,128)(2,1)S(1)} %get-tuple-element.25), channel_id=1, source_target_pairs={{0,8},{8,16},{16,24},{24,32},{32,40},{40,48},{48,56},{1,9},{9,17},... | collective-permute-start | bytes 786440 | tf_op jit(solution)/shard_map/ppermute | solution.py:538
  10.9 18.4 %collective-permute-start.1 = (bf16[10,128,128]{2,1,0:T(8,128)(2,1)S(1)}, bf16[10,128,128]{2,1,0:T(8,128)(2,1)S(1)}, u32[]{:S(2)}, u32[]{:S(2)}) collective-permute-start(bf16[10,128,128]{2,1,0:T(8,128)(2,1)S(1)} %get-tuple-element.26), channel_id=1, source_target_pairs={{8,0},{16,8},{24,16},{32,24},{40,32},{48,40},{56,48},{9,1},{17,9},... | collective-permute-start | bytes 983048 | tf_op jit(solution)/shard_map/ppermute | solution.py:539
  14.1 8.6 %collective-permute-start.4 = (bf16[12,8,128]{2,1,0:T(8,128)(2,1)S(1)}, bf16[12,8,128]{2,1,0:T(8,128)(2,1)S(1)}, u32[]{:S(2)}, u32[]{:S(2)}) collective-permute-start(bf16[12,8,128]{2,1,0:T(8,128)(2,1)S(1)} %get-tuple-element.31), channel_id=1, source_target_pairs={{0,8},{8,16},{16,24},{24,32},{32,40},{40,48},{48,56},{1,9},{9,17},... | collective-permute-start | bytes 73736 | tf_op jit(solution)/shard_map/ppermute | solution.py:557
  18.9 10.4 %collective-permute-start.5 = (bf16[14,8,128]{2,1,0:T(8,128)(2,1)S(1)}, bf16[14,8,128]{2,1,0:T(8,128)(2,1)S(1)}, u32[]{:S(2)}, u32[]{:S(2)}) collective-permute-start(bf16[14,8,128]{2,1,0:T(8,128)(2,1)S(1)} %get-tuple-element.32), channel_id=1, source_target_pairs={{8,0},{16,8},{24,16},{32,24},{40,32},{48,40},{56,48},{9,1},{17,9},... | collective-permute-start | bytes 86024 | tf_op jit(solution)/shard_map/ppermute | solution.py:558
  22.6 26.6 %copy-start = (bf16[3,3,3,128,128]{4,3,2,1,0:T(8,128)(2,1)}, bf16[3,3,3,128,128]{4,3,2,1,0:T(8,128)(2,1)S(1)}, u32[]{:S(2)}) copy-start(bf16[3,3,3,128,128]{4,3,2,1,0:T(8,128)(2,1)S(1)} %all_gather.3) | copy-start | bytes 2654212
  49.3 2.0 %collective-permute-start.6 = (bf16[32,64,128]{2,1,0:T(8,128)(2,1)S(1)}, bf16[32,64,128]{2,1,0:T(8,128)(2,1)S(1)}, u32[]{:S(2)}, u32[]{:S(2)}) collective-permute-start(bf16[32,64,128]{2,1,0:T(8,128)(2,1)S(1)} %get-tuple-element.35), channel_id=1, source_target_pairs={{0,64},{64,0},{1,65},{65,1},{2,66},{66,2},{3,67},{67,3},{4,68},{68... | collective-permute-start | bytes 1572872 | tf_op jit(solution)/shard_map/ppermute | solution.py:620
  52.2 22.6 %all-to-all-start = ((bf16[64,32,128]{2,1,0:T(8,128)(2,1)}), bf16[64,32,128]{2,1,0:T(8,128)(2,1)S(1)}, u32[]{:S(2)}, u32[]{:S(2)}) async-start(bf16[64,32,128]{2,1,0:T(8,128)(2,1)} %bitcast.6), calls=%async_computation | async-start | bytes 1048576 | tf_op jit(solution)/shard_map/all_to_all | solution.py:623
  75.8 17.1 %all-to-all-start.1 = ((bf16[64,32,128]{2,1,0:T(8,128)(2,1)}), bf16[64,32,128]{2,1,0:T(8,128)(2,1)S(1)}, u32[]{:S(2)}, u32[]{:S(2)}) async-start(bf16[64,32,128]{2,1,0:T(8,128)(2,1)} %broadcast_in_dim.17), calls=%async_computation.1 | async-start | bytes 1048576 | tf_op jit(solution)/shard_map/all_to_all | solution.py:627

commit v6 on v5

--- a/solution.py
+++ b/solution.py
@@ -14,7 +14,8 @@
 FIELD_LOW, FIELD_HIGH = 5, 6
 COT_LOW, COT_HIGH = 3, 4
 ROWS = 5
-PAIRS = 4
+PAIRS = 12
+CELL_PAIRS = 10
 CHUNKS = 4
 EDGE = 16
 LOW_ENDS, HIGH_ENDS = 2 * FIELD_LOW + 2, 2 * FIELD_HIGH + 2
@@ -276,10 +277,10 @@
         )
 
     def outer_strip(t, carry):
-        m = PAIRS * t
+        m = CELL_PAIRS * t
 
         def piece(ref, cells, every, row):
-            return ref[pl.ds(m + row // every, PAIRS), row % every, here, cells]
+            return ref[pl.ds(m + row // every, CELL_PAIRS), row % every, here, cells]
 
         every_lane, middle, first_lane = slice(None), slice(C, 2 * C), slice(0, C)
         outer(
@@ -299,7 +300,7 @@
         )
         return carry
 
-    lax.fori_loop(0, half_rows // (2 * PAIRS), outer_strip, 0)
+    lax.fori_loop(0, half_rows // (2 * CELL_PAIRS), outer_strip, 0)
 
     half = C // 2
     for tap in range(9):

time: 94.2 us -> 89.9 us (0.954)
  Pallas kernels: 32 us -> 27.8 us
    pallas_call x1, Pallas kernels: 20 us -> 15.7 us  [body(): pl.pallas_call(functools.partial(grads_kernel, half_rows, half_cols, lats...]
  transfers between devices with their start and end apart: 9 -> 9, of which waited for: 5 -> 5; matrix products, arithmetic and copies ran while one was open for 0% -> 0% of each run, Pallas kernels for 11% -> 12%
where the time goes in v6:
time: 89.9 us; the launch traced here: 89.5 us
  starting transfers between devices  29.8 us (33%)
  Pallas kernels  27.8 us (31%)
  waiting for transfers between devices  25.7 us (29%)
  blocking collectives  2.44 us (3%)
  local copies, waits for them, and re-layouts  1.84 us (2%)
  other arithmetic  1.13 us (1%)
    pallas_call x1, Pallas kernels, body(): pl.pallas_call(functools.partial(grads_kernel, half_rows, half_cols, lats...  15.7 us
    pallas_call x2, Pallas kernels, spread(): pl.pallas_call(functools.partial(up_kernel, above, kind, swapped), out_sh...  10.4 us
    all_to_all x1, starting transfers between devices, body(): pieces = lax.all_to_all(pieces, ('lat', 'lon'), 0, 0, tiled=True)  8.89 us
    all_to_all x1, waiting for transfers between devices, body(): pieces = lax.all_to_all(pieces, ('lat', 'lon'), 0, 0, tiled=True)  8.47 us
    all_to_all x1, waiting for transfers between devices, body(): lax.all_to_all(jnp.broadcast_to(piece, pieces.shape), ('lat', 'lon'), 0,...  7.09 us
    ppermute x1, waiting for transfers between devices, halos(): high_ends = lax.ppermute(down, 'lat', south)  6.61 us
    ppermute x1, starting transfers between devices, halos(): low = lax.ppermute(up, 'lat', north)  4.81 us
    ppermute x1, starting transfers between devices, halos(): low_ends = lax.ppermute(up, 'lat', north)  4.81 us
  transfers between devices with their start and end apart: 9, of which 5 were waited for; matrix products, arithmetic and copies ran while one was open for 0% of the time, Pallas kernels for 12%

profile of v6, /device:TPU:0, one launch (start us, length us, event | category | flops | bytes accessed | tf_op | source)
XLA Modules:
  0.0 89.5 jit_solution(18234362147868341649)
XLA Ops:
  0.6 0.0 copy-start.1
  0.6 0.0 copy-start.2
  0.7 0.0 copy-start.3
  0.7 1.5 %pack.1 = (bf16[80,8,128]{2,1,0:T(8,128)(2,1)S(1)}, bf16[100,8,128]{2,1,0:T(8,128)(2,1)S(1)}, bf16[8,128,128]{2,1,0:T(8,128)(2,1)S(1)}, bf16[10,128,128]{2,1,0:T(8,128)(2,1)S(1)}) custom-call(bf16[80,128,128]{2,1,0:T(8,128)(2,1)} %bitcast.19, bf16[80,128,128]{2,1,0:T(8,128)(2,1)} %bitcast.22), custom_call_target="tpu_custom_call" | custom-call | tf_op jit(solution)/shard_map/pack/pallas_call | solution.py:489
  2.2 3.9 %collective-permute-start.3 = (bf16[100,8,128]{2,1,0:T(8,128)(2,1)S(1)}, bf16[100,8,128]{2,1,0:T(8,128)(2,1)S(1)}, u32[]{:S(2)}, u32[]{:S(2)}) collective-permute-start(bf16[100,8,128]{2,1,0:T(8,128)(2,1)S(1)} %get-tuple-element.28), channel_id=1, source_target_pairs={{1,0},{2,1},{3,2},{4,3},{5,4},{6,5},{7,6},{0,7},{9,8},{10,9},{11,1... | collective-permute-start | bytes 614408 | tf_op jit(solution)/shard_map/ppermute | solution.py:538
  6.1 0.0 collective-permute-start.2
  6.1 4.8 %collective-permute-start = (bf16[8,128,128]{2,1,0:T(8,128)(2,1)S(1)}, bf16[8,128,128]{2,1,0:T(8,128)(2,1)S(1)}, u32[]{:S(2)}, u32[]{:S(2)}) collective-permute-start(bf16[8,128,128]{2,1,0:T(8,128)(2,1)S(1)} %get-tuple-element.25), channel_id=1, source_target_pairs={{0,8},{8,16},{16,24},{24,32},{32,40},{40,48},{48,56},{1,9},{9,17},... | collective-permute-start | bytes 786440 | tf_op jit(solution)/shard_map/ppermute | solution.py:539
  10.9 1.3 %collective-permute-start.1 = (bf16[10,128,128]{2,1,0:T(8,128)(2,1)S(1)}, bf16[10,128,128]{2,1,0:T(8,128)(2,1)S(1)}, u32[]{:S(2)}, u32[]{:S(2)}) collective-permute-start(bf16[10,128,128]{2,1,0:T(8,128)(2,1)S(1)} %get-tuple-element.26), channel_id=1, source_target_pairs={{8,0},{16,8},{24,16},{32,24},{40,32},{48,40},{56,48},{9,1},{17,9},... | collective-permute-start | bytes 983048 | tf_op jit(solution)/shard_map/ppermute | solution.py:540
  12.2 0.0 copy-done.1
  12.2 0.0 copy-done.2
  12.2 0.0 copy-done.3
  12.2 0.1 pad_maximum_fusion
  12.3 1.7 %collective-permute-done.2.refs_0_.west_hbm = bf16[80,8,128]{2,1,0:T(8,128)(2,1)S(1)} collective-permute-done((bf16[80,8,128]{2,1,0:T(8,128)(2,1)S(1)}, bf16[80,8,128]{2,1,0:T(8,128)(2,1)S(1)}, u32[]{:S(2)}, u32[]{:S(2)}) %collective-permute-start.2) | collective-permute-done | bytes 163872 | tf_op jit(solution)/shard_map/ppermute | solution.py:537
  14.0 0.0 collective-permute-done.3.refs_1_.east_hbm
  14.0 0.1 corners.1
  14.1 4.8 %collective-permute-start.4 = (bf16[12,8,128]{2,1,0:T(8,128)(2,1)S(1)}, bf16[12,8,128]{2,1,0:T(8,128)(2,1)S(1)}, u32[]{:S(2)}, u32[]{:S(2)}) collective-permute-start(bf16[12,8,128]{2,1,0:T(8,128)(2,1)S(1)} %get-tuple-element.31), channel_id=1, source_target_pairs={{0,8},{8,16},{16,24},{24,32},{32,40},{40,48},{48,56},{1,9},{9,17},... | collective-permute-start | bytes 73736 | tf_op jit(solution)/shard_map/ppermute | solution.py:558
  18.9 1.3 %collective-permute-start.5 = (bf16[14,8,128]{2,1,0:T(8,128)(2,1)S(1)}, bf16[14,8,128]{2,1,0:T(8,128)(2,1)S(1)}, u32[]{:S(2)}, u32[]{:S(2)}) collective-permute-start(bf16[14,8,128]{2,1,0:T(8,128)(2,1)S(1)} %get-tuple-element.32), channel_id=1, source_target_pairs={{8,0},{16,8},{24,16},{32,24},{40,32},{48,40},{56,48},{9,1},{17,9},... | collective-permute-start | bytes 86024 | tf_op jit(solution)/shard_map/ppermute | solution.py:559
  20.2 2.4 %all_gather.3 = bf16[3,3,3,128,128]{4,3,2,1,0:T(8,128)(2,1)S(1)} all-gather(bf16[3,3,3,64,128]{4,3,2,1,0:T(8,128)(2,1)S(1)} %pad_maximum_fusion), channel_id=1, replica_groups=mesh['dp'=2,'lat'=8,'lon'=8] {'dp'}, dimensions={3}, use_global_device_ids=true | all-gather | bytes 1327104 | tf_op jit(solution)/shard_map/all_gather | solution.py:560
  22.6 0.0 copy-start
  22.6 0.0 collective-permute-done.4.low_ends_hbm
  22.6 6.6 %collective-permute-done.5.high_ends_hbm = bf16[14,8,128]{2,1,0:T(8,128)(2,1)S(1)} collective-permute-done((bf16[14,8,128]{2,1,0:T(8,128)(2,1)S(1)}, bf16[14,8,128]{2,1,0:T(8,128)(2,1)S(1)}, u32[]{:S(2)}, u32[]{:S(2)}) %collective-permute-start.5) | collective-permute-done | bytes 28704 | tf_op jit(solution)/shard_map/ppermute | solution.py:559
  29.3 0.0 collective-permute-done.low_hbm
  29.3 0.0 collective-permute-done.1.high_hbm
  29.3 15.7 %grads.1 = (f32[32,64,128]{2,1,0:T(8,128)S(1)}, bf16[32,64,128]{2,1,0:T(8,128)(2,1)S(1)}, bf16[23,2,64,256]{3,2,1,0:T(8,128)(2,1)}, bf16[23,2,64,256]{3,2,1,0:T(8,128)(2,1)}) custom-call(bf16[80,128,128]{2,1,0:T(8,128)(2,1)} %bitcast.20, bf16[80,128,128]{2,1,0:T(8,128)(2,1)} %bitcast.23, bf16[8,128,128]{2,1,0:T(8,128)(2,1)S(1)} %collective-permute-done.low_hbm, ...), custom_call_target="tpu_custom_call" | custom-call | flops 5872025600 | bytes 8388608 | tf_op jit(solution)/shard_map/grads/pallas_call | solution.py:579
  45.0 0.0 copy-done
  45.0 0.1 collective-permute-start.6
  45.1 1.9 %collective-permute-done.6 = bf16[32,64,128]{2,1,0:T(8,128)(2,1)S(1)} collective-permute-done((bf16[32,64,128]{2,1,0:T(8,128)(2,1)S(1)}, bf16[32,64,128]{2,1,0:T(8,128)(2,1)S(1)}, u32[]{:S(2)}, u32[]{:S(2)}) %collective-permute-start.6) | collective-permute-done | bytes 524320 | tf_op jit(solution)/shard_map/ppermute | solution.py:621
  47.0 1.0 %add_convert_fusion = bf16[32,64,128]{2,1,0:T(8,128)(2,1)} fusion(f32[32,64,128]{2,1,0:T(8,128)S(1)} %get-tuple-element.34, bf16[32,64,128]{2,1,0:T(8,128)(2,1)S(1)} %collective-permute-done.6), kind=kLoop, calls=%fused_computation | loop fusion | flops 786432 | bytes 2097152 | tf_op jit(solution)/shard_map/convert_element_type | solution.py:622
  48.0 8.9 %all-to-all-start = ((bf16[64,32,128]{2,1,0:T(8,128)(2,1)}), bf16[64,32,128]{2,1,0:T(8,128)(2,1)S(1)}, u32[]{:S(2)}, u32[]{:S(2)}) async-start(bf16[64,32,128]{2,1,0:T(8,128)(2,1)} %bitcast.6), calls=%async_computation | async-start | bytes 1048576 | tf_op jit(solution)/shard_map/all_to_all | solution.py:624
  56.9 5.2 %level.1 = bf16[80,128,128]{2,1,0:T(8,128)(2,1)} custom-call(bf16[46,64,256]{2,1,0:T(8,128)(2,1)} %bitcast.28, bf16[80,128,128]{2,1,0:T(8,128)(2,1)} %bitcast.21, bf16[3,1152,128]{2,1,0:T(8,128)(2,1)} %bitcast.17), custom_call_target="tpu_custom_call" | custom-call | flops 754974720 | bytes 7340032 | tf_op jit(solution)/shard_map/level/pallas_call | solution.py:401
  62.1 8.5 %all-to-all-done = bf16[64,32,128]{2,1,0:T(8,128)(2,1)S(1)} async-done(((bf16[64,32,128]{2,1,0:T(8,128)(2,1)}), bf16[64,32,128]{2,1,0:T(8,128)(2,1)S(1)}, u32[]{:S(2)}, u32[]{:S(2)}) %all-to-all-start) | async-done | bytes 524320 | tf_op jit(solution)/shard_map/all_to_all | solution.py:624
  70.5 0.1 reduce_sum.12
  70.6 0.9 broadcast_in_dim.17
  71.5 4.7 %all-to-all-start.1 = ((bf16[64,32,128]{2,1,0:T(8,128)(2,1)}), bf16[64,32,128]{2,1,0:T(8,128)(2,1)S(1)}, u32[]{:S(2)}, u32[]{:S(2)}) async-start(bf16[64,32,128]{2,1,0:T(8,128)(2,1)} %broadcast_in_dim.17), calls=%async_computation.1 | async-start | bytes 1048576 | tf_op jit(solution)/shard_map/all_to_all | solution.py:628
  76.3 5.2 %gradient.1 = bf16[80,128,128]{2,1,0:T(8,128)(2,1)} custom-call(bf16[46,64,256]{2,1,0:T(8,128)(2,1)} %bitcast.27, bf16[80,128,128]{2,1,0:T(8,128)(2,1)} %bitcast.24, bf16[3,1152,128]{2,1,0:T(8,128)(2,1)} %bitcast.18), custom_call_target="tpu_custom_call" | custom-call | flops 754974720 | bytes 7340032 | tf_op jit(solution)/shard_map/gradient/pallas_call | solution.py:401
  81.5 7.1 %all-to-all-done.1 = bf16[64,32,128]{2,1,0:T(8,128)(2,1)S(1)} async-done(((bf16[64,32,128]{2,1,0:T(8,128)(2,1)}), bf16[64,32,128]{2,1,0:T(8,128)(2,1)S(1)}, u32[]{:S(2)}, u32[]{:S(2)}) %all-to-all-start.1) | async-done | bytes 524320 | tf_op jit(solution)/shard_map/all_to_all | solution.py:628
  88.6 0.9 %fusion = (f32[18,32,128]{2,1,0:T(8,128)}, f32[18,32,128]{2,1,0:T(8,128)}, f32[18,32,128]{2,1,0:T(8,128)}) fusion(bf16[64,32,128]{2,1,0:T(8,128)(2,1)S(1)} %all-to-all-done.1), kind=kLoop, calls=%fused_computation.2 | loop fusion | bytes 1769472 | tf_op jit(solution)/shard_map/slice | solution.py:635
  (1 shorter events, 0.0 us)
Async XLA Ops:
  0.6 11.6 %copy-start.1 = (bf16[3,3,64,128]{3,2,1,0:T(8,128)(2,1)S(1)}, bf16[3,3,64,128]{3,2,1,0:T(8,128)(2,1)}, u32[]{:S(2)}) copy-start(bf16[3,3,64,128]{3,2,1,0:T(8,128)(2,1)} %param.8) | copy-start | bytes 442372
  0.6 11.6 %copy-start.2 = (bf16[3,3,64,128]{3,2,1,0:T(8,128)(2,1)S(1)}, bf16[3,3,64,128]{3,2,1,0:T(8,128)(2,1)}, u32[]{:S(2)}) copy-start(bf16[3,3,64,128]{3,2,1,0:T(8,128)(2,1)} %param.7) | copy-start | bytes 442372
  0.7 11.6 %copy-start.3 = (bf16[3,3,64,128]{3,2,1,0:T(8,128)(2,1)S(1)}, bf16[3,3,64,128]{3,2,1,0:T(8,128)(2,1)}, u32[]{:S(2)}) copy-start(bf16[3,3,64,128]{3,2,1,0:T(8,128)(2,1)} %param.6) | copy-start | bytes 442372
  2.2 11.8 %collective-permute-start.3 = (bf16[100,8,128]{2,1,0:T(8,128)(2,1)S(1)}, bf16[100,8,128]{2,1,0:T(8,128)(2,1)S(1)}, u32[]{:S(2)}, u32[]{:S(2)}) collective-permute-start(bf16[100,8,128]{2,1,0:T(8,128)(2,1)S(1)} %get-tuple-element.28), channel_id=1, source_target_pairs={{1,0},{2,1},{3,2},{4,3},{5,4},{6,5},{7,6},{0,7},{9,8},{10,9},{11,1... | collective-permute-start | bytes 614408 | tf_op jit(solution)/shard_map/ppermute | solution.py:538
  6.1 7.9 %collective-permute-start.2 = (bf16[80,8,128]{2,1,0:T(8,128)(2,1)S(1)}, bf16[80,8,128]{2,1,0:T(8,128)(2,1)S(1)}, u32[]{:S(2)}, u32[]{:S(2)}) collective-permute-start(bf16[80,8,128]{2,1,0:T(8,128)(2,1)S(1)} %get-tuple-element.27), channel_id=1, source_target_pairs={{0,1},{1,2},{2,3},{3,4},{4,5},{5,6},{6,7},{7,0},{8,9},{9,10},{10,1... | collective-permute-start | bytes 491528 | tf_op jit(solution)/shard_map/ppermute | solution.py:537
  6.1 23.2 %collective-permute-start = (bf16[8,128,128]{2,1,0:T(8,128)(2,1)S(1)}, bf16[8,128,128]{2,1,0:T(8,128)(2,1)S(1)}, u32[]{:S(2)}, u32[]{:S(2)}) collective-permute-start(bf16[8,128,128]{2,1,0:T(8,128)(2,1)S(1)} %get-tuple-element.25), channel_id=1, source_target_pairs={{0,8},{8,16},{16,24},{24,32},{32,40},{40,48},{48,56},{1,9},{9,17},... | collective-permute-start | bytes 786440 | tf_op jit(solution)/shard_map/ppermute | solution.py:539
  10.9 18.4 %collective-permute-start.1 = (bf16[10,128,128]{2,1,0:T(8,128)(2,1)S(1)}, bf16[10,128,128]{2,1,0:T(8,128)(2,1)S(1)}, u32[]{:S(2)}, u32[]{:S(2)}) collective-permute-start(bf16[10,128,128]{2,1,0:T(8,128)(2,1)S(1)} %get-tuple-element.26), channel_id=1, source_target_pairs={{8,0},{16,8},{24,16},{32,24},{40,32},{48,40},{56,48},{9,1},{17,9},... | collective-permute-start | bytes 983048 | tf_op jit(solution)/shard_map/ppermute | solution.py:540
  14.1 8.6 %collective-permute-start.4 = (bf16[12,8,128]{2,1,0:T(8,128)(2,1)S(1)}, bf16[12,8,128]{2,1,0:T(8,128)(2,1)S(1)}, u32[]{:S(2)}, u32[]{:S(2)}) collective-permute-start(bf16[12,8,128]{2,1,0:T(8,128)(2,1)S(1)} %get-tuple-element.31), channel_id=1, source_target_pairs={{0,8},{8,16},{16,24},{24,32},{32,40},{40,48},{48,56},{1,9},{9,17},... | collective-permute-start | bytes 73736 | tf_op jit(solution)/shard_map/ppermute | solution.py:558
  18.9 10.4 %collective-permute-start.5 = (bf16[14,8,128]{2,1,0:T(8,128)(2,1)S(1)}, bf16[14,8,128]{2,1,0:T(8,128)(2,1)S(1)}, u32[]{:S(2)}, u32[]{:S(2)}) collective-permute-start(bf16[14,8,128]{2,1,0:T(8,128)(2,1)S(1)} %get-tuple-element.32), channel_id=1, source_target_pairs={{8,0},{16,8},{24,16},{32,24},{40,32},{48,40},{56,48},{9,1},{17,9},... | collective-permute-start | bytes 86024 | tf_op jit(solution)/shard_map/ppermute | solution.py:559
  22.6 22.4 %copy-start = (bf16[3,3,3,128,128]{4,3,2,1,0:T(8,128)(2,1)}, bf16[3,3,3,128,128]{4,3,2,1,0:T(8,128)(2,1)S(1)}, u32[]{:S(2)}) copy-start(bf16[3,3,3,128,128]{4,3,2,1,0:T(8,128)(2,1)S(1)} %all_gather.3) | copy-start | bytes 2654212
  45.0 2.0 %collective-permute-start.6 = (bf16[32,64,128]{2,1,0:T(8,128)(2,1)S(1)}, bf16[32,64,128]{2,1,0:T(8,128)(2,1)S(1)}, u32[]{:S(2)}, u32[]{:S(2)}) collective-permute-start(bf16[32,64,128]{2,1,0:T(8,128)(2,1)S(1)} %get-tuple-element.35), channel_id=1, source_target_pairs={{0,64},{64,0},{1,65},{65,1},{2,66},{66,2},{3,67},{67,3},{4,68},{68... | collective-permute-start | bytes 1572872 | tf_op jit(solution)/shard_map/ppermute | solution.py:621
  48.0 22.6 %all-to-all-start = ((bf16[64,32,128]{2,1,0:T(8,128)(2,1)}), bf16[64,32,128]{2,1,0:T(8,128)(2,1)S(1)}, u32[]{:S(2)}, u32[]{:S(2)}) async-start(bf16[64,32,128]{2,1,0:T(8,128)(2,1)} %bitcast.6), calls=%async_computation | async-start | bytes 1048576 | tf_op jit(solution)/shard_map/all_to_all | solution.py:624
  71.5 17.1 %all-to-all-start.1 = ((bf16[64,32,128]{2,1,0:T(8,128)(2,1)}), bf16[64,32,128]{2,1,0:T(8,128)(2,1)S(1)}, u32[]{:S(2)}, u32[]{:S(2)}) async-start(bf16[64,32,128]{2,1,0:T(8,128)(2,1)} %broadcast_in_dim.17), calls=%async_computation.1 | async-start | bytes 1048576 | tf_op jit(solution)/shard_map/all_to_all | solution.py:628

commit v7 on v6

--- a/solution.py
+++ b/solution.py
@@ -622,13 +622,12 @@
     both = (own + came.astype(F32)).astype(BF16)
     pieces = both.reshape(lats * lons, -1, C)
     pieces = lax.all_to_all(pieces, ("lat", "lon"), 0, 0, tiled=True)
-    level_out = spread("level", 1, 2, False, mid_pairs, fields, weights)
     piece = jnp.sum(pieces.astype(F32), axis=0, keepdims=True).astype(BF16)
-    piece, level_out = lax.optimization_barrier((piece, level_out))
     totals = lax.all_to_all(
         jnp.broadcast_to(piece, pieces.shape), ("lat", "lon"), 0, 0, tiled=True
     )
-    _, grad_pairs = lax.optimization_barrier((piece, grad_pairs))
+    _, mid_pairs, grad_pairs = lax.optimization_barrier((piece, mid_pairs, grad_pairs))
+    level_out = spread("level", 1, 2, False, mid_pairs, fields, weights)
     grad_fields = spread("gradient", 0, 0, True, grad_pairs, cotangent, weights)
     totals = totals.reshape(TAPS, C // 2, C).astype(F32)
     grad_down, grad_mid, grad_up = (

time: 89.9 us -> 88.8 us (0.988)
  blocking collectives: 2.44 us -> 24.8 us
  waiting for transfers between devices: 25.7 us -> 12.1 us
  starting transfers between devices: 29.8 us -> 20.9 us
    all_to_all x0 -> x1, blocking collectives: none -> 22.3 us  [body(): pieces = lax.all_to_all(pieces, ('lat', 'lon'), 0, 0, tiled=True)]
    all_to_all x1 -> x0, starting transfers between devices: 8.89 us -> none  [body(): pieces = lax.all_to_all(pieces, ('lat', 'lon'), 0, 0, tiled=True)]
    all_to_all x1 -> x0, waiting for transfers between devices: 8.47 us -> none  [body(): pieces = lax.all_to_all(pieces, ('lat', 'lon'), 0, 0, tiled=True)]
    all_to_all x1, waiting for transfers between devices: 7.09 us -> 1.9 us  [body(): lax.all_to_all(jnp.broadcast_to(piece, pieces.shape), ('lat', 'lon'), 0,...]
  transfers between devices with their start and end apart: 9 -> 8, of which waited for: 5 -> 4; matrix products, arithmetic and copies ran while one was open for 0% -> 0% of each run, Pallas kernels for 12% -> 12%
where the time goes in v7:
time: 88.8 us; the launch traced here: 88.5 us
  Pallas kernels  27.8 us (31%)
  blocking collectives  24.8 us (28%)
  starting transfers between devices  20.9 us (24%)
  waiting for transfers between devices  12.1 us (14%)
  local copies, waits for them, and re-layouts  1.83 us (2%)
    all_to_all x1, blocking collectives, body(): pieces = lax.all_to_all(pieces, ('lat', 'lon'), 0, 0, tiled=True)  22.3 us
    pallas_call x1, Pallas kernels, body(): pl.pallas_call(functools.partial(grads_kernel, half_rows, half_cols, lats...  15.7 us
    pallas_call x2, Pallas kernels, spread(): pl.pallas_call(functools.partial(up_kernel, above, kind, swapped), out_sh...  10.4 us
    ppermute x1, waiting for transfers between devices, halos(): high_ends = lax.ppermute(down, 'lat', south)  6.61 us
    ppermute x1, starting transfers between devices, halos(): low = lax.ppermute(up, 'lat', north)  4.81 us
    ppermute x1, starting transfers between devices, halos(): low_ends = lax.ppermute(up, 'lat', north)  4.81 us
    all_to_all x1, starting transfers between devices, body(): lax.all_to_all(jnp.broadcast_to(piece, pieces.shape), ('lat', 'lon'), 0,...  4.73 us
    ppermute x1, starting transfers between devices, halos(): from_east = lax.ppermute(west, 'lon', westward)  3.92 us
  transfers between devices with their start and end apart: 8, of which 4 were waited for; matrix products, arithmetic and copies ran while one was open for 0% of the time, Pallas kernels for 12%

profile of v7, /device:TPU:0, one launch (start us, length us, event | category | flops | bytes accessed | tf_op | source)
XLA Modules:
  0.0 88.5 jit_solution(11042358193513064154)
XLA Ops:
  0.6 0.0 copy-start.1
  0.6 0.0 copy-start.2
  0.7 0.0 copy-start.3
  0.7 1.5 %pack.1 = (bf16[80,8,128]{2,1,0:T(8,128)(2,1)S(1)}, bf16[100,8,128]{2,1,0:T(8,128)(2,1)S(1)}, bf16[8,128,128]{2,1,0:T(8,128)(2,1)S(1)}, bf16[10,128,128]{2,1,0:T(8,128)(2,1)S(1)}) custom-call(bf16[80,128,128]{2,1,0:T(8,128)(2,1)} %bitcast.17, bf16[80,128,128]{2,1,0:T(8,128)(2,1)} %bitcast.20), custom_call_target="tpu_custom_call" | custom-call | tf_op jit(solution)/shard_map/pack/pallas_call | solution.py:489
  2.2 3.9 %collective-permute-start.3 = (bf16[100,8,128]{2,1,0:T(8,128)(2,1)S(1)}, bf16[100,8,128]{2,1,0:T(8,128)(2,1)S(1)}, u32[]{:S(2)}, u32[]{:S(2)}) collective-permute-start(bf16[100,8,128]{2,1,0:T(8,128)(2,1)S(1)} %get-tuple-element.27), channel_id=1, source_target_pairs={{1,0},{2,1},{3,2},{4,3},{5,4},{6,5},{7,6},{0,7},{9,8},{10,9},{11,1... | collective-permute-start | bytes 614408 | tf_op jit(solution)/shard_map/ppermute | solution.py:538
  6.1 0.0 collective-permute-start.2
  6.1 4.8 %collective-permute-start = (bf16[8,128,128]{2,1,0:T(8,128)(2,1)S(1)}, bf16[8,128,128]{2,1,0:T(8,128)(2,1)S(1)}, u32[]{:S(2)}, u32[]{:S(2)}) collective-permute-start(bf16[8,128,128]{2,1,0:T(8,128)(2,1)S(1)} %get-tuple-element.24), channel_id=1, source_target_pairs={{0,8},{8,16},{16,24},{24,32},{32,40},{40,48},{48,56},{1,9},{9,17},... | collective-permute-start | bytes 786440 | tf_op jit(solution)/shard_map/ppermute | solution.py:539
  10.9 1.3 %collective-permute-start.1 = (bf16[10,128,128]{2,1,0:T(8,128)(2,1)S(1)}, bf16[10,128,128]{2,1,0:T(8,128)(2,1)S(1)}, u32[]{:S(2)}, u32[]{:S(2)}) collective-permute-start(bf16[10,128,128]{2,1,0:T(8,128)(2,1)S(1)} %get-tuple-element.25), channel_id=1, source_target_pairs={{8,0},{16,8},{24,16},{32,24},{40,32},{48,40},{56,48},{9,1},{17,9},... | collective-permute-start | bytes 983048 | tf_op jit(solution)/shard_map/ppermute | solution.py:540
  12.2 0.0 copy-done.1
  12.2 0.0 copy-done.2
  12.2 0.0 copy-done.3
  12.2 0.1 pad_maximum_fusion
  12.3 1.7 %collective-permute-done.2.refs_0_.west_hbm = bf16[80,8,128]{2,1,0:T(8,128)(2,1)S(1)} collective-permute-done((bf16[80,8,128]{2,1,0:T(8,128)(2,1)S(1)}, bf16[80,8,128]{2,1,0:T(8,128)(2,1)S(1)}, u32[]{:S(2)}, u32[]{:S(2)}) %collective-permute-start.2) | collective-permute-done | bytes 163872 | tf_op jit(solution)/shard_map/ppermute | solution.py:537
  14.0 0.0 collective-permute-done.3.refs_1_.east_hbm
  14.0 0.1 corners.1
  14.1 4.8 %collective-permute-start.4 = (bf16[12,8,128]{2,1,0:T(8,128)(2,1)S(1)}, bf16[12,8,128]{2,1,0:T(8,128)(2,1)S(1)}, u32[]{:S(2)}, u32[]{:S(2)}) collective-permute-start(bf16[12,8,128]{2,1,0:T(8,128)(2,1)S(1)} %get-tuple-element.30), channel_id=1, source_target_pairs={{0,8},{8,16},{16,24},{24,32},{32,40},{40,48},{48,56},{1,9},{9,17},... | collective-permute-start | bytes 73736 | tf_op jit(solution)/shard_map/ppermute | solution.py:558
  18.9 1.3 %collective-permute-start.5 = (bf16[14,8,128]{2,1,0:T(8,128)(2,1)S(1)}, bf16[14,8,128]{2,1,0:T(8,128)(2,1)S(1)}, u32[]{:S(2)}, u32[]{:S(2)}) collective-permute-start(bf16[14,8,128]{2,1,0:T(8,128)(2,1)S(1)} %get-tuple-element.31), channel_id=1, source_target_pairs={{8,0},{16,8},{24,16},{32,24},{40,32},{48,40},{56,48},{9,1},{17,9},... | collective-permute-start | bytes 86024 | tf_op jit(solution)/shard_map/ppermute | solution.py:559
  20.2 2.4 %all_gather.3 = bf16[3,3,3,128,128]{4,3,2,1,0:T(8,128)(2,1)S(1)} all-gather(bf16[3,3,3,64,128]{4,3,2,1,0:T(8,128)(2,1)S(1)} %pad_maximum_fusion), channel_id=1, replica_groups=mesh['dp'=2,'lat'=8,'lon'=8] {'dp'}, dimensions={3}, use_global_device_ids=true | all-gather | bytes 1327104 | tf_op jit(solution)/shard_map/all_gather | solution.py:560
  22.6 0.0 copy-start
  22.6 0.0 collective-permute-done.4.low_ends_hbm
  22.6 6.6 %collective-permute-done.5.high_ends_hbm = bf16[14,8,128]{2,1,0:T(8,128)(2,1)S(1)} collective-permute-done((bf16[14,8,128]{2,1,0:T(8,128)(2,1)S(1)}, bf16[14,8,128]{2,1,0:T(8,128)(2,1)S(1)}, u32[]{:S(2)}, u32[]{:S(2)}) %collective-permute-start.5) | collective-permute-done | bytes 28704 | tf_op jit(solution)/shard_map/ppermute | solution.py:559
  29.3 0.0 collective-permute-done.low_hbm
  29.3 0.0 collective-permute-done.1.high_hbm
  29.3 15.7 %grads.1 = (f32[32,64,128]{2,1,0:T(8,128)S(1)}, bf16[32,64,128]{2,1,0:T(8,128)(2,1)S(1)}, bf16[23,2,64,256]{3,2,1,0:T(8,128)(2,1)}, bf16[23,2,64,256]{3,2,1,0:T(8,128)(2,1)}) custom-call(bf16[80,128,128]{2,1,0:T(8,128)(2,1)} %bitcast.18, bf16[80,128,128]{2,1,0:T(8,128)(2,1)} %bitcast.21, bf16[8,128,128]{2,1,0:T(8,128)(2,1)S(1)} %collective-permute-done.low_hbm, ...), custom_call_target="tpu_custom_call" | custom-call | flops 5872025600 | bytes 8388608 | tf_op jit(solution)/shard_map/grads/pallas_call | solution.py:579
  45.0 0.0 copy-done
  45.0 0.1 collective-permute-start.6
  45.1 1.9 %collective-permute-done.6 = bf16[32,64,128]{2,1,0:T(8,128)(2,1)S(1)} collective-permute-done((bf16[32,64,128]{2,1,0:T(8,128)(2,1)S(1)}, bf16[32,64,128]{2,1,0:T(8,128)(2,1)S(1)}, u32[]{:S(2)}, u32[]{:S(2)}) %collective-permute-start.6) | collective-permute-done | bytes 524320 | tf_op jit(solution)/shard_map/ppermute | solution.py:621
  47.0 0.2 add_convert_fusion
  47.2 22.3 %all_to_all.10 = bf16[64,32,128]{2,1,0:T(8,128)(2,1)S(1)} all-to-all(bf16[64,32,128]{2,1,0:T(8,128)(2,1)S(1)} %bitcast.25), channel_id=1, replica_groups=mesh['dp'=2,'lat'=8,'lon'=8] {'lat','lon'}, dimensions={0} | all-to-all | bytes 1048576 | tf_op jit(solution)/shard_map/all_to_all | solution.py:624
  69.5 0.1 reduce_sum.12
  69.6 0.9 broadcast_in_dim.14
  70.5 4.7 %all-to-all-start.1 = ((bf16[64,32,128]{2,1,0:T(8,128)(2,1)}), bf16[64,32,128]{2,1,0:T(8,128)(2,1)S(1)}, u32[]{:S(2)}, u32[]{:S(2)}) async-start(bf16[64,32,128]{2,1,0:T(8,128)(2,1)} %broadcast_in_dim.14), calls=%async_computation.1 | async-start | bytes 1048576 | tf_op jit(solution)/shard_map/all_to_all | solution.py:626
  75.2 5.2 %level.1 = bf16[80,128,128]{2,1,0:T(8,128)(2,1)} custom-call(bf16[46,64,256]{2,1,0:T(8,128)(2,1)} %bitcast.27, bf16[80,128,128]{2,1,0:T(8,128)(2,1)} %bitcast.19, bf16[3,1152,128]{2,1,0:T(8,128)(2,1)} %bitcast.15), custom_call_target="tpu_custom_call" | custom-call | flops 754974720 | bytes 7340032 | tf_op jit(solution)/shard_map/level/pallas_call | solution.py:401
  80.4 5.2 %gradient.1 = bf16[80,128,128]{2,1,0:T(8,128)(2,1)} custom-call(bf16[46,64,256]{2,1,0:T(8,128)(2,1)} %bitcast.26, bf16[80,128,128]{2,1,0:T(8,128)(2,1)} %bitcast.22, bf16[3,1152,128]{2,1,0:T(8,128)(2,1)} %bitcast.16), custom_call_target="tpu_custom_call" | custom-call | flops 754974720 | bytes 7340032 | tf_op jit(solution)/shard_map/gradient/pallas_call | solution.py:401
  85.7 1.9 %all-to-all-done.1 = bf16[64,32,128]{2,1,0:T(8,128)(2,1)S(1)} async-done(((bf16[64,32,128]{2,1,0:T(8,128)(2,1)}), bf16[64,32,128]{2,1,0:T(8,128)(2,1)S(1)}, u32[]{:S(2)}, u32[]{:S(2)}) %all-to-all-start.1) | async-done | bytes 524320 | tf_op jit(solution)/shard_map/all_to_all | solution.py:626
  87.6 0.9 %fusion = (f32[18,32,128]{2,1,0:T(8,128)}, f32[18,32,128]{2,1,0:T(8,128)}, f32[18,32,128]{2,1,0:T(8,128)}) fusion(bf16[64,32,128]{2,1,0:T(8,128)(2,1)S(1)} %all-to-all-done.1), kind=kLoop, calls=%fused_computation.2 | loop fusion | bytes 1769472 | tf_op jit(solution)/shard_map/slice | solution.py:634
  (1 shorter events, 0.0 us)
Async XLA Ops:
  0.6 11.6 %copy-start.1 = (bf16[3,3,64,128]{3,2,1,0:T(8,128)(2,1)S(1)}, bf16[3,3,64,128]{3,2,1,0:T(8,128)(2,1)}, u32[]{:S(2)}) copy-start(bf16[3,3,64,128]{3,2,1,0:T(8,128)(2,1)} %param.8) | copy-start | bytes 442372
  0.6 11.6 %copy-start.2 = (bf16[3,3,64,128]{3,2,1,0:T(8,128)(2,1)S(1)}, bf16[3,3,64,128]{3,2,1,0:T(8,128)(2,1)}, u32[]{:S(2)}) copy-start(bf16[3,3,64,128]{3,2,1,0:T(8,128)(2,1)} %param.7) | copy-start | bytes 442372
  0.7 11.6 %copy-start.3 = (bf16[3,3,64,128]{3,2,1,0:T(8,128)(2,1)S(1)}, bf16[3,3,64,128]{3,2,1,0:T(8,128)(2,1)}, u32[]{:S(2)}) copy-start(bf16[3,3,64,128]{3,2,1,0:T(8,128)(2,1)} %param.6) | copy-start | bytes 442372
  2.2 11.8 %collective-permute-start.3 = (bf16[100,8,128]{2,1,0:T(8,128)(2,1)S(1)}, bf16[100,8,128]{2,1,0:T(8,128)(2,1)S(1)}, u32[]{:S(2)}, u32[]{:S(2)}) collective-permute-start(bf16[100,8,128]{2,1,0:T(8,128)(2,1)S(1)} %get-tuple-element.27), channel_id=1, source_target_pairs={{1,0},{2,1},{3,2},{4,3},{5,4},{6,5},{7,6},{0,7},{9,8},{10,9},{11,1... | collective-permute-start | bytes 614408 | tf_op jit(solution)/shard_map/ppermute | solution.py:538
  6.1 7.9 %collective-permute-start.2 = (bf16[80,8,128]{2,1,0:T(8,128)(2,1)S(1)}, bf16[80,8,128]{2,1,0:T(8,128)(2,1)S(1)}, u32[]{:S(2)}, u32[]{:S(2)}) collective-permute-start(bf16[80,8,128]{2,1,0:T(8,128)(2,1)S(1)} %get-tuple-element.26), channel_id=1, source_target_pairs={{0,1},{1,2},{2,3},{3,4},{4,5},{5,6},{6,7},{7,0},{8,9},{9,10},{10,1... | collective-permute-start | bytes 491528 | tf_op jit(solution)/shard_map/ppermute | solution.py:537
  6.1 23.2 %collective-permute-start = (bf16[8,128,128]{2,1,0:T(8,128)(2,1)S(1)}, bf16[8,128,128]{2,1,0:T(8,128)(2,1)S(1)}, u32[]{:S(2)}, u32[]{:S(2)}) collective-permute-start(bf16[8,128,128]{2,1,0:T(8,128)(2,1)S(1)} %get-tuple-element.24), channel_id=1, source_target_pairs={{0,8},{8,16},{16,24},{24,32},{32,40},{40,48},{48,56},{1,9},{9,17},... | collective-permute-start | bytes 786440 | tf_op jit(solution)/shard_map/ppermute | solution.py:539
  10.9 18.4 %collective-permute-start.1 = (bf16[10,128,128]{2,1,0:T(8,128)(2,1)S(1)}, bf16[10,128,128]{2,1,0:T(8,128)(2,1)S(1)}, u32[]{:S(2)}, u32[]{:S(2)}) collective-permute-start(bf16[10,128,128]{2,1,0:T(8,128)(2,1)S(1)} %get-tuple-element.25), channel_id=1, source_target_pairs={{8,0},{16,8},{24,16},{32,24},{40,32},{48,40},{56,48},{9,1},{17,9},... | collective-permute-start | bytes 983048 | tf_op jit(solution)/shard_map/ppermute | solution.py:540
  14.1 8.6 %collective-permute-start.4 = (bf16[12,8,128]{2,1,0:T(8,128)(2,1)S(1)}, bf16[12,8,128]{2,1,0:T(8,128)(2,1)S(1)}, u32[]{:S(2)}, u32[]{:S(2)}) collective-permute-start(bf16[12,8,128]{2,1,0:T(8,128)(2,1)S(1)} %get-tuple-element.30), channel_id=1, source_target_pairs={{0,8},{8,16},{16,24},{24,32},{32,40},{40,48},{48,56},{1,9},{9,17},... | collective-permute-start | bytes 73736 | tf_op jit(solution)/shard_map/ppermute | solution.py:558
  18.9 10.4 %collective-permute-start.5 = (bf16[14,8,128]{2,1,0:T(8,128)(2,1)S(1)}, bf16[14,8,128]{2,1,0:T(8,128)(2,1)S(1)}, u32[]{:S(2)}, u32[]{:S(2)}) collective-permute-start(bf16[14,8,128]{2,1,0:T(8,128)(2,1)S(1)} %get-tuple-element.31), channel_id=1, source_target_pairs={{8,0},{16,8},{24,16},{32,24},{40,32},{48,40},{56,48},{9,1},{17,9},... | collective-permute-start | bytes 86024 | tf_op jit(solution)/shard_map/ppermute | solution.py:559
  22.6 22.4 %copy-start = (bf16[3,3,3,128,128]{4,3,2,1,0:T(8,128)(2,1)}, bf16[3,3,3,128,128]{4,3,2,1,0:T(8,128)(2,1)S(1)}, u32[]{:S(2)}) copy-start(bf16[3,3,3,128,128]{4,3,2,1,0:T(8,128)(2,1)S(1)} %all_gather.3) | copy-start | bytes 2654212
  45.0 2.0 %collective-permute-start.6 = (bf16[32,64,128]{2,1,0:T(8,128)(2,1)S(1)}, bf16[32,64,128]{2,1,0:T(8,128)(2,1)S(1)}, u32[]{:S(2)}, u32[]{:S(2)}) collective-permute-start(bf16[32,64,128]{2,1,0:T(8,128)(2,1)S(1)} %get-tuple-element.38), channel_id=1, source_target_pairs={{0,64},{64,0},{1,65},{65,1},{2,66},{66,2},{3,67},{67,3},{4,68},{68... | collective-permute-start | bytes 1572872 | tf_op jit(solution)/shard_map/ppermute | solution.py:621
  70.5 17.1 %all-to-all-start.1 = ((bf16[64,32,128]{2,1,0:T(8,128)(2,1)}), bf16[64,32,128]{2,1,0:T(8,128)(2,1)S(1)}, u32[]{:S(2)}, u32[]{:S(2)}) async-start(bf16[64,32,128]{2,1,0:T(8,128)(2,1)} %broadcast_in_dim.14), calls=%async_computation.1 | async-start | bytes 1048576 | tf_op jit(solution)/shard_map/all_to_all | solution.py:626

commit v8 on v7

--- a/solution.py
+++ b/solution.py
@@ -130,6 +130,12 @@
     acc[...] = jnp.zeros_like(acc)
     for packed in (p_down, p_mid, p_up_t, p_mid_t):
         packed[...] = jnp.zeros_like(packed)
+    for taps, end in (
+        (field_taps, FIELD_LOW + rows + FIELD_HIGH),
+        (cot_taps, COT_LOW + rows + COT_HIGH),
+    ):
+        for p in (end, end + 1):
+            taps[p // 4, p % 4] = jnp.zeros((slots, 3 * C), BF16)
     for copy in edge_copies:
         copy.wait()
 

time: 88.8 us -> 88.8 us (level)
  no operation moved by 1% of the time
where the time goes in v8:
time: 88.8 us; the launch traced here: 88.5 us
  Pallas kernels  27.8 us (31%)
  blocking collectives  24.8 us (28%)
  starting transfers between devices  20.9 us (24%)
  waiting for transfers between devices  12.1 us (14%)
  local copies, waits for them, and re-layouts  1.83 us (2%)
    all_to_all x1, blocking collectives, body(): pieces = lax.all_to_all(pieces, ('lat', 'lon'), 0, 0, tiled=True)  22.3 us
    pallas_call x1, Pallas kernels, body(): pl.pallas_call(functools.partial(grads_kernel, half_rows, half_cols, lats...  15.7 us
    pallas_call x2, Pallas kernels, spread(): pl.pallas_call(functools.partial(up_kernel, above, kind, swapped), out_sh...  10.4 us
    ppermute x1, waiting for transfers between devices, halos(): high_ends = lax.ppermute(down, 'lat', south)  6.61 us
    ppermute x1, starting transfers between devices, halos(): low = lax.ppermute(up, 'lat', north)  4.81 us
    ppermute x1, starting transfers between devices, halos(): low_ends = lax.ppermute(up, 'lat', north)  4.81 us
    all_to_all x1, starting transfers between devices, body(): lax.all_to_all(jnp.broadcast_to(piece, pieces.shape), ('lat', 'lon'), 0,...  4.73 us
    ppermute x1, starting transfers between devices, halos(): from_east = lax.ppermute(west, 'lon', westward)  3.92 us
  transfers between devices with their start and end apart: 8, of which 4 were waited for; matrix products, arithmetic and copies ran while one was open for 0% of the time, Pallas kernels for 12%

profile of v8, /device:TPU:0, one launch (start us, length us, event | category | flops | bytes accessed | tf_op | source)
XLA Modules:
  0.0 88.5 jit_solution(7359486519804126751)
XLA Ops:
  0.6 0.0 copy-start.1
  0.6 0.0 copy-start.2
  0.7 0.0 copy-start.3
  0.7 1.5 %pack.1 = (bf16[80,8,128]{2,1,0:T(8,128)(2,1)S(1)}, bf16[100,8,128]{2,1,0:T(8,128)(2,1)S(1)}, bf16[8,128,128]{2,1,0:T(8,128)(2,1)S(1)}, bf16[10,128,128]{2,1,0:T(8,128)(2,1)S(1)}) custom-call(bf16[80,128,128]{2,1,0:T(8,128)(2,1)} %bitcast.17, bf16[80,128,128]{2,1,0:T(8,128)(2,1)} %bitcast.20), custom_call_target="tpu_custom_call" | custom-call | tf_op jit(solution)/shard_map/pack/pallas_call | solution.py:495
  2.2 3.9 %collective-permute-start.3 = (bf16[100,8,128]{2,1,0:T(8,128)(2,1)S(1)}, bf16[100,8,128]{2,1,0:T(8,128)(2,1)S(1)}, u32[]{:S(2)}, u32[]{:S(2)}) collective-permute-start(bf16[100,8,128]{2,1,0:T(8,128)(2,1)S(1)} %get-tuple-element.27), channel_id=1, source_target_pairs={{1,0},{2,1},{3,2},{4,3},{5,4},{6,5},{7,6},{0,7},{9,8},{10,9},{11,1... | collective-permute-start | bytes 614408 | tf_op jit(solution)/shard_map/ppermute | solution.py:544
  6.1 0.0 collective-permute-start.2
  6.1 4.8 %collective-permute-start = (bf16[8,128,128]{2,1,0:T(8,128)(2,1)S(1)}, bf16[8,128,128]{2,1,0:T(8,128)(2,1)S(1)}, u32[]{:S(2)}, u32[]{:S(2)}) collective-permute-start(bf16[8,128,128]{2,1,0:T(8,128)(2,1)S(1)} %get-tuple-element.24), channel_id=1, source_target_pairs={{0,8},{8,16},{16,24},{24,32},{32,40},{40,48},{48,56},{1,9},{9,17},... | collective-permute-start | bytes 786440 | tf_op jit(solution)/shard_map/ppermute | solution.py:545
  10.9 1.3 %collective-permute-start.1 = (bf16[10,128,128]{2,1,0:T(8,128)(2,1)S(1)}, bf16[10,128,128]{2,1,0:T(8,128)(2,1)S(1)}, u32[]{:S(2)}, u32[]{:S(2)}) collective-permute-start(bf16[10,128,128]{2,1,0:T(8,128)(2,1)S(1)} %get-tuple-element.25), channel_id=1, source_target_pairs={{8,0},{16,8},{24,16},{32,24},{40,32},{48,40},{56,48},{9,1},{17,9},... | collective-permute-start | bytes 983048 | tf_op jit(solution)/shard_map/ppermute | solution.py:546
  12.2 0.0 copy-done.1
  12.2 0.0 copy-done.2
  12.2 0.0 copy-done.3
  12.2 0.1 pad_maximum_fusion
  12.3 1.7 %collective-permute-done.2.refs_0_.west_hbm = bf16[80,8,128]{2,1,0:T(8,128)(2,1)S(1)} collective-permute-done((bf16[80,8,128]{2,1,0:T(8,128)(2,1)S(1)}, bf16[80,8,128]{2,1,0:T(8,128)(2,1)S(1)}, u32[]{:S(2)}, u32[]{:S(2)}) %collective-permute-start.2) | collective-permute-done | bytes 163872 | tf_op jit(solution)/shard_map/ppermute | solution.py:543
  14.0 0.0 collective-permute-done.3.refs_1_.east_hbm
  14.0 0.1 corners.1
  14.1 4.8 %collective-permute-start.4 = (bf16[12,8,128]{2,1,0:T(8,128)(2,1)S(1)}, bf16[12,8,128]{2,1,0:T(8,128)(2,1)S(1)}, u32[]{:S(2)}, u32[]{:S(2)}) collective-permute-start(bf16[12,8,128]{2,1,0:T(8,128)(2,1)S(1)} %get-tuple-element.30), channel_id=1, source_target_pairs={{0,8},{8,16},{16,24},{24,32},{32,40},{40,48},{48,56},{1,9},{9,17},... | collective-permute-start | bytes 73736 | tf_op jit(solution)/shard_map/ppermute | solution.py:564
  18.9 1.3 %collective-permute-start.5 = (bf16[14,8,128]{2,1,0:T(8,128)(2,1)S(1)}, bf16[14,8,128]{2,1,0:T(8,128)(2,1)S(1)}, u32[]{:S(2)}, u32[]{:S(2)}) collective-permute-start(bf16[14,8,128]{2,1,0:T(8,128)(2,1)S(1)} %get-tuple-element.31), channel_id=1, source_target_pairs={{8,0},{16,8},{24,16},{32,24},{40,32},{48,40},{56,48},{9,1},{17,9},... | collective-permute-start | bytes 86024 | tf_op jit(solution)/shard_map/ppermute | solution.py:565
  20.2 2.4 %all_gather.3 = bf16[3,3,3,128,128]{4,3,2,1,0:T(8,128)(2,1)S(1)} all-gather(bf16[3,3,3,64,128]{4,3,2,1,0:T(8,128)(2,1)S(1)} %pad_maximum_fusion), channel_id=1, replica_groups=mesh['dp'=2,'lat'=8,'lon'=8] {'dp'}, dimensions={3}, use_global_device_ids=true | all-gather | bytes 1327104 | tf_op jit(solution)/shard_map/all_gather | solution.py:566
  22.6 0.0 copy-start
  22.6 0.0 collective-permute-done.4.low_ends_hbm
  22.6 6.6 %collective-permute-done.5.high_ends_hbm = bf16[14,8,128]{2,1,0:T(8,128)(2,1)S(1)} collective-permute-done((bf16[14,8,128]{2,1,0:T(8,128)(2,1)S(1)}, bf16[14,8,128]{2,1,0:T(8,128)(2,1)S(1)}, u32[]{:S(2)}, u32[]{:S(2)}) %collective-permute-start.5) | collective-permute-done | bytes 28704 | tf_op jit(solution)/shard_map/ppermute | solution.py:565
  29.3 0.0 collective-permute-done.low_hbm
  29.3 0.0 collective-permute-done.1.high_hbm
  29.3 15.7 %grads.1 = (f32[32,64,128]{2,1,0:T(8,128)S(1)}, bf16[32,64,128]{2,1,0:T(8,128)(2,1)S(1)}, bf16[23,2,64,256]{3,2,1,0:T(8,128)(2,1)}, bf16[23,2,64,256]{3,2,1,0:T(8,128)(2,1)}) custom-call(bf16[80,128,128]{2,1,0:T(8,128)(2,1)} %bitcast.18, bf16[80,128,128]{2,1,0:T(8,128)(2,1)} %bitcast.21, bf16[8,128,128]{2,1,0:T(8,128)(2,1)S(1)} %collective-permute-done.low_hbm, ...), custom_call_target="tpu_custom_call" | custom-call | flops 5872025600 | bytes 8388608 | tf_op jit(solution)/shard_map/grads/pallas_call | solution.py:585
  45.0 0.0 copy-done
  45.0 0.1 collective-permute-start.6
  45.1 1.9 %collective-permute-done.6 = bf16[32,64,128]{2,1,0:T(8,128)(2,1)S(1)} collective-permute-done((bf16[32,64,128]{2,1,0:T(8,128)(2,1)S(1)}, bf16[32,64,128]{2,1,0:T(8,128)(2,1)S(1)}, u32[]{:S(2)}, u32[]{:S(2)}) %collective-permute-start.6) | collective-permute-done | bytes 524320 | tf_op jit(solution)/shard_map/ppermute | solution.py:627
  47.0 0.2 add_convert_fusion
  47.2 22.3 %all_to_all.10 = bf16[64,32,128]{2,1,0:T(8,128)(2,1)S(1)} all-to-all(bf16[64,32,128]{2,1,0:T(8,128)(2,1)S(1)} %bitcast.25), channel_id=1, replica_groups=mesh['dp'=2,'lat'=8,'lon'=8] {'lat','lon'}, dimensions={0} | all-to-all | bytes 1048576 | tf_op jit(solution)/shard_map/all_to_all | solution.py:630
  69.5 0.1 reduce_sum.12
  69.6 0.9 broadcast_in_dim.14
  70.5 4.7 %all-to-all-start.1 = ((bf16[64,32,128]{2,1,0:T(8,128)(2,1)}), bf16[64,32,128]{2,1,0:T(8,128)(2,1)S(1)}, u32[]{:S(2)}, u32[]{:S(2)}) async-start(bf16[64,32,128]{2,1,0:T(8,128)(2,1)} %broadcast_in_dim.14), calls=%async_computation.1 | async-start | bytes 1048576 | tf_op jit(solution)/shard_map/all_to_all | solution.py:632
  75.2 5.2 %level.1 = bf16[80,128,128]{2,1,0:T(8,128)(2,1)} custom-call(bf16[46,64,256]{2,1,0:T(8,128)(2,1)} %bitcast.27, bf16[80,128,128]{2,1,0:T(8,128)(2,1)} %bitcast.19, bf16[3,1152,128]{2,1,0:T(8,128)(2,1)} %bitcast.15), custom_call_target="tpu_custom_call" | custom-call | flops 754974720 | bytes 7340032 | tf_op jit(solution)/shard_map/level/pallas_call | solution.py:407
  80.4 5.2 %gradient.1 = bf16[80,128,128]{2,1,0:T(8,128)(2,1)} custom-call(bf16[46,64,256]{2,1,0:T(8,128)(2,1)} %bitcast.26, bf16[80,128,128]{2,1,0:T(8,128)(2,1)} %bitcast.22, bf16[3,1152,128]{2,1,0:T(8,128)(2,1)} %bitcast.16), custom_call_target="tpu_custom_call" | custom-call | flops 754974720 | bytes 7340032 | tf_op jit(solution)/shard_map/gradient/pallas_call | solution.py:407
  85.7 1.9 %all-to-all-done.1 = bf16[64,32,128]{2,1,0:T(8,128)(2,1)S(1)} async-done(((bf16[64,32,128]{2,1,0:T(8,128)(2,1)}), bf16[64,32,128]{2,1,0:T(8,128)(2,1)S(1)}, u32[]{:S(2)}, u32[]{:S(2)}) %all-to-all-start.1) | async-done | bytes 524320 | tf_op jit(solution)/shard_map/all_to_all | solution.py:632
  87.6 0.9 %fusion = (f32[18,32,128]{2,1,0:T(8,128)}, f32[18,32,128]{2,1,0:T(8,128)}, f32[18,32,128]{2,1,0:T(8,128)}) fusion(bf16[64,32,128]{2,1,0:T(8,128)(2,1)S(1)} %all-to-all-done.1), kind=kLoop, calls=%fused_computation.2 | loop fusion | bytes 1769472 | tf_op jit(solution)/shard_map/slice | solution.py:640
  (1 shorter events, 0.0 us)
Async XLA Ops:
  0.6 11.6 %copy-start.1 = (bf16[3,3,64,128]{3,2,1,0:T(8,128)(2,1)S(1)}, bf16[3,3,64,128]{3,2,1,0:T(8,128)(2,1)}, u32[]{:S(2)}) copy-start(bf16[3,3,64,128]{3,2,1,0:T(8,128)(2,1)} %param.8) | copy-start | bytes 442372
  0.6 11.6 %copy-start.2 = (bf16[3,3,64,128]{3,2,1,0:T(8,128)(2,1)S(1)}, bf16[3,3,64,128]{3,2,1,0:T(8,128)(2,1)}, u32[]{:S(2)}) copy-start(bf16[3,3,64,128]{3,2,1,0:T(8,128)(2,1)} %param.7) | copy-start | bytes 442372
  0.7 11.6 %copy-start.3 = (bf16[3,3,64,128]{3,2,1,0:T(8,128)(2,1)S(1)}, bf16[3,3,64,128]{3,2,1,0:T(8,128)(2,1)}, u32[]{:S(2)}) copy-start(bf16[3,3,64,128]{3,2,1,0:T(8,128)(2,1)} %param.6) | copy-start | bytes 442372
  2.2 11.8 %collective-permute-start.3 = (bf16[100,8,128]{2,1,0:T(8,128)(2,1)S(1)}, bf16[100,8,128]{2,1,0:T(8,128)(2,1)S(1)}, u32[]{:S(2)}, u32[]{:S(2)}) collective-permute-start(bf16[100,8,128]{2,1,0:T(8,128)(2,1)S(1)} %get-tuple-element.27), channel_id=1, source_target_pairs={{1,0},{2,1},{3,2},{4,3},{5,4},{6,5},{7,6},{0,7},{9,8},{10,9},{11,1... | collective-permute-start | bytes 614408 | tf_op jit(solution)/shard_map/ppermute | solution.py:544
  6.1 7.9 %collective-permute-start.2 = (bf16[80,8,128]{2,1,0:T(8,128)(2,1)S(1)}, bf16[80,8,128]{2,1,0:T(8,128)(2,1)S(1)}, u32[]{:S(2)}, u32[]{:S(2)}) collective-permute-start(bf16[80,8,128]{2,1,0:T(8,128)(2,1)S(1)} %get-tuple-element.26), channel_id=1, source_target_pairs={{0,1},{1,2},{2,3},{3,4},{4,5},{5,6},{6,7},{7,0},{8,9},{9,10},{10,1... | collective-permute-start | bytes 491528 | tf_op jit(solution)/shard_map/ppermute | solution.py:543
  6.1 23.2 %collective-permute-start = (bf16[8,128,128]{2,1,0:T(8,128)(2,1)S(1)}, bf16[8,128,128]{2,1,0:T(8,128)(2,1)S(1)}, u32[]{:S(2)}, u32[]{:S(2)}) collective-permute-start(bf16[8,128,128]{2,1,0:T(8,128)(2,1)S(1)} %get-tuple-element.24), channel_id=1, source_target_pairs={{0,8},{8,16},{16,24},{24,32},{32,40},{40,48},{48,56},{1,9},{9,17},... | collective-permute-start | bytes 786440 | tf_op jit(solution)/shard_map/ppermute | solution.py:545
  10.9 18.4 %collective-permute-start.1 = (bf16[10,128,128]{2,1,0:T(8,128)(2,1)S(1)}, bf16[10,128,128]{2,1,0:T(8,128)(2,1)S(1)}, u32[]{:S(2)}, u32[]{:S(2)}) collective-permute-start(bf16[10,128,128]{2,1,0:T(8,128)(2,1)S(1)} %get-tuple-element.25), channel_id=1, source_target_pairs={{8,0},{16,8},{24,16},{32,24},{40,32},{48,40},{56,48},{9,1},{17,9},... | collective-permute-start | bytes 983048 | tf_op jit(solution)/shard_map/ppermute | solution.py:546
  14.1 8.6 %collective-permute-start.4 = (bf16[12,8,128]{2,1,0:T(8,128)(2,1)S(1)}, bf16[12,8,128]{2,1,0:T(8,128)(2,1)S(1)}, u32[]{:S(2)}, u32[]{:S(2)}) collective-permute-start(bf16[12,8,128]{2,1,0:T(8,128)(2,1)S(1)} %get-tuple-element.30), channel_id=1, source_target_pairs={{0,8},{8,16},{16,24},{24,32},{32,40},{40,48},{48,56},{1,9},{9,17},... | collective-permute-start | bytes 73736 | tf_op jit(solution)/shard_map/ppermute | solution.py:564
  18.9 10.4 %collective-permute-start.5 = (bf16[14,8,128]{2,1,0:T(8,128)(2,1)S(1)}, bf16[14,8,128]{2,1,0:T(8,128)(2,1)S(1)}, u32[]{:S(2)}, u32[]{:S(2)}) collective-permute-start(bf16[14,8,128]{2,1,0:T(8,128)(2,1)S(1)} %get-tuple-element.31), channel_id=1, source_target_pairs={{8,0},{16,8},{24,16},{32,24},{40,32},{48,40},{56,48},{9,1},{17,9},... | collective-permute-start | bytes 86024 | tf_op jit(solution)/shard_map/ppermute | solution.py:565
  22.6 22.4 %copy-start = (bf16[3,3,3,128,128]{4,3,2,1,0:T(8,128)(2,1)}, bf16[3,3,3,128,128]{4,3,2,1,0:T(8,128)(2,1)S(1)}, u32[]{:S(2)}) copy-start(bf16[3,3,3,128,128]{4,3,2,1,0:T(8,128)(2,1)S(1)} %all_gather.3) | copy-start | bytes 2654212
  45.0 2.0 %collective-permute-start.6 = (bf16[32,64,128]{2,1,0:T(8,128)(2,1)S(1)}, bf16[32,64,128]{2,1,0:T(8,128)(2,1)S(1)}, u32[]{:S(2)}, u32[]{:S(2)}) collective-permute-start(bf16[32,64,128]{2,1,0:T(8,128)(2,1)S(1)} %get-tuple-element.38), channel_id=1, source_target_pairs={{0,64},{64,0},{1,65},{65,1},{2,66},{66,2},{3,67},{67,3},{4,68},{68... | collective-permute-start | bytes 1572872 | tf_op jit(solution)/shard_map/ppermute | solution.py:627
  70.5 17.1 %all-to-all-start.1 = ((bf16[64,32,128]{2,1,0:T(8,128)(2,1)}), bf16[64,32,128]{2,1,0:T(8,128)(2,1)S(1)}, u32[]{:S(2)}, u32[]{:S(2)}) async-start(bf16[64,32,128]{2,1,0:T(8,128)(2,1)} %broadcast_in_dim.14), calls=%async_computation.1 | async-start | bytes 1048576 | tf_op jit(solution)/shard_map/all_to_all | solution.py:632
